TPU v7x, 32 devices: a whole 2x2x4 slice. The times are simulated.
32 devices in a mesh: dp: 16 (over z, x, core), tensor: 2 (over y).
Axes of the slice: x: 2, y: 2, z: 4, core: 2. Of those that a mesh axis runs over, the one named last changes fastest.
Arguments:
- src_embed: bfloat16 [512, 16, 768], P('tensor', 'dp'), may hold values from -6 to 6
- tgt_embed: bfloat16 [256, 16, 768], P('tensor', 'dp'), may hold values from -6 to 6
- src_mask: int32 [16, 512], P('dp'), may hold values from 0 to 1, as said below
- tgt_mask: int32 [16, 256], P('dp'), may hold values from 0 to 1, as said below
- objective: int32 [16], P('dp'), may hold values from 0 to 1
- loss_mask: int32 [16, 256], P('dp', 'tensor'), may hold values 0 or 1
- enc_cot: bfloat16 [512, 16, 768], P('tensor', 'dp'), may hold values from -6 to 6
- dec_cot: bfloat16 [256, 16, 768], P('tensor', 'dp'), may hold values from -6 to 6
- norm_gain: float32 [5, 768], replicated, may hold values from 0.1 to 1.9
- norm_bias: float32 [5, 768], replicated, may hold values from -4 to 4
- attn_in: bfloat16 [3, 3, 768, 768], P(None, None, None, 'tensor'), may hold values from -0.21875 to 0.21875
- attn_in_bias: float32 [3, 2, 768], P(None, None, 'tensor'), may hold values from -4 to 4
- attn_out: bfloat16 [3, 768, 768], P(None, 'tensor'), may hold values from -0.625 to 0.625
- attn_out_bias: float32 [3, 768], replicated, may hold values from -4 to 4
- ffn_in: bfloat16 [2, 768, 3072], P(None, None, 'tensor'), may hold values from -0.21875 to 0.21875
- ffn_in_bias: float32 [2, 3072], P(None, 'tensor'), may hold values from -4 to 4
- ffn_out: bfloat16 [2, 3072, 768], P(None, 'tensor'), may hold values from -0.109375 to 0.109375
- ffn_out_bias: float32 [2, 768], replicated, may hold values from -4 to 4
Outputs:
- enc_out: bfloat16 [512, 16, 768], P('tensor', 'dp')
- dec_out: bfloat16 [256, 16, 768], P('tensor', 'dp')
- src_grad: float32 [512, 16, 768], P('tensor', 'dp')
- tgt_grad: float32 [256, 16, 768], P('tensor', 'dp')
- norm_gain_grad: float32 [5, 768], replicated
- norm_bias_grad: float32 [5, 768], replicated
- attn_in_grad: float32 [3, 3, 768, 768], P(None, None, None, 'tensor')
- attn_in_bias_grad: float32 [3, 2, 768], P(None, None, 'tensor')
- attn_out_grad: float32 [3, 768, 768], P(None, 'tensor')
- attn_out_bias_grad: float32 [3, 768], replicated
- ffn_in_grad: float32 [2, 768, 3072], P(None, None, 'tensor')
- ffn_in_bias_grad: float32 [2, 3072], P(None, 'tensor')
- ffn_out_grad: float32 [2, 3072, 768], P(None, 'tensor')
- ffn_out_bias_grad: float32 [2, 768], replicated
Inputs may be any that keep to these rules, and one draw needn't show every extreme that they name: `src_mask`: each example's ones form a prefix longer than 256; example 0 has exactly 257 ones and the last example has 512. `tgt_mask`: each example's ones form a prefix longer than 128; example 0 has exactly 129 ones and the last example has 256.
All inputs are finite; a program needn't handle non-finite values. No bound on the sum of `loss_mask` on one device may be relied on, other than what follows from the above.
Results may differ from a plain program's by a relative error of at most 0.025.
Values may be sent and summed in bfloat16 or wider, within the bound.
No kernel may reach another device: no remote copies, remote signals or barrier semaphores. Data moves between devices by JAX's collectives and lax.ppermute only.
A program may use at most 192 MiB of HBM per device.

v0:
```python
import jax
import jax.numpy as jnp
from jax import lax
from jax.sharding import PartitionSpec as P

HEAD = 64


EPSILON = 1e-05
MASKED_SCORE = -1000000000.0


def norm_forward(inputs, norm_scale, offset):
    centre = inputs - jnp.mean(inputs, axis=-1, keepdims=True)
    variance = jnp.mean(centre * centre, axis=-1, keepdims=True)
    inverse = lax.rsqrt(variance + EPSILON)
    normed = centre * inverse
    return (normed * norm_scale + offset, (normed, inverse))


def norm_backward(gradient, norm_kept, norm_scale):
    normed, inverse = norm_kept
    scale_grad = jnp.sum(gradient * normed, axis=(0, 1))
    offset_grad = jnp.sum(gradient, axis=(0, 1))
    scaled = gradient * norm_scale
    mean_plain = jnp.mean(scaled, axis=-1, keepdims=True)
    mean_normed = jnp.mean(scaled * normed, axis=-1, keepdims=True)
    return (inverse * (scaled - mean_plain - normed * mean_normed), scale_grad, offset_grad)


def spread_rows(values):
    return lax.all_gather(values, "tensor", axis=0, tiled=True)


def collect_rows(source, weight):
    local_rows = source.shape[0] // lax.axis_size("tensor")

    def term(first_row, row_count):
        return jnp.einsum("sef,fd->sed", source, weight, preferred_element_type=jnp.float32)

    return lax.psum_scatter(
        term(jnp.int32(0), lax.axis_size("tensor") * local_rows),
        "tensor",
        scatter_dimension=0,
        tiled=True,
    )


def spread_grads(values):
    return lax.all_gather(values, "tensor", axis=0, tiled=True)


def collect_grads(gradients, weights):
    local_rows = gradients.shape[1] // lax.axis_size("tensor")

    def term(first_row, row_count):
        return jnp.einsum("csef,cdf->sed", gradients, weights, preferred_element_type=jnp.float32)

    return lax.psum_scatter(
        term(jnp.int32(0), lax.axis_size("tensor") * local_rows),
        "tensor",
        scatter_dimension=0,
        tiled=True,
    )


def split_heads(values):
    return values.reshape(values.shape[0], values.shape[1], values.shape[2] // HEAD, HEAD)


def head_scores(queries, key_rows, allowed):
    scores = jnp.einsum(
        "qehd,kehd->ehqk",
        split_heads(queries),
        split_heads(key_rows),
        preferred_element_type=jnp.float32,
    ) * HEAD ** (-0.5)
    return jnp.where(allowed, scores, MASKED_SCORE)


def attend(queries, key_rows, value_rows, allowed):
    scores = head_scores(queries, key_rows, allowed)
    row_max = jnp.max(scores, axis=-1, keepdims=True)
    exponent = jnp.exp(scores - row_max)
    row_total = jnp.sum(exponent, axis=-1, keepdims=True)
    weights = (exponent / row_total).astype(jnp.bfloat16)
    mixture = jnp.einsum(
        "ehqk,kehd->qehd", weights, split_heads(value_rows), preferred_element_type=jnp.float32
    )
    return (mixture.reshape(queries.shape).astype(jnp.bfloat16), row_max + jnp.log(row_total))


def attend_backward(mixture_grad, queries, key_rows, value_rows, allowed, log_total):
    scale = HEAD ** (-0.5)
    scores = head_scores(queries, key_rows, allowed)
    probs = jnp.exp(scores - log_total)
    grad_heads = split_heads(mixture_grad)
    prob_grad = jnp.einsum(
        "qehd,kehd->ehqk", grad_heads, split_heads(value_rows), preferred_element_type=jnp.float32
    )
    row_inner = jnp.sum(probs * prob_grad, axis=-1, keepdims=True)
    score_grad = (probs * (prob_grad - row_inner)).astype(jnp.bfloat16)
    query_grad = (
        jnp.einsum(
            "ehqk,kehd->qehd", score_grad, split_heads(key_rows), preferred_element_type=jnp.float32
        )
        * scale
    )
    key_grad = (
        jnp.einsum(
            "ehqk,qehd->kehd", score_grad, split_heads(queries), preferred_element_type=jnp.float32
        )
        * scale
    )
    value_grad = jnp.einsum(
        "ehqk,qehd->kehd",
        probs.astype(jnp.bfloat16),
        grad_heads,
        preferred_element_type=jnp.float32,
    )
    return (
        query_grad.reshape(queries.shape).astype(jnp.bfloat16),
        key_grad.reshape(key_rows.shape).astype(jnp.bfloat16),
        value_grad.reshape(value_rows.shape).astype(jnp.bfloat16),
    )


def self_forward(inputs, norm_scale, offset, in_weights, in_biases, out_weights, out_bias, allowed):
    normed, norm_kept = norm_forward(inputs, norm_scale, offset)
    gathered = spread_rows(normed.astype(jnp.bfloat16))
    projected = jnp.einsum(
        "sed,cdf->csef", gathered, in_weights, preferred_element_type=jnp.float32
    )
    queries = (projected[0] + in_biases[0]).astype(jnp.bfloat16)
    key_rows = projected[1].astype(jnp.bfloat16)
    value_rows = (projected[2] + in_biases[1]).astype(jnp.bfloat16)
    mixture, log_total = attend(queries, key_rows, value_rows, allowed)
    result = inputs + (collect_rows(mixture, out_weights) + out_bias)
    return (result, (norm_kept, gathered, queries, key_rows, value_rows, mixture, log_total))


def cross_forward(
    inputs, memory_rows, norm_scale, offset, in_weights, in_biases, out_weights, out_bias, allowed
):
    normed, norm_kept = norm_forward(inputs, norm_scale, offset)
    gathered = spread_rows(normed.astype(jnp.bfloat16))
    queries = (
        jnp.einsum("sed,df->sef", gathered, in_weights[0], preferred_element_type=jnp.float32)
        + in_biases[0]
    ).astype(jnp.bfloat16)
    projected = jnp.einsum(
        "sed,cdf->csef", memory_rows, in_weights[1:], preferred_element_type=jnp.float32
    )
    key_rows = projected[0].astype(jnp.bfloat16)
    value_rows = (projected[1] + in_biases[1]).astype(jnp.bfloat16)
    mixture, log_total = attend(queries, key_rows, value_rows, allowed)
    result = inputs + (collect_rows(mixture, out_weights) + out_bias)
    return (
        result,
        (norm_kept, gathered, memory_rows, queries, key_rows, value_rows, mixture, log_total),
    )


def ffn_forward(inputs, norm_scale, offset, first_weight, first_bias, second_weight, second_bias):
    normed, norm_kept = norm_forward(inputs, norm_scale, offset)
    gathered = spread_rows(normed.astype(jnp.bfloat16))
    hidden = (
        jnp.einsum("sed,df->sef", gathered, first_weight, preferred_element_type=jnp.float32)
        + first_bias
    )
    active = jax.nn.gelu(hidden).astype(jnp.bfloat16)
    result = inputs + (collect_rows(active, second_weight) + second_bias)
    return (result, (norm_kept, gathered, hidden, active))


def output_backward(gradient, mixture, out_weights):
    low_grad = gradient.astype(jnp.bfloat16)
    out_bias_grad = jnp.sum(low_grad, axis=(0, 1), dtype=jnp.float32)
    full_grad = spread_grads(low_grad)
    out_weight_grad = jnp.einsum(
        "sef,sed->fd", mixture, full_grad, preferred_element_type=jnp.float32
    )
    mixture_grad = jnp.einsum(
        "sed,fd->sef", full_grad, out_weights, preferred_element_type=jnp.float32
    ).astype(jnp.bfloat16)
    return (mixture_grad, out_weight_grad, out_bias_grad)


def self_backward(gradient, saved_state, norm_scale, in_weights, out_weights, allowed):
    norm_kept, gathered, queries, key_rows, value_rows, mixture, log_total = saved_state
    mixture_grad, out_weight_grad, out_bias_grad = output_backward(gradient, mixture, out_weights)
    query_grad, key_grad, value_grad = attend_backward(
        mixture_grad, queries, key_rows, value_rows, allowed, log_total
    )
    stacked = jnp.stack([query_grad, key_grad, value_grad])
    in_weight_grad = jnp.einsum(
        "sed,csef->cdf", gathered, stacked, preferred_element_type=jnp.float32
    )
    in_bias_grad = jnp.stack(
        [
            jnp.sum(query_grad, axis=(0, 1), dtype=jnp.float32),
            jnp.sum(value_grad, axis=(0, 1), dtype=jnp.float32),
        ]
    )
    normed_grad = collect_grads(stacked, in_weights)
    input_grad, scale_grad, offset_grad = norm_backward(normed_grad, norm_kept, norm_scale)
    return (
        gradient + input_grad,
        (in_weight_grad, in_bias_grad, out_weight_grad, out_bias_grad, scale_grad, offset_grad),
    )


def cross_backward(gradient, saved_state, norm_scale, in_weights, out_weights, allowed):
    norm_kept, gathered, memory_rows, queries, key_rows, value_rows, mixture, log_total = (
        saved_state
    )
    mixture_grad, out_weight_grad, out_bias_grad = output_backward(gradient, mixture, out_weights)
    query_grad, key_grad, value_grad = attend_backward(
        mixture_grad, queries, key_rows, value_rows, allowed, log_total
    )
    memory_stack = jnp.stack([key_grad, value_grad])
    query_weight_grad = jnp.einsum(
        "sed,sef->df", gathered, query_grad, preferred_element_type=jnp.float32
    )
    memory_weight_grad = jnp.einsum(
        "sed,csef->cdf", memory_rows, memory_stack, preferred_element_type=jnp.float32
    )
    in_weight_grad = jnp.concatenate([query_weight_grad[None], memory_weight_grad], axis=0)
    in_bias_grad = jnp.stack(
        [
            jnp.sum(query_grad, axis=(0, 1), dtype=jnp.float32),
            jnp.sum(value_grad, axis=(0, 1), dtype=jnp.float32),
        ]
    )
    normed_grad = collect_grads(query_grad[None], in_weights[0:1])
    memory_grad = collect_grads(memory_stack, in_weights[1:])
    input_grad, scale_grad, offset_grad = norm_backward(normed_grad, norm_kept, norm_scale)
    return (
        gradient + input_grad,
        memory_grad,
        (in_weight_grad, in_bias_grad, out_weight_grad, out_bias_grad, scale_grad, offset_grad),
    )


def ffn_backward(gradient, saved_state, norm_scale, first_weight, second_weight):
    norm_kept, gathered, hidden, active = saved_state
    low_grad = gradient.astype(jnp.bfloat16)
    second_bias_grad = jnp.sum(low_grad, axis=(0, 1), dtype=jnp.float32)
    full_grad = spread_grads(low_grad)
    second_weight_grad = jnp.einsum(
        "sef,sed->fd", active, full_grad, preferred_element_type=jnp.float32
    )
    active_grad = jnp.einsum(
        "sed,fd->sef", full_grad, second_weight, preferred_element_type=jnp.float32
    )
    unused, gelu_pullback = jax.vjp(jax.nn.gelu, hidden)
    hidden_grad = gelu_pullback(active_grad)[0].astype(jnp.bfloat16)
    first_weight_grad = jnp.einsum(
        "sed,sef->df", gathered, hidden_grad, preferred_element_type=jnp.float32
    )
    first_bias_grad = jnp.sum(hidden_grad, axis=(0, 1), dtype=jnp.float32)
    normed_grad = collect_grads(hidden_grad[None], first_weight[None])
    input_grad, scale_grad, offset_grad = norm_backward(normed_grad, norm_kept, norm_scale)
    return (
        gradient + input_grad,
        (
            first_weight_grad,
            first_bias_grad,
            second_weight_grad,
            second_bias_grad,
            scale_grad,
            offset_grad,
        ),
    )


def run_encoder(inputs, params, source_keys):
    (
        norm_gain,
        norm_bias,
        attn_in,
        attn_in_bias,
        attn_out,
        attn_out_bias,
        ffn_in,
        ffn_in_bias,
        ffn_out,
        ffn_out_bias,
    ) = params
    middle, first_state = self_forward(
        inputs,
        norm_gain[0],
        norm_bias[0],
        attn_in[0],
        attn_in_bias[0],
        attn_out[0],
        attn_out_bias[0],
        source_keys,
    )
    result, second = ffn_forward(
        middle, norm_gain[1], norm_bias[1], ffn_in[0], ffn_in_bias[0], ffn_out[0], ffn_out_bias[0]
    )
    return (result, (first_state, second))


def run_decoder(inputs, memory_low, params, target_allowed, source_keys):
    (
        norm_gain,
        norm_bias,
        attn_in,
        attn_in_bias,
        attn_out,
        attn_out_bias,
        ffn_in,
        ffn_in_bias,
        ffn_out,
        ffn_out_bias,
    ) = params
    memory_rows = spread_rows(memory_low)
    middle, first_state = self_forward(
        inputs,
        norm_gain[2],
        norm_bias[2],
        attn_in[1],
        attn_in_bias[1],
        attn_out[1],
        attn_out_bias[1],
        target_allowed,
    )
    later, second = cross_forward(
        middle,
        memory_rows,
        norm_gain[3],
        norm_bias[3],
        attn_in[2],
        attn_in_bias[2],
        attn_out[2],
        attn_out_bias[2],
        source_keys,
    )
    result, third_state = ffn_forward(
        later, norm_gain[4], norm_bias[4], ffn_in[1], ffn_in_bias[1], ffn_out[1], ffn_out_bias[1]
    )
    return (result, (first_state, second, third_state))


def decoder_backward(gradient, saved_states, params, target_allowed, source_keys):
    norm_gain, attn_in, attn_out, ffn_in, ffn_out = (
        params[0],
        params[2],
        params[4],
        params[6],
        params[8],
    )
    first_state, second, third_state = saved_states
    later_grad, ffn_grads = ffn_backward(gradient, third_state, norm_gain[4], ffn_in[1], ffn_out[1])
    middle_grad, memory_grad, cross_grads = cross_backward(
        later_grad, second, norm_gain[3], attn_in[2], attn_out[2], source_keys
    )
    input_grad, self_grads = self_backward(
        middle_grad, first_state, norm_gain[2], attn_in[1], attn_out[1], target_allowed
    )
    sharded = (
        jnp.stack([self_grads[0], cross_grads[0]]),
        jnp.stack([self_grads[1], cross_grads[1]]),
        jnp.stack([self_grads[2], cross_grads[2]]),
        ffn_grads[0][None],
        ffn_grads[1][None],
        ffn_grads[2][None],
    )
    shared = (
        jnp.stack([self_grads[4], cross_grads[4], ffn_grads[4]]),
        jnp.stack([self_grads[5], cross_grads[5], ffn_grads[5]]),
        jnp.stack([self_grads[3], cross_grads[3]]),
        ffn_grads[3][None],
    )
    return (input_grad, memory_grad, sharded, shared)


def encoder_backward(gradient, saved_states, params, source_keys):
    norm_gain, attn_in, attn_out, ffn_in, ffn_out = (
        params[0],
        params[2],
        params[4],
        params[6],
        params[8],
    )
    first_state, second = saved_states
    middle_grad, ffn_grads = ffn_backward(gradient, second, norm_gain[1], ffn_in[0], ffn_out[0])
    input_grad, self_grads = self_backward(
        middle_grad, first_state, norm_gain[0], attn_in[0], attn_out[0], source_keys
    )
    sharded = (
        self_grads[0][None],
        self_grads[1][None],
        self_grads[2][None],
        ffn_grads[0][None],
        ffn_grads[1][None],
        ffn_grads[2][None],
    )
    shared = (
        jnp.stack([self_grads[4], ffn_grads[4]]),
        jnp.stack([self_grads[5], ffn_grads[5]]),
        self_grads[3][None],
        ffn_grads[3][None],
    )
    return (input_grad, sharded, shared)


def on_device(
    src_embed,
    tgt_embed,
    src_mask,
    tgt_mask,
    objective,
    loss_mask,
    enc_cot,
    dec_cot,
    norm_gain,
    norm_bias,
    attn_in,
    attn_in_bias,
    attn_out,
    attn_out_bias,
    ffn_in,
    ffn_in_bias,
    ffn_out,
    ffn_out_bias,
):
    params = (
        norm_gain,
        norm_bias,
        attn_in,
        attn_in_bias,
        attn_out,
        attn_out_bias,
        ffn_in,
        ffn_in_bias,
        ffn_out,
        ffn_out_bias,
    )
    source_keys = (src_mask == 1)[:, None, None, :]
    target_len = tgt_mask.shape[1]
    causal = lax.broadcasted_iota(jnp.int32, (target_len, target_len), 0) >= lax.broadcasted_iota(
        jnp.int32, (target_len, target_len), 1
    )
    target_allowed = (tgt_mask == 1)[:, None, None, :] & causal[None, None]
    source_in = src_embed.astype(jnp.float32)
    target_in = tgt_embed.astype(jnp.float32)
    encoded, enc_states = run_encoder(source_in, params, source_keys)
    memory_low = encoded.astype(jnp.bfloat16)
    decoded, dec_states = run_decoder(target_in, memory_low, params, target_allowed, source_keys)
    flag = objective.astype(jnp.float32)
    weight_enc = 1.0 - 0.5 * flag
    weight_dec = 0.5 + 0.5 * flag
    position_weight = jnp.transpose(0.25 + 0.75 * loss_mask.astype(jnp.float32))
    enc_cotan = enc_cot.astype(jnp.float32) * weight_enc[None, :, None]
    dec_cotan = (
        dec_cot.astype(jnp.float32) * weight_dec[None, :, None] * position_weight[:, :, None]
    )
    target_again, memory_again, params_again = lax.optimization_barrier(
        (target_in, memory_low, params)
    )
    unused_out, dec_states = run_decoder(
        target_again, memory_again, params_again, target_allowed, source_keys
    )
    target_grad, memory_grad, dec_sharded, dec_shared = decoder_backward(
        dec_cotan, dec_states, params, target_allowed, source_keys
    )
    source_again, params_again = lax.optimization_barrier((source_in, params))
    unused_out, enc_states = run_encoder(source_again, params_again, source_keys)
    source_grad, enc_sharded, enc_shared = encoder_backward(
        enc_cotan + memory_grad, enc_states, params, source_keys
    )
    (
        in_weight_sum,
        in_bias_sum,
        out_weight_sum,
        first_weight_sum,
        first_bias_sum,
        second_weight_sum,
    ) = lax.psum(
        (
            jnp.concatenate([enc_sharded[0], dec_sharded[0]], axis=0),
            jnp.concatenate([enc_sharded[1], dec_sharded[1]], axis=0),
            jnp.concatenate([enc_sharded[2], dec_sharded[2]], axis=0),
            jnp.concatenate([enc_sharded[3], dec_sharded[3]], axis=0),
            jnp.concatenate([enc_sharded[4], dec_sharded[4]], axis=0),
            jnp.concatenate([enc_sharded[5], dec_sharded[5]], axis=0),
        ),
        "dp",
    )
    gain_sum, shift_sum, attn_bias_sum, ffn_bias_sum = lax.psum(
        (
            jnp.concatenate([enc_shared[0], dec_shared[0]], axis=0),
            jnp.concatenate([enc_shared[1], dec_shared[1]], axis=0),
            jnp.concatenate([enc_shared[2], dec_shared[2]], axis=0),
            jnp.concatenate([enc_shared[3], dec_shared[3]], axis=0),
        ),
        ("dp", "tensor"),
    )
    return (
        memory_low,
        decoded.astype(jnp.bfloat16),
        source_grad,
        target_grad,
        gain_sum,
        shift_sum,
        in_weight_sum,
        in_bias_sum,
        out_weight_sum,
        attn_bias_sum,
        first_weight_sum,
        first_bias_sum,
        second_weight_sum,
        ffn_bias_sum,
    )


def solution(mesh):
    return jax.shard_map(
        on_device,
        mesh=mesh,
        in_specs=(
            P("tensor", "dp", None),
            P("tensor", "dp", None),
            P("dp", None),
            P("dp", None),
            P("dp"),
            P("dp", "tensor"),
            P("tensor", "dp", None),
            P("tensor", "dp", None),
            P(),
            P(),
            P(None, None, None, "tensor"),
            P(None, None, "tensor"),
            P(None, "tensor", None),
            P(),
            P(None, None, "tensor"),
            P(None, "tensor"),
            P(None, "tensor", None),
            P(),
        ),
        out_specs=(
            P("tensor", "dp", None),
            P("tensor", "dp", None),
            P("tensor", "dp", None),
            P("tensor", "dp", None),
            P(),
            P(),
            P(None, None, None, "tensor"),
            P(None, None, "tensor"),
            P(None, "tensor", None),
            P(),
            P(None, None, "tensor"),
            P(None, "tensor"),
            P(None, "tensor", None),
            P(),
        ),
        check_vma=False,
    )
```

profile of v0, /device:TPU:0, one launch (start us, length us, event | category | flops | bytes accessed | tf_op | source)
XLA Modules:
  0.0 1189.7 jit_solution(12436464618606596135)
XLA Ops:
  14.0 12.8 %all_gather.51 = bf16[512,1,768]{2,0,1:T(8,128)(2,1)S(1)} all-gather(bf16[256,1,768]{2,0,1:T(8,128)(2,1)S(1)} %add_convert_fusion.10), channel_id=1, replica_groups=mesh['dp'=16,'tensor'=2] {'tensor'}, dimensions={0}, use_global_device_ids=true | all-gather | bytes 1179648 | tf_op jit(solution)/shard_map/all_gather | solution.py:32
  30.9 5.2 fusion.279
  36.1 3.6 fusion.146
  42.8 26.4 %reduce-scatter.15.cloned.1.call-done = f32[256,1,768]{2,0,1:T(8,128)} async-done(((f32[512,1,768]{2,0,1:T(8,128)}), f32[256,1,768]{2,0,1:T(8,128)}) %reduce-scatter.15.cloned.1.call-update) | async-done | bytes 786448 | tf_op jit(solution)/shard_map/reduce_scatter | solution.py:41
  73.3 11.7 all_gather.52
  85.0 6.7 fusion.119
  94.5 23.3 %reduce-scatter.17.cloned.1.call-done = f32[256,1,768]{2,0,1:T(8,128)} async-done(((f32[512,1,768]{2,0,1:T(8,128)}), f32[256,1,768]{2,0,1:T(8,128)}) %reduce-scatter.17.cloned.1.call-update) | async-done | bytes 786448 | tf_op jit(solution)/shard_map/reduce_scatter | solution.py:41
  121.9 7.8 all_gather.57
  129.7 8.7 copy.82
  152.1 19.1 %all_gather.59 = bf16[512,1,768]{2,0,1:T(8,128)(2,1)S(1)} all-gather(bf16[256,1,768]{2,0,1:T(8,128)(2,1)S(1)} %copy-done.20), channel_id=1, replica_groups=mesh['dp'=16,'tensor'=2] {'tensor'}, dimensions={0}, use_global_device_ids=true | all-gather | bytes 1179648 | tf_op jit(solution)/shard_map/all_gather | solution.py:32
  178.1 6.3 all_gather.58
  197.2 8.6 copy.90
  205.8 13.7 %all_gather.63 = bf16[512,1,768]{2,0,1:T(8,128)(2,1)S(1)} all-gather(bf16[256,1,768]{2,0,1:T(8,128)(2,1)} %add_convert_fusion.3), channel_id=1, replica_groups=mesh['dp'=16,'tensor'=2] {'tensor'}, dimensions={0}, use_global_device_ids=true | all-gather | bytes 1179648 | tf_op jit(solution)/shard_map/all_gather | solution.py:32
  223.9 6.4 all_gather.60
  235.1 6.3 all_gather.61
  244.8 4.4 convert_reduce_fusion.1
  252.0 5.6 fusion.284
  258.9 3.8 fusion.3
  277.9 10.5 all_gather.62
  311.7 9.0 reduce-scatter.39.cloned.1.call-done
  325.4 7.3 all_gather.67
  357.7 19.3 %all_gather.65 = bf16[512,1,768]{2,0,1:T(8,128)(2,1)} all-gather(bf16[256,1,768]{2,0,1:T(8,128)(2,1)S(1)} %add_convert_fusion), channel_id=1, replica_groups=mesh['dp'=16,'tensor'=2] {'tensor'}, dimensions={0}, use_global_device_ids=true | all-gather | bytes 1179648 | tf_op jit(solution)/shard_map/all_gather | solution.py:32
  386.0 4.8 convolution_add_fusion
  390.8 16.8 %all_gather.54 = bf16[512,1,768]{2,0,1:T(8,128)(2,1)S(1)} all-gather(bf16[256,1,768]{2,0,1:T(8,128)(2,1)S(1)} %copy-done.21), channel_id=1, replica_groups=mesh['dp'=16,'tensor'=2] {'tensor'}, dimensions={0}, use_global_device_ids=true | all-gather | bytes 1179648 | tf_op jit(solution)/shard_map/all_gather | solution.py:32
  418.8 6.3 all_gather.53
  435.0 12.9 %all_gather.64 = bf16[512,1,768]{2,0,1:T(8,128)(2,1)S(1)} all-gather(bf16[256,1,768]{2,0,1:T(8,128)(2,1)S(1)} %get-tuple-element.152), channel_id=1, replica_groups=mesh['dp'=16,'tensor'=2] {'tensor'}, dimensions={0}, use_global_device_ids=true | all-gather | bytes 1179648 | tf_op jit(solution)/shard_map/all_gather | solution.py:50
  448.0 6.0 convert_reduce_fusion
  455.2 4.3 fusion.116
  460.1 4.1 convolution_bitcast_fusion.2
  472.5 10.5 all_gather.55
  486.3 4.0 fusion.283
  499.6 15.3 %all_gather.66 = bf16[512,1,768]{2,0,1:T(8,128)(2,1)S(1)} all-gather(bf16[256,1,768]{2,0,1:T(8,128)(2,1)S(1)} %get-tuple-element.156), channel_id=1, replica_groups=mesh['dp'=16,'tensor'=2] {'tensor'}, dimensions={0}, use_global_device_ids=true | all-gather | bytes 1179648 | tf_op jit(solution)/shard_map/all_gather | solution.py:50
  515.8 4.6 convert_reduce_fusion.5
  521.4 7.5 multiply_reduce_fusion
  530.5 6.3 all_gather.56
  536.8 4.8 fusion.130
  541.7 6.4 multiply_convert_fusion
  556.4 4.2 fusion.112
  565.4 3.9 convolution_bitcast_fusion.1
  569.3 8.2 pad_maximum_fusion.2
  577.5 4.6 pad_maximum_fusion.1
  587.7 5.2 pad_maximum_fusion
  595.7 61.0 %all-reduce.1 = (f32[3,2,384]{2,1,0:T(2,128)}, f32[2,1536]{1,0:T(2,128)}) all-reduce(f32[3,2,384]{2,1,0:T(2,128)S(1)} %pad_maximum_fusion.6, f32[2,1536]{1,0:T(2,128)S(1)} %pad_maximum_fusion.5), channel_id=1, replica_groups=mesh['dp'=16,'tensor'=2] {'dp'}, use_global_device_ids=true, to_apply=%region_78.79 | all-reduce | flops 5376 | bytes 43008 | tf_op jit(solution)/shard_map/psum | solution.py:482
  663.3 40.8 %all-reduce = (f32[5,768]{1,0:T(8,128)}, f32[5,768]{1,0:T(8,128)}, f32[3,768]{1,0:T(4,128)}, f32[2,768]{1,0:T(2,128)}) all-reduce(f32[5,768]{1,0:T(8,128)S(1)} %concatenate.33, f32[5,768]{1,0:T(8,128)S(1)} %concatenate.34, f32[3,768]{1,0:T(4,128)S(1)} %pad_maximum_fusion.4, ...), channel_id=1, replica_groups=mesh['dp'=16,'tensor'=2] {'dp','tensor'}, use_global_device_ids=true, to_apply=%region_64.65 | all-reduce | flops 11520 | bytes 92160 | tf_op jit(solution)/shard_map/psum | solution.py:493
  704.0 451.6 %all-reduce.5.cloned.1.call-done = (f32[3,3,768,384]{2,3,1,0:T(8,128)}, f32[3,384,768]{2,1,0:T(8,128)}, f32[2,768,1536]{2,1,0:T(8,128)}, f32[2,1536,768]{2,1,0:T(8,128)}) async-done(((f32[3,3,768,384]{2,3,1,0:T(8,128)}, f32[3,384,768]{2,1,0:T(8,128)}, f32[2,768,1536]{2,1,0:T(8,128)}, f32[2,1536,768]{2,1,0:T(8,128)}), (f32[3,3,768,384]{2,3,1,0:T(8,128)}, f32[3,384,768]{2,1,0:T(8,128)}, ...) | async-done | bytes 33030160 | tf_op jit(solution)/shard_map/psum | solution.py:482
  1155.6 12.8 %copy.112 = f32[3,3,768,384]{3,2,1,0:T(8,128)} copy(f32[3,3,768,384]{2,3,1,0:T(8,128)} %get-tuple-element.147) | data formatting | bytes 21233664
  1170.2 9.0 copy.137
  1179.3 3.7 copy.138
  (625 shorter events, 226.5 us)
Async XLA Ops:
  7.2 62.0 %reduce-scatter.15.cloned.1.call-start = ((), (), s32[]{:S(2)}) async-start(), calls=%async_computation.14 | async-start | bytes 2359296 | tf_op jit(solution)/shard_map/reduce_scatter | solution.py:41
  11.2 60.7 %copy-start.93 = (f32[768]{0:T(1024)}, f32[768]{0:T(1024)S(1)}, u32[]{:S(2)}) copy-start(f32[768]{0:T(1024)S(1)} %get-tuple-element.113) | copy-start | bytes 9220
  39.7 29.5 %copy-start.5 = (bf16[256,1,768]{2,0,1:T(8,128)(2,1)S(1)}, bf16[256,1,768]{2,0,1:T(8,128)(2,1)}, u32[]{:S(2)}) copy-start(bf16[256,1,768]{2,0,1:T(8,128)(2,1)} %param.18) | copy-start | bytes 1179652
  41.5 76.3 %reduce-scatter.17.cloned.1.call-start = ((), (), s32[]{:S(2)}) async-start(), calls=%async_computation.15 | async-start | bytes 2359296 | tf_op jit(solution)/shard_map/reduce_scatter | solution.py:41
  85.0 32.9 %copy-start.12 = (f32[256,1,768]{2,0,1:T(8,128)S(1)}, f32[256,1,768]{2,0,1:T(8,128)}, u32[]{:S(2)}) copy-start(f32[256,1,768]{2,0,1:T(8,128)} %reduce-scatter.15.cloned.1.call-done) | copy-start | bytes 2359300
  91.6 84.5 %reduce-scatter.25.cloned.1.call-start = ((), (), s32[]{:S(2)}) async-start(), calls=%async_computation.19 | async-start | bytes 1179648 | tf_op jit(solution)/shard_map/reduce_scatter | solution.py:41
  129.7 8.7 copy-start.47
  148.0 84.2 %reduce-scatter.27.cloned.1.call-start = ((), (), s32[]{:S(2)}) async-start(), calls=%async_computation.20 | async-start | bytes 1179648 | tf_op jit(solution)/shard_map/reduce_scatter | solution.py:41
  148.1 25.5 %copy-start.3 = (f32[256,1,768]{2,0,1:T(8,128)}, f32[256,1,768]{2,0,1:T(8,128)S(1)}, u32[]{:S(2)}) copy-start(f32[256,1,768]{2,0,1:T(8,128)S(1)} %convert_element_type.660) | copy-start | bytes 2359300
  150.3 23.3 %copy-start.107 = (f32[256]{0:T(256)}, f32[256]{0:T(256)S(1)}, u32[]{:S(2)}) copy-start(f32[256]{0:T(256)S(1)} %broadcast_multiply_fusion.5) | copy-start | bytes 3076
  173.7 11.6 copy-start.161
  194.5 78.7 %reduce-scatter.29.cloned.1.call-start = ((), (), s32[]{:S(2)}) async-start(), calls=%async_computation.21 | async-start | bytes 1179648 | tf_op jit(solution)/shard_map/reduce_scatter | solution.py:59
  233.5 11.3 copy-start.73
  242.2 7.9 slice-start.5
  251.8 55.6 %reduce-scatter.33.cloned.1.call-start = ((), (), s32[]{:S(2)}) async-start(), calls=%async_computation.23 | async-start | bytes 2359296 | tf_op jit(solution)/shard_map/reduce_scatter | solution.py:41
  269.5 51.1 %reduce-scatter.39.cloned.1.call-start = ((), (), s32[]{:S(2)}) async-start(), calls=%async_computation.26 | async-start | bytes 1179648 | tf_op jit(solution)/shard_map/reduce_scatter | solution.py:59
  273.2 22.1 %copy-start.83 = (f32[6,256]{1,0:T(8,128)}, f32[6,256]{1,0:T(8,128)S(1)}, u32[]{:S(2)}) copy-start(f32[6,256]{1,0:T(8,128)S(1)} %log_add_fusion.2) | copy-start | bytes 18436
  297.2 7.7 copy-start.166
  301.6 113.4 %reduce-scatter.41.cloned.1.call-start = ((), (), s32[]{:S(2)}) async-start(), calls=%async_computation.27 | async-start | bytes 1179648 | tf_op jit(solution)/shard_map/reduce_scatter | solution.py:59
  354.3 78.8 %reduce-scatter.31.cloned.1.call-start = ((), (), s32[]{:S(2)}) async-start(), calls=%async_computation.22 | async-start | bytes 2359296 | tf_op jit(solution)/shard_map/reduce_scatter | solution.py:59
  354.4 22.6 %copy-start.41 = (bf16[256,384]{0,1:T(8,128)(2,1)S(1)}, bf16[256,384]{0,1:T(8,128)(2,1)}, u32[]{:S(2)}) copy-start(bf16[256,384]{0,1:T(8,128)(2,1)} %copy.86) | copy-start | bytes 589828
  354.4 22.6 %copy-start.84 = (f32[6,256]{1,0:T(8,128)S(1)}, f32[6,256]{1,0:T(8,128)}, u32[]{:S(2)}) copy-start(f32[6,256]{1,0:T(8,128)} %copy-done.83) | copy-start | bytes 18436
  382.5 8.3 copy-start.60
  385.9 83.0 %reduce-scatter.19.cloned.1.call-start = ((), (), s32[]{:S(2)}) async-start(), calls=%async_computation.16 | async-start | bytes 1179648 | tf_op jit(solution)/shard_map/reduce_scatter | solution.py:41
  433.1 61.3 %reduce-scatter.35.cloned.1.call-start = ((), (), s32[]{:S(2)}) async-start(), calls=%async_computation.24 | async-start | bytes 2359296 | tf_op jit(solution)/shard_map/reduce_scatter | solution.py:59
  459.6 69.3 %reduce-scatter.21.cloned.1.call-start = ((), (), s32[]{:S(2)}) async-start(), calls=%async_computation.17 | async-start | bytes 1179648 | tf_op jit(solution)/shard_map/reduce_scatter | solution.py:41
  466.9 16.1 %copy-start.163 = (f32[384]{0:T(512)S(1)}, f32[384]{0:T(512)}, u32[]{:S(2)}) copy-start(f32[384]{0:T(512)} %get-tuple-element.134) | copy-start | bytes 4612
  468.9 17.4 %copy-start.75 = (bf16[1,512,1,384]{1,3,0,2:T(8,128)(2,1)S(1)}, bf16[1,512,1,384]{1,3,0,2:T(8,128)(2,1)}, u32[]{:S(2)}) copy-start(bf16[1,512,1,384]{1,3,0,2:T(8,128)(2,1)} %slice.606) | copy-start | bytes 1179652
  494.3 162.4 %reduce-scatter.23.cloned.1.call-start = ((), (), s32[]{:S(2)}) async-start(), calls=%async_computation.18 | async-start | bytes 1179648 | tf_op jit(solution)/shard_map/reduce_scatter | solution.py:41
  521.3 7.6 copy-start.16
  521.3 7.6 copy-start.86
  521.4 8.9 copy-start.92
  521.4 8.9 copy-start.115
  521.4 15.4 %copy-start.142 = (f32[1536]{0:T(1024)S(1)}, f32[1536]{0:T(1024)}, u32[]{:S(2)}) copy-start(f32[1536]{0:T(1024)} %get-tuple-element.122) | copy-start | bytes 18436
  541.7 116.8 %reduce-scatter.37.cloned.1.call-start = ((), (), s32[]{:S(2)}) async-start(), calls=%async_computation.25 | async-start | bytes 2359296 | tf_op jit(solution)/shard_map/reduce_scatter | solution.py:59
  560.7 594.9 %all-reduce.5.cloned.1.call-start = ((), (), s32[]{:S(2)}) async-start(), calls=%async_computation.28 | async-start | bytes 66060288 | tf_op jit(solution)/shard_map/psum | solution.py:482
  565.4 12.1 %slice-start = ((s8[4718592]{0:T(1024)(128)(4,1)}), s8[4194304]{0:T(1024)(128)(4,1)S(1)}, s32[]{:S(2)}) async-start(s8[4718592]{0:T(1024)(128)(4,1)} %bitcast.457), calls=%async_computation.29 | async-start | bytes 8388608
  569.3 8.2 slice-start.1
  593.1 63.6 %copy-start.114 = (f32[768]{0:T(1024)S(1)}, f32[768]{0:T(1024)}, u32[]{:S(2)}) copy-start(f32[768]{0:T(1024)} %get-tuple-element.139) | copy-start | bytes 9220
  593.2 65.3 %copy-start.4 = (f32[256,1,768]{2,0,1:T(8,128)S(1)}, f32[256,1,768]{2,0,1:T(8,128)}, u32[]{:S(2)}) copy-start(f32[256,1,768]{2,0,1:T(8,128)} %copy-done.3) | copy-start | bytes 2359300
  593.2 65.3 %copy-start.91 = (f32[768]{0:T(1024)S(1)}, f32[768]{0:T(1024)}, u32[]{:S(2)}) copy-start(f32[768]{0:T(1024)} %copy-done.90) | copy-start | bytes 9220
  593.2 65.3 %copy-start.108 = (f32[256]{0:T(256)S(1)}, f32[256]{0:T(256)}, u32[]{:S(2)}) copy-start(f32[256]{0:T(256)} %copy-done.107) | copy-start | bytes 3076
  593.2 65.3 %copy-start.112 = (f32[256]{0:T(256)S(1)}, f32[256]{0:T(256)}, u32[]{:S(2)}) copy-start(f32[256]{0:T(256)} %copy-done.111) | copy-start | bytes 3076
  593.2 66.8 %copy-start.30 = (f32[256,1,768]{2,0,1:T(8,128)S(1)}, f32[256,1,768]{2,0,1:T(8,128)}, u32[]{:S(2)}) copy-start(f32[256,1,768]{2,0,1:T(8,128)} %get-tuple-element.157) | copy-start | bytes 2359300
  1155.6 12.8 %copy-start.19 = (f32[3,384,768]{2,1,0:T(8,128)S(1)}, f32[3,384,768]{2,1,0:T(8,128)}, u32[]{:S(2)}) copy-start(f32[3,384,768]{2,1,0:T(8,128)} %get-tuple-element.229) | copy-start | bytes 10616836
  1168.4 10.8 slice-start.2
  1170.2 9.0 slice-start.3
  1170.2 9.0 slice-start.4
  (146 other events, 442.7 us)
Sparse Core Ops, SparseCore 0:
  41.6 27.5 reduce-scatter.14
  91.8 26.0 reduce-scatter.16
  148.1 24.0 reduce-scatter.24
  194.6 22.5 reduce-scatter.26
  251.9 17.4 reduce-scatter.28
  272.2 28.1 reduce-scatter.32
  303.2 17.4 reduce-scatter.38
  354.4 23.6 reduce-scatter.40
  386.1 32.3 reduce-scatter.30
  433.2 19.7 reduce-scatter.18
  459.7 28.1 reduce-scatter.34
  494.4 20.8 reduce-scatter.20
  541.8 17.4 reduce-scatter.22
  561.5 26.0 reduce-scatter.36
  593.4 562.1 all-reduce.4
where the time goes:
time: 1200 us; the launch traced here: 1190 us
  waiting for transfers between devices  511 us (43%)
  blocking collectives  291 us (24%)
  matrix products  165 us (14%)
  local copies, waits for them, and re-layouts  111 us (9%)
  other arithmetic  93.7 us (8%)
  between operations  16.9 us (1%)
    psum x1, waiting for transfers between devices, on_device(): lax.psum((jnp.concatenate([enc_sharded[0], dec_sharded[0]], axis=0), jnp....  452 us
    all_gather x12, blocking collectives, spread_rows(): return lax.all_gather(values, 'tensor', axis=0, tiled=True)  137 us
    psum x1, blocking collectives, on_device(): lax.psum((jnp.concatenate([enc_sharded[0], dec_sharded[0]], axis=0), jnp....  61 us
    all_gather x5, blocking collectives, spread_grads(): return lax.all_gather(values, 'tensor', axis=0, tiled=True)  52.5 us
    reduce_scatter x8, waiting for transfers between devices, collect_rows(): lax.psum_scatter(term(jnp.int32(0), lax.axis_size('tensor') * local_rows)...  49.8 us
    unnamed x364, local copies, waits for them, and re-layouts  48.2 us
    psum x1, blocking collectives, on_device(): lax.psum((jnp.concatenate([enc_shared[0], dec_shared[0]], axis=0), jnp.co...  40.8 us
  transfers between devices with their start and end apart: 15, of which 4 were waited for; matrix products, arithmetic and copies ran while one was open for 18% of the time, Pallas kernels for 0%

commit v1 on v0

v1 whole, which is shorter than its diff:
```python
import functools

import jax
import jax.numpy as jnp
from jax import lax
from jax.experimental import pallas as pl
from jax.experimental.pallas import tpu as pltpu
from jax.sharding import PartitionSpec as P

HEAD = 64
EPSILON = 1e-05
MASKED_SCORE = -1000000000.0
BF16 = jnp.bfloat16
F32 = jnp.float32


def dot(left, right, contract):
    return lax.dot_general(left, right, (contract, ((), ())), preferred_element_type=F32)


def rows_by_cols(left, right):
    return dot(left, right, ((1,), (0,)))


def rows_by_rows(left, right):
    return dot(left, right, ((1,), (1,)))


def cols_by_cols(left, right):
    return dot(left, right, ((0,), (0,)))


def swap(values):
    return lax.ppermute(values, "tensor", [(0, 1), (1, 0)])


def flip(values):
    half = values.shape[0] // 2
    return jnp.concatenate([values[half:], values[:half]], axis=0)


def both_halves(own):
    return jnp.concatenate([own, swap(own)], axis=0)


def pair_sum(partial):
    return partial + flip(swap(partial.astype(BF16))).astype(F32)


def own_sum(partial):
    half = partial.shape[0] // 2
    return partial[:half] + swap(partial[half:].astype(BF16)).astype(F32)


def norm_forward(inputs, gain, offset):
    centre = inputs - jnp.mean(inputs, axis=-1, keepdims=True)
    inverse = lax.rsqrt(jnp.mean(centre * centre, axis=-1, keepdims=True) + EPSILON)
    normed = centre * inverse
    return (normed * gain + offset).astype(BF16), (normed, inverse)


def norm_backward(gradient, kept, gain):
    normed, inverse = kept
    half = (normed.shape[0] // 2)
    gain_grad = jnp.sum(gradient[:half] * normed[:half], axis=0)
    offset_grad = jnp.sum(gradient[:half], axis=0)
    scaled = gradient * gain
    mean_plain = jnp.mean(scaled, axis=-1, keepdims=True)
    mean_normed = jnp.mean(scaled * normed, axis=-1, keepdims=True)
    return inverse * (scaled - mean_plain - normed * mean_normed), gain_grad, offset_grad


def split_heads(values):
    return values.reshape(values.shape[0], values.shape[1] // HEAD, HEAD)


def head_scores(queries, key_rows, allowed):
    scores = jnp.einsum(
        "qhd,khd->hqk", split_heads(queries), split_heads(key_rows), preferred_element_type=F32
    ) * HEAD ** (-0.5)
    return jnp.where(allowed, scores, MASKED_SCORE)


def attend(queries, key_rows, value_rows, allowed):
    scores = head_scores(queries, key_rows, allowed)
    row_max = jnp.max(scores, axis=-1, keepdims=True)
    exponent = jnp.exp(scores - row_max)
    row_total = jnp.sum(exponent, axis=-1, keepdims=True)
    weights = (exponent / row_total).astype(BF16)
    mixture = jnp.einsum(
        "hqk,khd->qhd", weights, split_heads(value_rows), preferred_element_type=F32
    )
    return mixture.reshape(queries.shape).astype(BF16), row_max + jnp.log(row_total)


def attend_backward(mixture_grad, queries, key_rows, value_rows, allowed, log_total):
    scale = HEAD ** (-0.5)
    probs = jnp.exp(head_scores(queries, key_rows, allowed) - log_total)
    grad_heads = split_heads(mixture_grad)
    prob_grad = jnp.einsum(
        "qhd,khd->hqk", grad_heads, split_heads(value_rows), preferred_element_type=F32
    )
    row_inner = jnp.sum(probs * prob_grad, axis=-1, keepdims=True)
    score_grad = (probs * (prob_grad - row_inner)).astype(BF16)
    query_grad = (
        jnp.einsum("hqk,khd->qhd", score_grad, split_heads(key_rows), preferred_element_type=F32)
        * scale
    )
    key_grad = (
        jnp.einsum("hqk,qhd->khd", score_grad, split_heads(queries), preferred_element_type=F32)
        * scale
    )
    value_grad = jnp.einsum(
        "hqk,qhd->khd", probs.astype(BF16), grad_heads, preferred_element_type=F32
    )
    return (
        query_grad.reshape(queries.shape).astype(BF16),
        key_grad.reshape(key_rows.shape).astype(BF16),
        value_grad.reshape(value_rows.shape).astype(BF16),
    )


def bits_of_dp():
    count = lax.axis_size("dp")
    here = lax.axis_index("dp")
    return [(1 << b, (here >> b) & 1) for b in range(count.bit_length() - 1)]


def across(values, stride):
    count = lax.axis_size("dp")
    return lax.ppermute(values, "dp", [(i, i ^ stride) for i in range(count)])


def join_body(bit_ref, own_ref, other_ref, out_ref):
    bit = bit_ref[0]
    out_ref[pl.ds(bit, 1)] = own_ref[...][None]
    out_ref[pl.ds(1 - bit, 1)] = other_ref[...][None]


def join(bit, own, other):
    rows, width = own.shape
    return pl.pallas_call(
        join_body,
        out_shape=jax.ShapeDtypeStruct((2, rows, width), own.dtype),
        in_specs=[
            pl.BlockSpec(memory_space=pltpu.SMEM),
            pl.BlockSpec(memory_space=pltpu.VMEM),
            pl.BlockSpec(memory_space=pltpu.VMEM),
        ],
        out_specs=pl.BlockSpec(memory_space=pltpu.VMEM),
    )(bit.reshape(1), own, other).reshape(2 * rows, width)


def place_body(parts, bit_ref, own_ref, other_ref, *refs):
    out_ref = refs[-1]
    bit = bit_ref[0]
    width = own_ref.shape[1] // parts
    for part in range(parts):
        columns = pl.ds(part * width, width)
        out_ref[0, part, pl.ds(bit, 1)] = own_ref[:, columns].astype(F32)[None]
        out_ref[0, part, pl.ds(1 - bit, 1)] = other_ref[:, columns].astype(F32)[None]


def place(bit, own, other, stacked, layer, layers, parts):
    rows, width = own.shape
    block = rows
    while block * width > 192 * 1024 and block % 32 == 0:
        block //= 2
    shape = (layers, parts, 2, rows, width // parts)
    aliased = stacked is not None
    return pl.pallas_call(
        functools.partial(place_body, parts),
        grid=(rows // block,),
        out_shape=jax.ShapeDtypeStruct(shape, F32),
        in_specs=[
            pl.BlockSpec(memory_space=pltpu.SMEM),
            pl.BlockSpec((block, width), lambda i: (i, 0)),
            pl.BlockSpec((block, width), lambda i: (i, 0)),
        ]
        + ([pl.BlockSpec(memory_space=pl.ANY)] if aliased else []),
        out_specs=pl.BlockSpec(
            (1, parts, 2, block, width // parts), lambda i: (layer, 0, 0, i, 0)
        ),
        input_output_aliases={3: 0} if aliased else {},
    )(bit.reshape(1), own, other, *([stacked] if aliased else []))


def scatter_sum(payload):
    current = payload
    for stride, bit in bits_of_dp():
        halves = current.reshape(2, current.shape[0] // 2, current.shape[1])
        send = lax.dynamic_index_in_dim(halves, 1 - bit, 0, keepdims=False)
        keep = lax.dynamic_index_in_dim(halves, bit, 0, keepdims=False)
        received = across(send.astype(BF16), stride)
        current = keep.astype(F32) + received.astype(F32)
        current = current.astype(BF16)
    return current


def gather_sum(shard, place_last):
    bits = bits_of_dp()
    current = shard
    for stride, bit in bits[:0:-1]:
        current = join(bit, current, across(current, stride))
    stride, bit = bits[0]
    return place_last(bit, current, across(current, stride))


def total_small(values):
    for stride, bit in bits_of_dp():
        values = values + across(values, stride)
    return values


def gelu_parts(hidden):
    cubic = 0.7978845608028654 * (hidden + 0.044715 * hidden * hidden * hidden)
    bent = jnp.tanh(cubic)
    return 0.5 * hidden * (1.0 + bent), bent


def gelu_slope(hidden, bent):
    inner = 0.7978845608028654 * (1.0 + 3 * 0.044715 * hidden * hidden)
    return 0.5 * (1.0 + bent) + 0.5 * hidden * (1.0 - bent * bent) * inner


def on_device(
    src_embed,
    tgt_embed,
    src_mask,
    tgt_mask,
    objective,
    loss_mask,
    enc_cot,
    dec_cot,
    norm_gain,
    norm_bias,
    attn_in,
    attn_in_bias,
    attn_out,
    attn_out_bias,
    ffn_in,
    ffn_in_bias,
    ffn_out,
    ffn_out_bias,
):
    here = lax.axis_index("tensor")
    width = src_embed.shape[2]
    local = attn_in.shape[3]
    source = both_halves(src_embed.reshape(-1, width)).astype(F32)
    target = both_halves(tgt_embed.reshape(-1, width)).astype(F32)
    enc_seed = both_halves(enc_cot.reshape(-1, width))
    dec_seed = both_halves(dec_cot.reshape(-1, width))
    loss_seed = both_halves(loss_mask.reshape(-1, 1).astype(F32))
    source_count = source.shape[0]
    target_count = target.shape[0]

    def positions(count):
        half = count // 2
        index = jnp.arange(count, dtype=jnp.int32)
        return lax.rem(index + here * half, count)

    source_real = src_mask.reshape(2, -1)
    source_real = jnp.where(here == 0, source_real, source_real[::-1]).reshape(-1) == 1
    target_real = tgt_mask.reshape(2, -1)
    target_real = jnp.where(here == 0, target_real, target_real[::-1]).reshape(-1) == 1
    target_position = positions(target_count)
    source_allowed = source_real[None, None, :]
    target_allowed = (
        target_real[None, :] & (target_position[:, None] >= target_position[None, :])
    )[None]

    def project(inputs, layer, which):
        result = rows_by_cols(inputs, attn_in[layer, which])
        if which == 0:
            result = result + attn_in_bias[layer, 0]
        if which == 2:
            result = result + attn_in_bias[layer, 1]
        return result.astype(BF16)

    def attention(inputs, memory, norm, layer, allowed):
        hidden, kept = norm_forward(inputs, norm_gain[norm], norm_bias[norm])
        keys_from = hidden if memory is None else memory
        queries = project(hidden, layer, 0)
        key_rows = project(keys_from, layer, 1)
        value_rows = project(keys_from, layer, 2)
        mixture, log_total = attend(queries, key_rows, value_rows, allowed)
        partial = rows_by_cols(mixture, attn_out[layer])
        result = inputs + (pair_sum(partial) + attn_out_bias[layer])
        return result, (kept, hidden, keys_from, queries, key_rows, value_rows, mixture, log_total)

    def feed(inputs, norm, layer):
        hidden, kept = norm_forward(inputs, norm_gain[norm], norm_bias[norm])
        before = rows_by_cols(hidden, ffn_in[layer]) + ffn_in_bias[layer]
        active, bent = gelu_parts(before)
        active = active.astype(BF16)
        partial = rows_by_cols(active, ffn_out[layer])
        return partial, (kept, hidden, before, active)

    middle, enc_attention = attention(source, None, 0, 0, source_allowed)
    partial, enc_feed = feed(middle, 1, 0)
    encoded = middle + (pair_sum(partial) + ffn_out_bias[0])
    memory = encoded.astype(BF16)
    first, dec_attention = attention(target, None, 2, 1, target_allowed)
    second, dec_cross = attention(first, memory, 3, 2, source_allowed)
    partial, dec_feed = feed(second, 4, 1)
    half = target_count // 2
    decoded = second[:half] + (own_sum(partial) + ffn_out_bias[1])

    flag = objective.astype(F32)[0]
    enc_cotan = enc_seed.astype(F32) * (1.0 - 0.5 * flag)
    dec_cotan = dec_seed.astype(F32) * (0.5 + 0.5 * flag) * (0.25 + 0.75 * loss_seed)

    small = {}

    def feed_backward(gradient, kept_all, norm, layer):
        kept, hidden, before, active = kept_all
        low = gradient.astype(BF16)
        small["ffn_out_bias", layer] = jnp.sum(low[: low.shape[0] // 2].astype(F32), axis=0)
        out_grad = cols_by_cols(active, low).astype(BF16)
        active_grad = rows_by_rows(low, ffn_out[layer])
        unused, bent = gelu_parts(before)
        before_grad = (active_grad * gelu_slope(before, bent)).astype(BF16)
        in_grad = cols_by_cols(hidden, before_grad).astype(BF16)
        small["ffn_in_bias", layer] = jnp.sum(before_grad.astype(F32), axis=0)
        partial = rows_by_rows(before_grad, ffn_in[layer])
        input_grad, gain_grad, offset_grad = norm_backward(
            pair_sum(partial), kept, norm_gain[norm]
        )
        small["gain", norm], small["offset", norm] = gain_grad, offset_grad
        return gradient + input_grad, in_grad, out_grad

    def attention_backward(gradient, kept_all, norm, layer, allowed, cross, last):
        kept, hidden, keys_from, queries, key_rows, value_rows, mixture, log_total = kept_all
        low = gradient.astype(BF16)
        small["attn_out_bias", layer] = jnp.sum(low[: low.shape[0] // 2].astype(F32), axis=0)
        out_grad = cols_by_cols(mixture, low).astype(BF16)
        mixture_grad = rows_by_rows(low, attn_out[layer]).astype(BF16)
        query_grad, key_grad, value_grad = attend_backward(
            mixture_grad, queries, key_rows, value_rows, allowed, log_total
        )
        in_grad = jnp.concatenate(
            [
                cols_by_cols(hidden, query_grad).astype(BF16),
                cols_by_cols(keys_from, key_grad).astype(BF16),
                cols_by_cols(keys_from, value_grad).astype(BF16),
            ],
            axis=1,
        )
        small["attn_in_bias", layer] = jnp.concatenate(
            [jnp.sum(query_grad.astype(F32), axis=0), jnp.sum(value_grad.astype(F32), axis=0)]
        )
        query_part = rows_by_rows(query_grad, attn_in[layer, 0])
        key_part = rows_by_rows(key_grad, attn_in[layer, 1]) + rows_by_rows(
            value_grad, attn_in[layer, 2]
        )
        memory_grad = None
        if cross:
            memory_grad = pair_sum(key_part)
        else:
            query_part = query_part + key_part
        if last:
            total = own_sum(query_part)
            rows = total.shape[0]
            kept = (kept[0][:rows], kept[1][:rows])
            gradient = gradient[:rows]
            normed, inverse = kept
            small["gain", norm] = jnp.sum(total * normed, axis=0)
            small["offset", norm] = jnp.sum(total, axis=0)
            scaled = total * norm_gain[norm]
            mean_plain = jnp.mean(scaled, axis=-1, keepdims=True)
            mean_normed = jnp.mean(scaled * normed, axis=-1, keepdims=True)
            input_grad = inverse * (scaled - mean_plain - normed * mean_normed)
        else:
            input_grad, gain_grad, offset_grad = norm_backward(
                pair_sum(query_part), kept, norm_gain[norm]
            )
            small["gain", norm], small["offset", norm] = gain_grad, offset_grad
        return gradient + input_grad, memory_grad, in_grad, out_grad

    shards = {}
    gradient, in_grad, out_grad = feed_backward(dec_cotan, dec_feed, 4, 1)
    shards["ffn_out", 1] = scatter_sum(out_grad)
    shards["ffn_in", 1] = scatter_sum(in_grad)
    gradient, memory_grad, in_grad, out_grad = attention_backward(
        gradient, dec_cross, 3, 2, source_allowed, True, False
    )
    shards["attn_out", 2] = scatter_sum(out_grad)
    shards["attn_in", 2] = scatter_sum(in_grad)
    target_grad, unused, in_grad, out_grad = attention_backward(
        gradient, dec_attention, 2, 1, target_allowed, False, True
    )
    shards["attn_out", 1] = scatter_sum(out_grad)
    shards["attn_in", 1] = scatter_sum(in_grad)
    gradient, in_grad, out_grad = feed_backward(enc_cotan + memory_grad, enc_feed, 1, 0)
    shards["ffn_out", 0] = scatter_sum(out_grad)
    shards["ffn_in", 0] = scatter_sum(in_grad)
    source_grad, unused, in_grad, out_grad = attention_backward(
        gradient, enc_attention, 0, 0, source_allowed, False, True
    )
    shards["attn_out", 0] = scatter_sum(out_grad)
    shards["attn_in", 0] = scatter_sum(in_grad)

    stacks = {}
    counts = {"ffn_out": (2, 1), "ffn_in": (2, 1), "attn_out": (3, 1), "attn_in": (3, 3)}
    for (name, layer), shard in shards.items():
        layers, parts = counts[name]
        stacks[name] = gather_sum(
            shard,
            lambda bit, own, other: place(
                bit, own, other, stacks.get(name), layer, layers, parts
            ),
        )

    shared = jnp.stack(
        [small["gain", i] for i in range(5)]
        + [small["offset", i] for i in range(5)]
        + [small["attn_out_bias", i] for i in range(3)]
        + [small["ffn_out_bias", i] for i in range(2)]
    )
    apart = jnp.concatenate(
        [small["attn_in_bias", i] for i in range(3)] + [small["ffn_in_bias", i] for i in range(2)]
    ).reshape(-1, width)
    shared = shared + swap(shared)
    summed = total_small(jnp.concatenate([shared, apart], axis=0))
    shared, apart = summed[:15], summed[15:].reshape(-1)
    bias_rows = apart[: 6 * local].reshape(3, 2, local)
    hidden_rows = apart[6 * local :].reshape(2, -1)
    half = source_count // 2
    return (
        memory[:half][:, None],
        decoded.astype(BF16)[:, None],
        source_grad[:, None],
        target_grad[:, None],
        shared[0:5],
        shared[5:10],
        stacks["attn_in"].reshape(attn_in.shape),
        bias_rows,
        stacks["attn_out"].reshape(attn_out.shape),
        shared[10:13],
        stacks["ffn_in"].reshape(ffn_in.shape),
        hidden_rows,
        stacks["ffn_out"].reshape(ffn_out.shape),
        shared[13:15],
    )


def solution(mesh):
    return jax.shard_map(
        on_device,
        mesh=mesh,
        in_specs=(
            P("tensor", "dp", None),
            P("tensor", "dp", None),
            P("dp", None),
            P("dp", None),
            P("dp"),
            P("dp", "tensor"),
            P("tensor", "dp", None),
            P("tensor", "dp", None),
            P(),
            P(),
            P(None, None, None, "tensor"),
            P(None, None, "tensor"),
            P(None, "tensor", None),
            P(),
            P(None, None, "tensor"),
            P(None, "tensor"),
            P(None, "tensor", None),
            P(),
        ),
        out_specs=(
            P("tensor", "dp", None),
            P("tensor", "dp", None),
            P("tensor", "dp", None),
            P("tensor", "dp", None),
            P(),
            P(),
            P(None, None, None, "tensor"),
            P(None, None, "tensor"),
            P(None, "tensor", None),
            P(),
            P(None, None, "tensor"),
            P(None, "tensor"),
            P(None, "tensor", None),
            P(),
        ),
        check_vma=False,
    )
```

time: 1200 us -> 715 us (0.60)
  blocking collectives: 291 us -> 0 us
  waiting for transfers between devices: 511 us -> 235 us
  starting transfers between devices: 1.43 us -> 100 us
  Pallas kernels: 0 us -> 91.6 us
  matrix products: 165 us -> 86.2 us
  other arithmetic: 93.7 us -> 72.5 us
    psum x1 -> x0, waiting for transfers between devices: 452 us -> none  [on_device(): lax.psum((jnp.concatenate([enc_sharded[0], dec_sharded[0]], axis=0), jnp....]
    ppermute x0 -> x101, waiting for transfers between devices: none -> 235 us  [the longest x84 198 us: across(): return lax.ppermute(values, 'dp', [(i, i ^ stride) for i in range(count)])]
    all_gather x17 -> x0, blocking collectives: 189 us -> none  [the longest x12 137 us: spread_rows(): return lax.all_gather(values, 'tensor', axis=0, tiled=True)]
    psum x2 -> x0, blocking collectives: 102 us -> none  [the longest x1 61 us: on_device(): lax.psum((jnp.concatenate([enc_sharded[0], dec_sharded[0]], axis=0), jnp....]
    ppermute x0 -> x101, starting transfers between devices: none -> 100 us  [the longest x84 77.6 us: across(): return lax.ppermute(values, 'dp', [(i, i ^ stride) for i in range(count)])]
    pallas_call x0 -> x40, Pallas kernels: none -> 91.6 us  [the longest x30 55.6 us: join(): pl.pallas_call(join_body, out_shape=jax.ShapeDtypeStruct((2, rows, width)...]
    dot_general x61 -> x66, matrix products: 154 us -> 86.2 us  [the longest x48 66.3 us: dot(): lax.dot_general(left, right, (contract, ((), ())), preferred_element_type...]
    reduce_scatter x14 -> x0, waiting for transfers between devices: 58.8 us -> none  [the longest x8 49.8 us: collect_rows(): lax.psum_scatter(term(jnp.int32(0), lax.axis_size('tensor') * local_rows)...]
  transfers between devices with their start and end apart: 15 -> 101, of which waited for: 4 -> 42; matrix products, arithmetic and copies ran while one was open for 18% -> 34% of each run, Pallas kernels for 0% -> 12%
where the time goes in v1:
time: 715 us; the launch traced here: 702 us
  waiting for transfers between devices  235 us (33%)
  local copies, waits for them, and re-layouts  102 us (14%)
  starting transfers between devices  100 us (14%)
  Pallas kernels  91.6 us (13%)
  matrix products  86.2 us (12%)
  other arithmetic  72.5 us (10%)
  between operations  15.2 us (2%)
    ppermute x84, waiting for transfers between devices, across(): return lax.ppermute(values, 'dp', [(i, i ^ stride) for i in range(count)])  198 us
    ppermute x84, starting transfers between devices, across(): return lax.ppermute(values, 'dp', [(i, i ^ stride) for i in range(count)])  77.6 us
    dot_general x48, matrix products, dot(): lax.dot_general(left, right, (contract, ((), ())), preferred_element_type...  66.3 us
    pallas_call x30, Pallas kernels, join(): pl.pallas_call(join_body, out_shape=jax.ShapeDtypeStruct((2, rows, width)...  55.6 us
    ppermute x17, waiting for transfers between devices, swap(): return lax.ppermute(values, 'tensor', [(0, 1), (1, 0)])  36.4 us
    pallas_call x10, Pallas kernels, place(): pl.pallas_call(functools.partial(place_body, parts), grid=(rows // block,...  36 us
    squeeze x40, local copies, waits for them, and re-layouts, scatter_sum(): send = lax.dynamic_index_in_dim(halves, 1 - bit, 0, keepdims=False)  27.5 us
    convert_element_type x40, other arithmetic, scatter_sum(): current = current.astype(BF16)  26.9 us
  transfers between devices with their start and end apart: 101, of which 42 were waited for; matrix products, arithmetic and copies ran while one was open for 34% of the time, Pallas kernels for 12%

profile of v1, /device:TPU:0, one launch (start us, length us, event | category | flops | bytes accessed | tf_op | source)
XLA Modules:
  0.0 701.9 jit_solution(16679661891416344721)
XLA Ops:
  0.6 3.0 collective-permute-start
  49.9 14.0 %collective-permute-done.1 = bf16[512,768]{1,0:T(8,128)(2,1)S(1)} collective-permute-done((bf16[512,768]{1,0:T(8,128)(2,1)S(1)}, bf16[512,768]{1,0:T(8,128)(2,1)S(1)}, u32[]{:S(2)}, u32[]{:S(2)}) %collective-permute-start.1) | collective-permute-done | bytes 786464 | tf_op jit(solution)/shard_map/ppermute | solution.py:34
  79.3 2.9 fusion.206
  86.8 12.6 %collective-permute-done.2 = bf16[512,768]{1,0:T(8,128)(2,1)} collective-permute-done((bf16[512,768]{1,0:T(8,128)(2,1)}, bf16[512,768]{1,0:T(8,128)(2,1)}, u32[]{:S(2)}, u32[]{:S(2)}) %collective-permute-start.2) | collective-permute-done | bytes 786464 | tf_op jit(solution)/shard_map/ppermute | solution.py:34
  110.6 5.7 collective-permute-done.5
  128.7 4.1 collective-permute-done.10
  156.2 3.9 copy.98
  196.7 4.1 copy.97
  238.4 5.1 convert_reduce_fusion
  243.5 2.8 fusion.213
  263.4 4.6 collective-permute-done.56
  285.0 6.3 collective-permute-done.59.other_ref
  297.7 8.2 %collective-permute-done.38 = bf16[192,1152]{1,0:T(8,128)(2,1)S(1)} collective-permute-done((bf16[192,1152]{1,0:T(8,128)(2,1)}, bf16[192,1152]{1,0:T(8,128)(2,1)S(1)}, u32[]{:S(2)}, u32[]{:S(2)}) %collective-permute-start.38) | collective-permute-done | bytes 442400 | tf_op jit(solution)/shard_map/ppermute | solution.py:131
  309.3 12.8 %collective-permute-done.94 = bf16[384,768]{1,0:T(8,128)(2,1)S(1)} collective-permute-done((bf16[384,768]{1,0:T(8,128)(2,1)S(1)}, bf16[384,768]{1,0:T(8,128)(2,1)S(1)}, u32[]{:S(2)}, u32[]{:S(2)}) %collective-permute-start.94) | collective-permute-done | bytes 589856 | tf_op jit(solution)/shard_map/ppermute | solution.py:131
  326.0 5.1 collective-permute-done.39
  332.6 3.8 collective-permute-start.40
  338.7 2.9 fusion.189
  363.3 4.0 copy.96
  373.9 5.1 collective-permute-done.95
  380.5 2.9 collective-permute-start.80
  390.8 6.5 collective-permute-done.96
  401.8 5.3 collective-permute-done.31
  411.4 3.8 collective-permute-done.97.other_ref
  431.3 5.3 collective-permute-done.32
  442.4 3.1 collective-permute-start.48
  447.5 2.9 collective-permute-start.33
  450.4 4.6 collective-permute-done.33.other_ref
  459.9 11.1 %collective-permute-done.70 = bf16[192,1536]{1,0:T(8,128)(2,1)S(1)} collective-permute-done((bf16[192,1536]{1,0:T(8,128)(2,1)}, bf16[192,1536]{1,0:T(8,128)(2,1)S(1)}, u32[]{:S(2)}, u32[]{:S(2)}) %collective-permute-start.70) | collective-permute-done | bytes 589856 | tf_op jit(solution)/shard_map/ppermute | solution.py:131
  472.1 11.0 %collective-permute-done.86 = bf16[384,768]{1,0:T(8,128)(2,1)S(1)} collective-permute-done((bf16[384,768]{1,0:T(8,128)(2,1)S(1)}, bf16[384,768]{1,0:T(8,128)(2,1)S(1)}, u32[]{:S(2)}, u32[]{:S(2)}) %collective-permute-start.86) | collective-permute-done | bytes 589856 | tf_op jit(solution)/shard_map/ppermute | solution.py:131
  484.5 8.0 %collective-permute-done.71 = bf16[96,1536]{1,0:T(8,128)(2,1)S(1)} collective-permute-done((bf16[96,1536]{1,0:T(8,128)(2,1)S(1)}, bf16[96,1536]{1,0:T(8,128)(2,1)S(1)}, u32[]{:S(2)}, u32[]{:S(2)}) %collective-permute-start.71) | collective-permute-done | bytes 294944 | tf_op jit(solution)/shard_map/ppermute | solution.py:131
  494.0 5.3 collective-permute-done.87
  500.3 7.2 %collective-permute-done.22 = bf16[192,1152]{1,0:T(8,128)(2,1)S(1)} collective-permute-done((bf16[192,1152]{1,0:T(8,128)(2,1)S(1)}, bf16[192,1152]{1,0:T(8,128)(2,1)S(1)}, u32[]{:S(2)}, u32[]{:S(2)}) %collective-permute-start.22) | collective-permute-done | bytes 442400 | tf_op jit(solution)/shard_map/ppermute | solution.py:131
  508.8 6.6 collective-permute-done.72
  515.5 7.8 %collective-permute-done.88 = bf16[96,768]{1,0:T(8,128)(2,1)S(1)} collective-permute-done((bf16[96,768]{1,0:T(8,128)(2,1)S(1)}, bf16[96,768]{1,0:T(8,128)(2,1)S(1)}, u32[]{:S(2)}, u32[]{:S(2)}) %collective-permute-start.88) | collective-permute-done | bytes 147488 | tf_op jit(solution)/shard_map/ppermute | solution.py:131
  524.4 4.9 collective-permute-done.23
  534.5 2.7 collective-permute-start.89
  537.8 12.7 %collective-permute-done.34.other_ref = bf16[96,1152]{1,0:T(8,128)(2,1)S(1)} collective-permute-done((bf16[96,1152]{1,0:T(8,128)(2,1)S(1)}, bf16[96,1152]{1,0:T(8,128)(2,1)S(1)}, u32[]{:S(2)}, u32[]{:S(2)}) %collective-permute-start.34) | collective-permute-done | bytes 221216 | tf_op jit(solution)/shard_map/ppermute | solution.py:131
  571.3 7.8 %collective-permute-done.74.other_ref = bf16[96,1536]{1,0:T(8,128)(2,1)} collective-permute-done((bf16[96,1536]{1,0:T(8,128)(2,1)}, bf16[96,1536]{1,0:T(8,128)(2,1)}, u32[]{:S(2)}, u32[]{:S(2)}) %collective-permute-start.74) | collective-permute-done | bytes 294944 | tf_op jit(solution)/shard_map/ppermute | solution.py:131
  595.2 7.9 %collective-permute-done.51.other_ref = bf16[96,768]{1,0:T(8,128)(2,1)S(1)} collective-permute-done((bf16[96,768]{1,0:T(8,128)(2,1)S(1)}, bf16[96,768]{1,0:T(8,128)(2,1)S(1)}, u32[]{:S(2)}, u32[]{:S(2)}) %collective-permute-start.51) | collective-permute-done | bytes 147488 | tf_op jit(solution)/shard_map/ppermute | solution.py:131
  615.9 12.6 %collective-permute-done.75.other_ref = bf16[192,1536]{1,0:T(8,128)(2,1)} collective-permute-done((bf16[192,1536]{1,0:T(8,128)(2,1)}, bf16[192,1536]{1,0:T(8,128)(2,1)}, u32[]{:S(2)}, u32[]{:S(2)}) %collective-permute-start.75) | collective-permute-done | bytes 589856 | tf_op jit(solution)/shard_map/ppermute | solution.py:131
  631.0 10.2 %collective-permute-done.91.other_ref = bf16[384,768]{1,0:T(8,128)(2,1)} collective-permute-done((bf16[384,768]{1,0:T(8,128)(2,1)}, bf16[384,768]{1,0:T(8,128)(2,1)}, u32[]{:S(2)}, u32[]{:S(2)}) %collective-permute-start.91) | collective-permute-done | bytes 589856 | tf_op jit(solution)/shard_map/ppermute | solution.py:131
  672.1 4.1 shard_map.290.refs_0_
  676.2 4.1 shard_map.291.refs_0_
  680.3 4.3 shard_map.311.refs_0_
  684.6 4.3 shard_map.319.refs_0_
  688.9 4.1 shard_map.292
  693.0 4.3 shard_map.312
  697.3 4.3 shard_map.320
  (954 shorter events, 396.2 us)
Async XLA Ops:
  0.6 31.6 %collective-permute-start = (bf16[256,768]{1,0:T(8,128)(2,1)}, bf16[256,768]{1,0:T(8,128)(2,1)S(1)}, u32[]{:S(2)}, u32[]{:S(2)}) collective-permute-start(bf16[256,768]{1,0:T(8,128)(2,1)} %bitcast.546), channel_id=1, source_target_pairs={{0,1},{1,0},{2,3},{3,2},{4,5},{5,4},{6,7},{7,6},{8,9},{9,8},{10,11... | collective-permute-start | bytes 1179656 | tf_op jit(solution)/shard_map/ppermute | solution.py:34
  6.4 25.7 %collective-permute-start.8 = (bf16[128,768]{1,0:T(8,128)(2,1)}, bf16[128,768]{1,0:T(8,128)(2,1)S(1)}, u32[]{:S(2)}, u32[]{:S(2)}) collective-permute-start(bf16[128,768]{1,0:T(8,128)(2,1)} %bitcast.702), channel_id=1, source_target_pairs={{0,1},{1,0},{2,3},{3,2},{4,5},{5,4},{6,7},{7,6},{8,9},{9,8},{10,11... | collective-permute-start | bytes 589832 | tf_op jit(solution)/shard_map/ppermute | solution.py:34
  6.4 229.7 %collective-permute-start.7 = (bf16[256,768]{1,0:T(8,128)(2,1)}, bf16[256,768]{1,0:T(8,128)(2,1)}, u32[]{:S(2)}, u32[]{:S(2)}) collective-permute-start(bf16[256,768]{1,0:T(8,128)(2,1)} %bitcast.649), channel_id=1, source_target_pairs={{0,1},{1,0},{2,3},{3,2},{4,5},{5,4},{6,7},{7,6},{8,9},{9,8},{10,11... | collective-permute-start | bytes 1179656 | tf_op jit(solution)/shard_map/ppermute | solution.py:34
  153.5 20.0 %collective-permute-start.14 = (bf16[256,768]{1,0:T(8,128)(2,1)}, bf16[256,768]{1,0:T(8,128)(2,1)}, u32[]{:S(2)}, u32[]{:S(2)}) collective-permute-start(bf16[256,768]{1,0:T(8,128)(2,1)} %get-tuple-element.149), channel_id=1, source_target_pairs={{0,1},{1,0},{2,3},{3,2},{4,5},{5,4},{6,7},{7,6},{8,9},{9,8},{10,11... | collective-permute-start | bytes 1179656 | tf_op jit(solution)/shard_map/ppermute | solution.py:34
  163.7 70.5 %collective-permute-start.11 = (bf16[512,768]{1,0:T(8,128)(2,1)}, bf16[512,768]{1,0:T(8,128)(2,1)}, u32[]{:S(2)}, u32[]{:S(2)}) collective-permute-start(bf16[512,768]{1,0:T(8,128)(2,1)} %get-tuple-element.143), channel_id=1, source_target_pairs={{0,1},{1,0},{2,3},{3,2},{4,5},{5,4},{6,7},{7,6},{8,9},{9,8},{10,11... | collective-permute-start | bytes 2359304 | tf_op jit(solution)/shard_map/ppermute | solution.py:34
  172.0 31.5 %collective-permute-start.62 = (bf16[96,768]{1,0:T(8,128)(2,1)}, bf16[96,768]{1,0:T(8,128)(2,1)}, u32[]{:S(2)}, u32[]{:S(2)}) collective-permute-start(bf16[96,768]{1,0:T(8,128)(2,1)} %dynamic-slice_bitcast_fusion.28), channel_id=1, source_target_pairs={{0,4},{2,6},{4,0},{6,2},{8,12},{10,14},{12,8},{14,10},{16,20},{18,... | collective-permute-start | bytes 442376 | tf_op jit(solution)/shard_map/ppermute | solution.py:131
  192.5 33.4 %collective-permute-start.15 = (bf16[128,768]{1,0:T(8,128)(2,1)}, bf16[128,768]{1,0:T(8,128)(2,1)}, u32[]{:S(2)}, u32[]{:S(2)}) collective-permute-start(bf16[128,768]{1,0:T(8,128)(2,1)} %slice.650), channel_id=1, source_target_pairs={{0,1},{1,0},{2,3},{3,2},{4,5},{5,4},{6,7},{7,6},{8,9},{9,8},{10,11... | collective-permute-start | bytes 589832 | tf_op jit(solution)/shard_map/ppermute | solution.py:34
  212.5 20.5 %collective-permute-start.53 = (bf16[192,768]{1,0:T(8,128)(2,1)}, bf16[192,768]{1,0:T(8,128)(2,1)}, u32[]{:S(2)}, u32[]{:S(2)}) collective-permute-start(bf16[192,768]{1,0:T(8,128)(2,1)} %dynamic-slice_bitcast_fusion.19), channel_id=1, source_target_pairs={{0,2},{2,0},{4,6},{6,4},{8,10},{10,8},{12,14},{14,12},{16,18},{18,... | collective-permute-start | bytes 884744 | tf_op jit(solution)/shard_map/ppermute | solution.py:131
  224.4 27.7 %collective-permute-start.77 = (bf16[384,1536]{1,0:T(8,128)(2,1)}, bf16[384,1536]{1,0:T(8,128)(2,1)}, u32[]{:S(2)}, u32[]{:S(2)}) collective-permute-start(bf16[384,1536]{1,0:T(8,128)(2,1)} %dynamic-slice_bitcast_fusion.2), channel_id=1, source_target_pairs={{0,2},{2,0},{4,6},{6,4},{8,10},{10,8},{12,14},{14,12},{16,18},{18,... | collective-permute-start | bytes 3538952 | tf_op jit(solution)/shard_map/ppermute | solution.py:131
  230.8 24.4 %collective-permute-start.93 = (bf16[768,768]{1,0:T(8,128)(2,1)}, bf16[768,768]{1,0:T(8,128)(2,1)}, u32[]{:S(2)}, u32[]{:S(2)}) collective-permute-start(bf16[768,768]{1,0:T(8,128)(2,1)} %dynamic-slice_bitcast_fusion), channel_id=1, source_target_pairs={{0,2},{2,0},{4,6},{6,4},{8,10},{10,8},{12,14},{14,12},{16,18},{18,... | collective-permute-start | bytes 3538952 | tf_op jit(solution)/shard_map/ppermute | solution.py:131
  233.1 42.6 %collective-permute-start.37 = (bf16[384,1152]{1,0:T(8,128)(2,1)}, bf16[384,1152]{1,0:T(8,128)(2,1)}, u32[]{:S(2)}, u32[]{:S(2)}) collective-permute-start(bf16[384,1152]{1,0:T(8,128)(2,1)} %dynamic-slice_bitcast_fusion.4), channel_id=1, source_target_pairs={{0,2},{2,0},{4,6},{6,4},{8,10},{10,8},{12,14},{14,12},{16,18},{18,... | collective-permute-start | bytes 2654216 | tf_op jit(solution)/shard_map/ppermute | solution.py:131
  234.3 59.3 %collective-permute-start.29 = (bf16[384,1152]{1,0:T(8,128)(2,1)}, bf16[384,1152]{1,0:T(8,128)(2,1)}, u32[]{:S(2)}, u32[]{:S(2)}) collective-permute-start(bf16[384,1152]{1,0:T(8,128)(2,1)} %dynamic-slice_bitcast_fusion.5), channel_id=1, source_target_pairs={{0,2},{2,0},{4,6},{6,4},{8,10},{10,8},{12,14},{14,12},{16,18},{18,... | collective-permute-start | bytes 2654216 | tf_op jit(solution)/shard_map/ppermute | solution.py:131
  236.2 33.6 %collective-permute-start.67 = (bf16[96,768]{1,0:T(8,128)(2,1)S(1)}, bf16[96,768]{1,0:T(8,128)(2,1)S(1)}, u32[]{:S(2)}, u32[]{:S(2)}) collective-permute-start(bf16[96,768]{1,0:T(8,128)(2,1)S(1)} %bitcast.718), channel_id=1, source_target_pairs={{0,4},{2,6},{4,0},{6,2},{8,12},{10,14},{12,8},{14,10},{16,20},{18,... | collective-permute-start | bytes 442376 | tf_op jit(solution)/shard_map/ppermute | solution.py:131
  255.3 77.4 %collective-permute-start.12 = (bf16[512,768]{1,0:T(8,128)(2,1)}, bf16[512,768]{1,0:T(8,128)(2,1)}, u32[]{:S(2)}, u32[]{:S(2)}) collective-permute-start(bf16[512,768]{1,0:T(8,128)(2,1)} %get-tuple-element.145), channel_id=1, source_target_pairs={{0,1},{1,0},{2,3},{3,2},{4,5},{5,4},{6,7},{7,6},{8,9},{9,8},{10,11... | collective-permute-start | bytes 2359304 | tf_op jit(solution)/shard_map/ppermute | solution.py:34
  270.4 149.6 %collective-permute-start.69 = (bf16[384,1536]{1,0:T(8,128)(2,1)}, bf16[384,1536]{1,0:T(8,128)(2,1)}, u32[]{:S(2)}, u32[]{:S(2)}) collective-permute-start(bf16[384,1536]{1,0:T(8,128)(2,1)} %dynamic-slice_bitcast_fusion.3), channel_id=1, source_target_pairs={{0,2},{2,0},{4,6},{6,4},{8,10},{10,8},{12,14},{14,12},{16,18},{18,... | collective-permute-start | bytes 3538952 | tf_op jit(solution)/shard_map/ppermute | solution.py:131
  272.9 34.5 %collective-permute-start.78 = (bf16[192,1536]{1,0:T(8,128)(2,1)}, bf16[192,1536]{1,0:T(8,128)(2,1)}, u32[]{:S(2)}, u32[]{:S(2)}) collective-permute-start(bf16[192,1536]{1,0:T(8,128)(2,1)} %dynamic-slice_bitcast_fusion.9), channel_id=1, source_target_pairs={{0,4},{2,6},{4,0},{6,2},{8,12},{10,14},{12,8},{14,10},{16,20},{18,... | collective-permute-start | bytes 1769480 | tf_op jit(solution)/shard_map/ppermute | solution.py:131
  291.3 133.0 %collective-permute-start.85 = (bf16[768,768]{1,0:T(8,128)(2,1)}, bf16[768,768]{1,0:T(8,128)(2,1)}, u32[]{:S(2)}, u32[]{:S(2)}) collective-permute-start(bf16[768,768]{1,0:T(8,128)(2,1)} %dynamic-slice_bitcast_fusion.1), channel_id=1, source_target_pairs={{0,2},{2,0},{4,6},{6,4},{8,10},{10,8},{12,14},{14,12},{16,18},{18,... | collective-permute-start | bytes 3538952 | tf_op jit(solution)/shard_map/ppermute | solution.py:131
  307.4 73.1 %collective-permute-start.30 = (bf16[192,1152]{1,0:T(8,128)(2,1)}, bf16[192,1152]{1,0:T(8,128)(2,1)}, u32[]{:S(2)}, u32[]{:S(2)}) collective-permute-start(bf16[192,1152]{1,0:T(8,128)(2,1)} %dynamic-slice_bitcast_fusion.12), channel_id=1, source_target_pairs={{0,4},{2,6},{4,0},{6,2},{8,12},{10,14},{12,8},{14,10},{16,20},{18,... | collective-permute-start | bytes 1327112 | tf_op jit(solution)/shard_map/ppermute | solution.py:131
  331.1 40.3 %collective-permute-start.79 = (bf16[96,1536]{1,0:T(8,128)(2,1)}, bf16[96,1536]{1,0:T(8,128)(2,1)}, u32[]{:S(2)}, u32[]{:S(2)}) collective-permute-start(bf16[96,1536]{1,0:T(8,128)(2,1)} %dynamic-slice_bitcast_fusion.16), channel_id=1, source_target_pairs={{0,8},{2,10},{4,12},{6,14},{8,0},{10,2},{12,4},{14,6},{16,24},{18,... | collective-permute-start | bytes 884744 | tf_op jit(solution)/shard_map/ppermute | solution.py:131
  332.6 37.8 %collective-permute-start.40 = (bf16[48,1152]{1,0:T(8,128)(2,1)}, bf16[48,1152]{1,0:T(8,128)(2,1)}, u32[]{:S(2)}, u32[]{:S(2)}) collective-permute-start(bf16[48,1152]{1,0:T(8,128)(2,1)} %dynamic-slice_bitcast_fusion.31), channel_id=1, source_target_pairs={{0,16},{2,18},{4,20},{6,22},{8,24},{10,26},{12,28},{14,30},{16,0},... | collective-permute-start | bytes 331784 | tf_op jit(solution)/shard_map/ppermute | solution.py:131
  371.4 46.2 %collective-permute-start.13 = (bf16[256,768]{1,0:T(8,128)(2,1)}, bf16[256,768]{1,0:T(8,128)(2,1)S(1)}, u32[]{:S(2)}, u32[]{:S(2)}) collective-permute-start(bf16[256,768]{1,0:T(8,128)(2,1)} %slice.649), channel_id=1, source_target_pairs={{0,1},{1,0},{2,3},{3,2},{4,5},{5,4},{6,7},{7,6},{8,9},{9,8},{10,11... | collective-permute-start | bytes 1179656 | tf_op jit(solution)/shard_map/ppermute | solution.py:34
  408.3 115.1 %collective-permute-start.6 = (bf16[128,768]{1,0:T(8,128)(2,1)}, bf16[128,768]{1,0:T(8,128)(2,1)}, u32[]{:S(2)}, u32[]{:S(2)}) collective-permute-start(bf16[128,768]{1,0:T(8,128)(2,1)} %slice.651), channel_id=1, source_target_pairs={{0,1},{1,0},{2,3},{3,2},{4,5},{5,4},{6,7},{7,6},{8,9},{9,8},{10,11... | collective-permute-start | bytes 589832 | tf_op jit(solution)/shard_map/ppermute | solution.py:34
  415.2 114.2 %collective-permute-start.68 = (bf16[192,768]{1,0:T(8,128)(2,1)}, bf16[192,768]{1,0:T(8,128)(2,1)}, u32[]{:S(2)}, u32[]{:S(2)}) collective-permute-start(bf16[192,768]{1,0:T(8,128)(2,1)} %bitcast.170.own_ref), channel_id=1, source_target_pairs={{0,2},{2,0},{4,6},{6,4},{8,10},{10,8},{12,14},{14,12},{16,18},{18,... | collective-permute-start | bytes 884744 | tf_op jit(solution)/shard_map/ppermute | solution.py:131
  417.6 39.8 %collective-permute-start.21 = (bf16[384,1152]{1,0:T(8,128)(2,1)}, bf16[384,1152]{1,0:T(8,128)(2,1)}, u32[]{:S(2)}, u32[]{:S(2)}) collective-permute-start(bf16[384,1152]{1,0:T(8,128)(2,1)} %dynamic-slice_bitcast_fusion.6), channel_id=1, source_target_pairs={{0,2},{2,0},{4,6},{6,4},{8,10},{10,8},{12,14},{14,12},{16,18},{18,... | collective-permute-start | bytes 2654216 | tf_op jit(solution)/shard_map/ppermute | solution.py:131
  429.2 100.2 %collective-permute-start.42 = (bf16[96,1152]{1,0:T(8,128)(2,1)S(1)}, bf16[96,1152]{1,0:T(8,128)(2,1)}, u32[]{:S(2)}, u32[]{:S(2)}) collective-permute-start(bf16[96,1152]{1,0:T(8,128)(2,1)S(1)} %bitcast.685), channel_id=1, source_target_pairs={{0,8},{2,10},{4,12},{6,14},{8,0},{10,2},{12,4},{14,6},{16,24},{18,... | collective-permute-start | bytes 663560 | tf_op jit(solution)/shard_map/ppermute | solution.py:131
  455.0 79.5 %collective-permute-start.82 = (bf16[96,1536]{1,0:T(8,128)(2,1)S(1)}, bf16[96,1536]{1,0:T(8,128)(2,1)}, u32[]{:S(2)}, u32[]{:S(2)}) collective-permute-start(bf16[96,1536]{1,0:T(8,128)(2,1)S(1)} %bitcast.679), channel_id=1, source_target_pairs={{0,8},{2,10},{4,12},{6,14},{8,0},{10,2},{12,4},{14,6},{16,24},{18,... | collective-permute-start | bytes 884744 | tf_op jit(solution)/shard_map/ppermute | solution.py:131
  529.4 35.3 %collective-permute-start.60 = (bf16[192,768]{1,0:T(8,128)(2,1)}, bf16[192,768]{1,0:T(8,128)(2,1)}, u32[]{:S(2)}, u32[]{:S(2)}) collective-permute-start(bf16[192,768]{1,0:T(8,128)(2,1)} %bitcast.154.own_ref), channel_id=1, source_target_pairs={{0,2},{2,0},{4,6},{6,4},{8,10},{10,8},{12,14},{14,12},{16,18},{18,... | collective-permute-start | bytes 884744 | tf_op jit(solution)/shard_map/ppermute | solution.py:131
  529.4 38.2 %collective-permute-start.98 = (bf16[192,768]{1,0:T(8,128)(2,1)}, bf16[192,768]{1,0:T(8,128)(2,1)}, u32[]{:S(2)}, u32[]{:S(2)}) collective-permute-start(bf16[192,768]{1,0:T(8,128)(2,1)} %bitcast.230.own_ref), channel_id=1, source_target_pairs={{0,8},{2,10},{4,12},{6,14},{8,0},{10,2},{12,4},{14,6},{16,24},{18,... | collective-permute-start | bytes 884744 | tf_op jit(solution)/shard_map/ppermute | solution.py:131
  530.7 19.8 %collective-permute-start.34 = (bf16[96,1152]{1,0:T(8,128)(2,1)S(1)}, bf16[96,1152]{1,0:T(8,128)(2,1)S(1)}, u32[]{:S(2)}, u32[]{:S(2)}) collective-permute-start(bf16[96,1152]{1,0:T(8,128)(2,1)S(1)} %bitcast.687), channel_id=1, source_target_pairs={{0,8},{2,10},{4,12},{6,14},{8,0},{10,2},{12,4},{14,6},{16,24},{18,... | collective-permute-start | bytes 663560 | tf_op jit(solution)/shard_map/ppermute | solution.py:131
  534.2 18.0 %collective-permute-start.73 = (bf16[48,1536]{1,0:T(8,128)(2,1)S(1)}, bf16[48,1536]{1,0:T(8,128)(2,1)S(1)}, u32[]{:S(2)}, u32[]{:S(2)}) collective-permute-start(bf16[48,1536]{1,0:T(8,128)(2,1)S(1)} %fusion.168.own_ref), channel_id=1, source_target_pairs={{0,16},{2,18},{4,20},{6,22},{8,24},{10,26},{12,28},{14,30},{16,0},... | collective-permute-start | bytes 442376 | tf_op jit(solution)/shard_map/ppermute | solution.py:131
  534.5 20.9 %collective-permute-start.89 = (bf16[96,768]{1,0:T(8,128)(2,1)S(1)}, bf16[96,768]{1,0:T(8,128)(2,1)S(1)}, u32[]{:S(2)}, u32[]{:S(2)}) collective-permute-start(bf16[96,768]{1,0:T(8,128)(2,1)S(1)} %fusion.166.own_ref), channel_id=1, source_target_pairs={{0,16},{2,18},{4,20},{6,22},{8,24},{10,26},{12,28},{14,30},{16,0},... | collective-permute-start | bytes 442376 | tf_op jit(solution)/shard_map/ppermute | solution.py:131
  550.5 19.1 %collective-permute-start.24 = (bf16[48,1152]{1,0:T(8,128)(2,1)}, bf16[48,1152]{1,0:T(8,128)(2,1)}, u32[]{:S(2)}, u32[]{:S(2)}) collective-permute-start(bf16[48,1152]{1,0:T(8,128)(2,1)} %dynamic-slice_bitcast_fusion.33), channel_id=1, source_target_pairs={{0,16},{2,18},{4,20},{6,22},{8,24},{10,26},{12,28},{14,30},{16,0},... | collective-permute-start | bytes 331784 | tf_op jit(solution)/shard_map/ppermute | solution.py:131
  564.7 20.8 %collective-permute-start.43 = (bf16[192,1152]{1,0:T(8,128)(2,1)S(1)}, bf16[192,1152]{1,0:T(8,128)(2,1)}, u32[]{:S(2)}, u32[]{:S(2)}) collective-permute-start(bf16[192,1152]{1,0:T(8,128)(2,1)S(1)} %bitcast.638), channel_id=1, source_target_pairs={{0,4},{2,6},{4,0},{6,2},{8,12},{10,14},{12,8},{14,10},{16,20},{18,... | collective-permute-start | bytes 1327112 | tf_op jit(solution)/shard_map/ppermute | solution.py:131
  565.6 39.5 %collective-permute-start.83 = (bf16[192,1536]{1,0:T(8,128)(2,1)S(1)}, bf16[192,1536]{1,0:T(8,128)(2,1)}, u32[]{:S(2)}, u32[]{:S(2)}) collective-permute-start(bf16[192,1536]{1,0:T(8,128)(2,1)S(1)} %bitcast.588), channel_id=1, source_target_pairs={{0,4},{2,6},{4,0},{6,2},{8,12},{10,14},{12,8},{14,10},{16,20},{18,... | collective-permute-start | bytes 1769480 | tf_op jit(solution)/shard_map/ppermute | solution.py:131
  566.8 36.4 %collective-permute-start.35 = (bf16[192,1152]{1,0:T(8,128)(2,1)}, bf16[192,1152]{1,0:T(8,128)(2,1)}, u32[]{:S(2)}, u32[]{:S(2)}) collective-permute-start(bf16[192,1152]{1,0:T(8,128)(2,1)} %bitcast.635), channel_id=1, source_target_pairs={{0,4},{2,6},{4,0},{6,2},{8,12},{10,14},{12,8},{14,10},{16,20},{18,... | collective-permute-start | bytes 1327112 | tf_op jit(solution)/shard_map/ppermute | solution.py:131
  586.6 29.2 %collective-permute-start.99 = (bf16[384,768]{1,0:T(8,128)(2,1)}, bf16[384,768]{1,0:T(8,128)(2,1)}, u32[]{:S(2)}, u32[]{:S(2)}) collective-permute-start(bf16[384,768]{1,0:T(8,128)(2,1)} %bitcast.591), channel_id=1, source_target_pairs={{0,4},{2,6},{4,0},{6,2},{8,12},{10,14},{12,8},{14,10},{16,20},{18,... | collective-permute-start | bytes 1769480 | tf_op jit(solution)/shard_map/ppermute | solution.py:131
  587.5 41.0 %collective-permute-start.75 = (bf16[192,1536]{1,0:T(8,128)(2,1)}, bf16[192,1536]{1,0:T(8,128)(2,1)}, u32[]{:S(2)}, u32[]{:S(2)}) collective-permute-start(bf16[192,1536]{1,0:T(8,128)(2,1)} %bitcast.593), channel_id=1, source_target_pairs={{0,4},{2,6},{4,0},{6,2},{8,12},{10,14},{12,8},{14,10},{16,20},{18,... | collective-permute-start | bytes 1769480 | tf_op jit(solution)/shard_map/ppermute | solution.py:131
  603.1 56.8 %collective-permute-start.44 = (bf16[384,1152]{1,0:T(8,128)(2,1)}, bf16[384,1152]{1,0:T(8,128)(2,1)}, u32[]{:S(2)}, u32[]{:S(2)}) collective-permute-start(bf16[384,1152]{1,0:T(8,128)(2,1)} %bitcast.121.own_ref), channel_id=1, source_target_pairs={{0,2},{2,0},{4,6},{6,4},{8,10},{10,8},{12,14},{14,12},{16,18},{18,... | collective-permute-start | bytes 2654216 | tf_op jit(solution)/shard_map/ppermute | solution.py:131
  605.1 36.0 %collective-permute-start.91 = (bf16[384,768]{1,0:T(8,128)(2,1)}, bf16[384,768]{1,0:T(8,128)(2,1)}, u32[]{:S(2)}, u32[]{:S(2)}) collective-permute-start(bf16[384,768]{1,0:T(8,128)(2,1)} %bitcast.595), channel_id=1, source_target_pairs={{0,4},{2,6},{4,0},{6,2},{8,12},{10,14},{12,8},{14,10},{16,20},{18,... | collective-permute-start | bytes 1769480 | tf_op jit(solution)/shard_map/ppermute | solution.py:131
  611.4 51.2 %collective-permute-start.36 = (bf16[384,1152]{1,0:T(8,128)(2,1)}, bf16[384,1152]{1,0:T(8,128)(2,1)}, u32[]{:S(2)}, u32[]{:S(2)}) collective-permute-start(bf16[384,1152]{1,0:T(8,128)(2,1)} %bitcast.583), channel_id=1, source_target_pairs={{0,2},{2,0},{4,6},{6,4},{8,10},{10,8},{12,14},{14,12},{16,18},{18,... | collective-permute-start | bytes 2654216 | tf_op jit(solution)/shard_map/ppermute | solution.py:131
  615.9 43.5 %collective-permute-start.52 = (bf16[192,768]{1,0:T(8,128)(2,1)}, bf16[192,768]{1,0:T(8,128)(2,1)}, u32[]{:S(2)}, u32[]{:S(2)}) collective-permute-start(bf16[192,768]{1,0:T(8,128)(2,1)} %bitcast.662), channel_id=1, source_target_pairs={{0,2},{2,0},{4,6},{6,4},{8,10},{10,8},{12,14},{14,12},{16,18},{18,... | collective-permute-start | bytes 884744 | tf_op jit(solution)/shard_map/ppermute | solution.py:131
  628.5 31.5 %collective-permute-start.27 = (bf16[192,1152]{1,0:T(8,128)(2,1)}, bf16[192,1152]{1,0:T(8,128)(2,1)}, u32[]{:S(2)}, u32[]{:S(2)}) collective-permute-start(bf16[192,1152]{1,0:T(8,128)(2,1)} %bitcast.639), channel_id=1, source_target_pairs={{0,4},{2,6},{4,0},{6,2},{8,12},{10,14},{12,8},{14,10},{16,20},{18,... | collective-permute-start | bytes 1327112 | tf_op jit(solution)/shard_map/ppermute | solution.py:131
  641.1 18.2 %collective-permute-start.20 = (f32[22,768]{1,0:T(8,128)}, f32[22,768]{1,0:T(8,128)}, u32[]{:S(2)}, u32[]{:S(2)}) collective-permute-start(f32[22,768]{1,0:T(8,128)} %add.749), channel_id=1, source_target_pairs={{0,16},{2,18},{4,20},{6,22},{8,24},{10,26},{12,28},{14,30},{16,0},... | collective-permute-start | bytes 202760 | tf_op jit(solution)/shard_map/ppermute | solution.py:131
  659.4 20.9 %collective-permute-start.84 = (bf16[384,1536]{1,0:T(8,128)(2,1)}, bf16[384,1536]{1,0:T(8,128)(2,1)}, u32[]{:S(2)}, u32[]{:S(2)}) collective-permute-start(bf16[384,1536]{1,0:T(8,128)(2,1)} %bitcast.557), channel_id=1, source_target_pairs={{0,2},{2,0},{4,6},{6,4},{8,10},{10,8},{12,14},{14,12},{16,18},{18,... | collective-permute-start | bytes 3538952 | tf_op jit(solution)/shard_map/ppermute | solution.py:131
  659.4 25.2 %collective-permute-start.100 = (bf16[768,768]{1,0:T(8,128)(2,1)}, bf16[768,768]{1,0:T(8,128)(2,1)}, u32[]{:S(2)}, u32[]{:S(2)}) collective-permute-start(bf16[768,768]{1,0:T(8,128)(2,1)} %bitcast.555), channel_id=1, source_target_pairs={{0,2},{2,0},{4,6},{6,4},{8,10},{10,8},{12,14},{14,12},{16,18},{18,... | collective-permute-start | bytes 3538952 | tf_op jit(solution)/shard_map/ppermute | solution.py:131
  659.9 33.1 %collective-permute-start.76 = (bf16[384,1536]{1,0:T(8,128)(2,1)S(1)}, bf16[384,1536]{1,0:T(8,128)(2,1)}, u32[]{:S(2)}, u32[]{:S(2)}) collective-permute-start(bf16[384,1536]{1,0:T(8,128)(2,1)S(1)} %bitcast.554), channel_id=1, source_target_pairs={{0,2},{2,0},{4,6},{6,4},{8,10},{10,8},{12,14},{14,12},{16,18},{18,... | collective-permute-start | bytes 3538952 | tf_op jit(solution)/shard_map/ppermute | solution.py:131
  660.0 37.4 %collective-permute-start.92 = (bf16[768,768]{1,0:T(8,128)(2,1)}, bf16[768,768]{1,0:T(8,128)(2,1)}, u32[]{:S(2)}, u32[]{:S(2)}) collective-permute-start(bf16[768,768]{1,0:T(8,128)(2,1)} %bitcast.551), channel_id=1, source_target_pairs={{0,2},{2,0},{4,6},{6,4},{8,10},{10,8},{12,14},{14,12},{16,18},{18,... | collective-permute-start | bytes 3538952 | tf_op jit(solution)/shard_map/ppermute | solution.py:131
  662.6 26.4 %collective-permute-start.28 = (bf16[384,1152]{1,0:T(8,128)(2,1)}, bf16[384,1152]{1,0:T(8,128)(2,1)}, u32[]{:S(2)}, u32[]{:S(2)}) collective-permute-start(bf16[384,1152]{1,0:T(8,128)(2,1)} %bitcast.585), channel_id=1, source_target_pairs={{0,2},{2,0},{4,6},{6,4},{8,10},{10,8},{12,14},{14,12},{16,18},{18,... | collective-permute-start | bytes 2654216 | tf_op jit(solution)/shard_map/ppermute | solution.py:131
  (281 other events, 2584.2 us)

commit v2 on v1

v2 whole, which is shorter than its diff:
```python
import functools

import jax
import jax.numpy as jnp
from jax import lax
from jax.experimental import pallas as pl
from jax.experimental.pallas import tpu as pltpu
from jax.sharding import PartitionSpec as P

HEAD = 64
PAIR = 2 * HEAD
EPSILON = 1e-05
MASKED_SCORE = -1000000000.0
FAR = 1e9
BF16 = jnp.bfloat16
F32 = jnp.float32
VMEM_LIMIT = 24 * 1024 * 1024
NN = ((1,), (0,))
NT = ((1,), (1,))
TN = ((0,), (0,))


def dot(left, right, contract):
    return lax.dot_general(left, right, (contract, ((), ())), preferred_element_type=F32)


def shape(rows, columns, dtype):
    return jax.ShapeDtypeStruct((rows, columns), dtype)


def run(body, outs, *args, scalars=0, scratch=(), flops=0):
    spaces = [pltpu.SMEM] * scalars + [pltpu.VMEM] * (len(args) - scalars)
    moved = sum(a.size * a.dtype.itemsize for a in (*args, *outs))
    return pl.pallas_call(
        body,
        out_shape=list(outs),
        in_specs=[pl.BlockSpec(memory_space=space) for space in spaces],
        out_specs=[pl.BlockSpec(memory_space=pltpu.VMEM)] * len(outs),
        scratch_shapes=list(scratch),
        compiler_params=pltpu.CompilerParams(vmem_limit_bytes=VMEM_LIMIT),
        cost_estimate=pl.CostEstimate(flops=flops, transcendentals=0, bytes_accessed=moved),
    )(*args)


def norm_parts(inputs):
    centre = inputs - jnp.mean(inputs, axis=-1, keepdims=True)
    inverse = lax.rsqrt(jnp.mean(centre * centre, axis=-1, keepdims=True) + EPSILON)
    return centre * inverse, inverse


def halves(count):
    half = count // 2
    return ((0, half), (half, 0))


def lane_half(which, rows):
    lanes = lax.broadcasted_iota(jnp.int32, (rows, PAIR), 1)
    return (lanes >= HEAD) if which else (lanes < HEAD)


def only_head(which, values):
    return jnp.where(lane_half(which, values.shape[0]), values, jnp.zeros_like(values))


def key_scores(key_pair, query_pair, which, key_at, query_at):
    scores = dot(only_head(which, key_pair), query_pair, NT)
    return jnp.where(key_at <= query_at, scores, MASKED_SCORE)


def attend(q_ref, k_ref, v_ref, key_at_ref, query_at_ref, turned_ref, o_ref, log_ref):
    queries, local = q_ref.shape
    block = min(queries, 256)
    key_at = key_at_ref[...]
    for pair in range(local // PAIR):
        columns = pl.ds(pair * PAIR, PAIR)
        key_pair = k_ref[:, columns]
        value_turned = v_ref[:, columns].astype(F32).T.astype(BF16)
        for start in range(0, queries, block):
            rows = pl.ds(start, block)
            query_pair = q_ref[rows, columns]
            query_at = query_at_ref[:, rows]
            for which in range(2):
                head = 2 * pair + which
                scores = key_scores(key_pair, query_pair, which, key_at, query_at)
                top = jnp.max(scores, axis=0, keepdims=True)
                exponent = jnp.exp(scores - top)
                total = jnp.sum(exponent, axis=0, keepdims=True)
                weights = (exponent * (1.0 / total)).astype(BF16)
                log_ref[pl.ds(head, 1), rows] = top + jnp.log(total)
                mixed = dot(value_turned[which * HEAD : (which + 1) * HEAD], weights, NN)
                turned_ref[pl.ds(head * HEAD, HEAD), rows] = mixed.astype(BF16)
    o_ref[...] = turned_ref[...].astype(F32).T.astype(BF16)


def project(hidden, w_ref, which, bias):
    result = dot(hidden, w_ref[which], NN)
    return result if bias is None else result + bias


def finish(base_ref, send_ref, rows, base, partial):
    base_ref[rows] = base + partial
    send_ref[rows] = partial.astype(BF16)


def first_attention_body(
    own_ref, other_ref, gain_ref, offset_ref, w_in_ref, b_in_ref, w_out_ref, b_out_ref,
    key_at_ref, query_at_ref,
    h_ref, q_ref, k_ref, v_ref, turned_ref, log_ref, base_ref, send_ref, o_ref,
):
    half = own_ref.shape[0]
    for part, source in enumerate((own_ref, other_ref)):
        rows = pl.ds(part * half, half)
        normed, unused = norm_parts(source[...].astype(F32))
        hidden = (normed * gain_ref[...] + offset_ref[...]).astype(BF16)
        h_ref[rows] = hidden
        q_ref[rows] = (project(hidden, w_in_ref, 0, b_in_ref[0:1]).astype(BF16) * HEAD ** (-0.5)).astype(BF16)
        k_ref[rows] = project(hidden, w_in_ref, 1, None).astype(BF16)
        v_ref[rows] = project(hidden, w_in_ref, 2, b_in_ref[1:2]).astype(BF16)
    attend(q_ref, k_ref, v_ref, key_at_ref, query_at_ref, turned_ref, o_ref, log_ref)
    for part, source in enumerate((own_ref, other_ref)):
        rows = pl.ds(part * half, half)
        partial = dot(o_ref[rows], w_out_ref[...], NN)
        finish(base_ref, send_ref, rows, source[...].astype(F32) + b_out_ref[...], partial)


def cross_attention_body(
    before_ref, recv_ref, gain_ref, offset_ref, w_in_ref, b_in_ref, w_out_ref, b_out_ref,
    k_ref, v_ref, key_at_ref, query_at_ref,
    x_ref, h_ref, q_ref, turned_ref, log_ref, base_ref, send_ref, o_ref,
):
    count = before_ref.shape[0]
    half = count // 2
    for mine, theirs in halves(count):
        rows = pl.ds(mine, half)
        value = before_ref[rows] + recv_ref[pl.ds(theirs, half)].astype(F32)
        x_ref[rows] = value
        normed, unused = norm_parts(value)
        hidden = (normed * gain_ref[...] + offset_ref[...]).astype(BF16)
        h_ref[rows] = hidden
        q_ref[rows] = (project(hidden, w_in_ref, 0, b_in_ref[0:1]).astype(BF16) * HEAD ** (-0.5)).astype(BF16)
    attend(q_ref, k_ref, v_ref, key_at_ref, query_at_ref, turned_ref, o_ref, log_ref)
    partial = dot(o_ref[...], w_out_ref[...], NN)
    finish(base_ref, send_ref, slice(None), x_ref[...] + b_out_ref[...], partial)


def memory_body(before_ref, recv_ref, w_in_ref, b_in_ref, mem_ref, k_ref, v_ref):
    count = before_ref.shape[0]
    half = count // 2
    for mine, theirs in halves(count):
        rows = pl.ds(mine, half)
        memory = (before_ref[rows] + recv_ref[pl.ds(theirs, half)].astype(F32)).astype(BF16)
        mem_ref[rows] = memory
        k_ref[rows] = project(memory, w_in_ref, 1, None).astype(BF16)
        v_ref[rows] = project(memory, w_in_ref, 2, b_in_ref[1:2]).astype(BF16)


ROOT = 0.7978845608028654
CUBIC = 0.044715


def feed_body(
    before_ref, recv_ref, gain_ref, offset_ref, w1_ref, b1_ref, w2_ref, b2_ref,
    x_ref, h_ref, f_ref, slope_ref, base_ref, send_ref,
):
    count = before_ref.shape[0]
    half = count // 2
    for mine, theirs in halves(count):
        rows = pl.ds(mine, half)
        value = before_ref[rows] + recv_ref[pl.ds(theirs, half)].astype(F32)
        x_ref[rows] = value
        normed, unused = norm_parts(value)
        hidden = (normed * gain_ref[...] + offset_ref[...]).astype(BF16)
        h_ref[rows] = hidden
        u = dot(hidden, w1_ref[...], NN) + b1_ref[...]
        square = u * u
        bent = jnp.tanh(u * (ROOT + (ROOT * CUBIC) * square))
        upper = 0.5 + 0.5 * bent
        active = (u * upper).astype(BF16)
        f_ref[rows] = active
        slope = upper + (0.5 * u) * (1.0 - bent * bent) * (ROOT + (3 * ROOT * CUBIC) * square)
        slope_ref[rows] = slope.astype(BF16)
        finish(base_ref, send_ref, rows, value + b2_ref[...], dot(active, w2_ref[...], NN))


def norm_back(gradient, normed, inverse, gain):
    scaled = gradient * gain
    mean_plain = jnp.mean(scaled, axis=-1, keepdims=True)
    mean_normed = jnp.mean(scaled * normed, axis=-1, keepdims=True)
    return inverse * (scaled - mean_plain - normed * mean_normed)


def column_sum(values):
    return jnp.sum(values.astype(F32), axis=0, keepdims=True)


def feed_back_body(kind, *refs):
    if kind == "dec":
        (cot_ref, cot_other_ref, weight_ref, w1_ref, w2_ref, slope_ref,
         g_ref, low_ref, du_ref, base_ref, send_ref, sums_ref, hidden_sums_ref) = refs
    else:
        (cot_ref, cot_other_ref, weight_ref, mem_base_ref, mem_recv_ref, w1_ref, w2_ref, slope_ref,
         g_ref, low_ref, du_ref, base_ref, send_ref, sums_ref, hidden_sums_ref) = refs
    count = g_ref.shape[0]
    half = count // 2
    hidden_sum = None
    for part, (mine, theirs) in enumerate(halves(count)):
        rows = pl.ds(mine, half)
        cot = (cot_ref if part == 0 else cot_other_ref)[...].astype(F32)
        gradient = cot * weight_ref[rows]
        if kind == "enc":
            gradient = gradient + (
                mem_base_ref[rows] + mem_recv_ref[pl.ds(theirs, half)].astype(F32)
            )
        g_ref[rows] = gradient
        low = gradient.astype(BF16)
        low_ref[rows] = low
        if part == 0:
            sums_ref[...] = column_sum(low)
        du = (dot(low, w2_ref[...], NT) * slope_ref[rows].astype(F32)).astype(BF16)
        du_ref[rows] = du
        partial_sum = column_sum(du)
        hidden_sum = partial_sum if hidden_sum is None else hidden_sum + partial_sum
        partial = dot(du, w1_ref[...], NT)
        base_ref[rows] = partial
        send_ref[rows] = partial.astype(BF16)
    hidden_sums_ref[...] = hidden_sum


def attention_back_body(kind, *refs):
    if kind == "cross":
        (g_in_ref, dh_ref, dh_recv_ref, x_ref, gain_ref, w_in_ref, w_out_ref, q_ref, k_ref, v_ref,
         log_ref, key_at_ref, query_at_ref,
         g_ref, low_ref, dq_ref, dk_ref, dv_ref, base_ref, send_ref, mem_base_ref, mem_send_ref,
         norm_sums_ref, sums_ref, bias_sums_ref, do_ref, turned_ref) = refs
    else:
        (g_in_ref, dh_ref, dh_recv_ref, x_ref, gain_ref, w_in_ref, w_out_ref, q_ref, k_ref, v_ref,
         log_ref, key_at_ref, query_at_ref,
         g_ref, low_ref, dq_ref, dk_ref, dv_ref, base_ref, send_ref,
         norm_sums_ref, sums_ref, bias_sums_ref, do_ref, turned_ref) = refs
    count, local = q_ref.shape
    half = count // 2
    for part, (mine, theirs) in enumerate(halves(count)):
        rows = pl.ds(mine, half)
        normed, inverse = norm_parts(x_ref[rows])
        dh = dh_ref[rows] + dh_recv_ref[pl.ds(theirs, half)].astype(F32)
        gradient = g_in_ref[rows] + norm_back(dh, normed, inverse, gain_ref[...])
        g_ref[rows] = gradient
        low = gradient.astype(BF16)
        low_ref[rows] = low
        if part == 0:
            norm_sums_ref[0:1] = column_sum(dh * normed)
            norm_sums_ref[1:2] = column_sum(dh)
            sums_ref[...] = column_sum(low)
        do_ref[rows] = dot(low, w_out_ref[...], NT).astype(BF16)
    block = min(count, 256)
    key_at = key_at_ref[...]
    keys = k_ref.shape[0]
    for pair in range(local // PAIR):
        columns = pl.ds(pair * PAIR, PAIR)
        key_pair = k_ref[:, columns]
        key_turned = key_pair.astype(F32).T.astype(BF16)
        value_pair = v_ref[:, columns]
        dk = [None, None]
        dv = [None, None]
        for start in range(0, count, block):
            rows = pl.ds(start, block)
            query_pair = q_ref[rows, columns]
            do_pair = do_ref[rows, columns]
            query_at = query_at_ref[:, rows]
            for which in range(2):
                head = 2 * pair + which
                scores = key_scores(key_pair, query_pair, which, key_at, query_at)
                probs = jnp.exp(scores - log_ref[pl.ds(head, 1), rows])
                prob_grad = dot(only_head(which, value_pair), do_pair, NT)
                product = probs * prob_grad
                inner = jnp.sum(product, axis=0, keepdims=True)
                score_grad = (product - probs * inner).astype(BF16)
                dv_part = dot(probs.astype(BF16), do_pair, NN)
                dk_part = dot(score_grad, query_pair, NN)
                dq_part = dot(key_turned[which * HEAD : (which + 1) * HEAD], score_grad, NN)
                turned_ref[pl.ds(head * HEAD, HEAD), rows] = dq_part * HEAD ** (-0.5)
                dk[which] = dk_part if dk[which] is None else dk[which] + dk_part
                dv[which] = dv_part if dv[which] is None else dv[which] + dv_part
        first = lane_half(0, keys)
        dk_ref[:, columns] = jnp.where(first, dk[0], dk[1]).astype(BF16)
        dv_ref[:, columns] = jnp.where(first, dv[0], dv[1]).astype(BF16)
    dq_ref[...] = turned_ref[...].T.astype(BF16)
    bias_sums_ref[0:1] = column_sum(dq_ref[...])
    bias_sums_ref[1:2] = column_sum(dv_ref[...])
    if kind == "cross":
        partial = dot(dq_ref[...], w_in_ref[0], NT)
        base_ref[...] = partial
        send_ref[...] = partial.astype(BF16)
        partial = dot(dk_ref[...], w_in_ref[1], NT) + dot(dv_ref[...], w_in_ref[2], NT)
        mem_base_ref[...] = partial
        mem_send_ref[...] = partial.astype(BF16)
    else:
        rest = pl.ds(half, half)
        own = pl.ds(0, half)
        for rows in (rest, own):
            partial = (
                dot(dq_ref[rows], w_in_ref[0], NT)
                + dot(dk_ref[rows], w_in_ref[1], NT)
                + dot(dv_ref[rows], w_in_ref[2], NT)
            )
            if rows is rest:
                send_ref[...] = partial.astype(BF16)
            else:
                base_ref[...] = partial


def last_norm_body(g_ref, dh_ref, recv_ref, x_ref, gain_ref, out_ref, norm_sums_ref):
    half = dh_ref.shape[0]
    normed, inverse = norm_parts(x_ref[...].astype(F32))
    dh = dh_ref[...] + recv_ref[...].astype(F32)
    norm_sums_ref[0:1] = column_sum(dh * normed)
    norm_sums_ref[1:2] = column_sum(dh)
    out_ref[...] = g_ref[0:half] + norm_back(dh, normed, inverse, gain_ref[...])


def feed_weights_body(bit_ref, h_ref, du_ref, f_ref, low_ref, send_ref, keep_ref):
    bit = bit_ref[0]
    width = h_ref.shape[1]
    part = width // 2
    for which, out_ref in ((1 - bit, send_ref), (bit, keep_ref)):
        left = h_ref[:, pl.ds(pl.multiple_of(which * part, 128), part)]
        for side in range(2):
            out_ref[pl.ds(side * part, part)] = dot(
                left, du_ref[:, pl.ds(side * width, width)], TN
            ).astype(BF16)
        left = f_ref[:, pl.ds(pl.multiple_of(which * width, 128), width)]
        out_ref[pl.ds(width, width)] = dot(left, low_ref[...], TN).astype(BF16)


def attention_weights_body(
    bit_ref, h_ref, mem_ref, dq_ref, dk_ref, dv_ref, turned_ref, low_ref, send_ref, keep_ref
):
    bit = bit_ref[0]
    width = h_ref.shape[1]
    part = width // 2
    quarter = width // 4
    left_side = pl.ds(0, part)
    right_side = pl.ds(part, part)
    for which, out_ref in ((1 - bit, send_ref), (bit, keep_ref)):
        columns = pl.ds(pl.multiple_of(which * part, 128), part)
        out_ref[pl.ds(0, part), left_side] = dot(h_ref[:, columns], dq_ref[...], TN).astype(BF16)
        memory = mem_ref[:, columns]
        out_ref[pl.ds(0, part), right_side] = dot(memory, dk_ref[...], TN).astype(BF16)
        values = dot(memory, dv_ref[...], TN).astype(BF16)
        out_ref[pl.ds(part, quarter), left_side] = values[:quarter]
        out_ref[pl.ds(part, quarter), right_side] = values[quarter:]
        rows = pl.ds(pl.multiple_of(which * quarter, 64), quarter)
        out_ref[pl.ds(part + quarter, quarter)] = dot(turned_ref[rows], low_ref[...], NN).astype(BF16)


def add_split_body(bit_ref, keep_ref, recv_ref, send_ref, next_ref):
    bit = bit_ref[0]
    rows = send_ref.shape[0]
    for which, out_ref in ((1 - bit, send_ref), (bit, next_ref)):
        part = pl.ds(pl.multiple_of(which * rows, 8), rows)
        out_ref[...] = (keep_ref[part].astype(F32) + recv_ref[part].astype(F32)).astype(BF16)


def swap(values):
    return lax.ppermute(values, "tensor", [(0, 1), (1, 0)])


def bits_of_dp():
    count = lax.axis_size("dp")
    here = lax.axis_index("dp")
    return [(1 << b, ((here >> b) & 1).reshape(1)) for b in range(count.bit_length() - 1)]


def across(values, stride):
    count = lax.axis_size("dp")
    return lax.ppermute(values, "dp", [(i, i ^ stride) for i in range(count)])


def scatter_sum(send, keep):
    bits = bits_of_dp()
    for step, (stride, unused) in enumerate(bits):
        received = across(send, stride)
        if step + 1 == len(bits):
            return (keep.astype(F32) + received.astype(F32)).astype(BF16)
        rows, width = keep.shape
        out = shape(rows // 2, width, BF16)
        send, keep = run(
            add_split_body, (out, out), bits[step + 1][1], keep, received, scalars=1
        )


def turned_index(index, count):
    bits = count.bit_length() - 1
    return sum(((index >> b) & 1) << (bits - 1 - b) for b in range(bits))


def place_body(in_ref, *refs):
    out_ref = refs[-1]
    out_ref[...] = in_ref[...].astype(F32).reshape(out_ref.shape)


def place(gathered, stacked, out_shape, grid, in_block, in_map, out_block, out_map):
    aliased = stacked is not None
    return pl.pallas_call(
        place_body,
        grid=grid,
        out_shape=jax.ShapeDtypeStruct(out_shape, F32),
        in_specs=[pl.BlockSpec(in_block, in_map)]
        + ([pl.BlockSpec(memory_space=pl.ANY)] if aliased else []),
        out_specs=pl.BlockSpec(out_block, out_map),
        input_output_aliases={1: 0} if aliased else {},
        compiler_params=pltpu.CompilerParams(vmem_limit_bytes=VMEM_LIMIT),
    )(gathered, *([stacked] if aliased else []))


def place_feed(gathered, at, layer, stacks, shapes):
    count = gathered.shape[0]
    width = gathered.shape[2]
    rows = 4 * width // count
    per_half = count // 2
    part = width // 2
    narrow = part // rows
    stacks["ffn_in"] = place(
        gathered, stacks.get("ffn_in"), shapes["ffn_in"], (2, 2, narrow),
        (1, rows, width),
        lambda h, c, j: (turned_index(h * per_half + c * narrow + j, count), at // rows, 0),
        (1, rows, width),
        lambda h, c, j: (layer, h * narrow + j, c),
    )
    wide = width // rows
    stacks["ffn_out"] = place(
        gathered, stacks.get("ffn_out"), shapes["ffn_out"], (2, wide),
        (1, rows, width),
        lambda h, j: (turned_index(h * per_half + wide + j, count), at // rows, 0),
        (1, rows, width),
        lambda h, j: (layer, h * wide + j, 0),
    )


def place_attention(gathered, at, layer, stacks, shapes):
    count = gathered.shape[0]
    width = gathered.shape[2]
    rows = 2 * width // count
    per_half = count // 2
    part = width // 2
    narrow = part // rows
    quarter = narrow // 2

    def in_map(c, h, j):
        value = c == 2
        shard = jnp.where(value, narrow + lax.rem(j, quarter), j)
        side = jnp.where(value, lax.div(j, quarter), c)
        return turned_index(h * per_half + shard, count), at // rows, side

    stacks["attn_in"] = place(
        gathered, stacks.get("attn_in"), shapes["attn_in"], (3, 2, narrow),
        (1, rows, part), in_map,
        (1, 1, rows, part),
        lambda c, h, j: (layer, c, h * narrow + j, 0),
    )
    stacks["attn_out"] = place(
        gathered, stacks.get("attn_out"), shapes["attn_out"], (2, quarter),
        (1, rows, width),
        lambda h, j: (turned_index(h * per_half + narrow + quarter + j, count), at // rows, 0),
        (1, rows, width),
        lambda h, j: (layer, h * quarter + j, 0),
    )


def total_small(values):
    for stride, unused in bits_of_dp():
        values = values + across(values, stride)
    return values


def on_device(
    src_embed, tgt_embed, src_mask, tgt_mask, objective, loss_mask, enc_cot, dec_cot,
    norm_gain, norm_bias, attn_in, attn_in_bias, attn_out, attn_out_bias,
    ffn_in, ffn_in_bias, ffn_out, ffn_out_bias,
):
    here = lax.axis_index("tensor")
    width = src_embed.shape[2]
    local = attn_in.shape[3]
    hidden_width = ffn_in.shape[2]
    source_own = src_embed.reshape(-1, width)
    target_own = tgt_embed.reshape(-1, width)
    enc_own = enc_cot.reshape(-1, width)
    dec_own = dec_cot.reshape(-1, width)
    source_other = swap(source_own)
    target_other = swap(target_own)
    enc_other = swap(enc_own)
    dec_other = swap(dec_own)
    loss_own = loss_mask.reshape(-1, 1).astype(F32)
    loss_all = jnp.concatenate([loss_own, swap(loss_own)], axis=0)
    sources = 2 * source_own.shape[0]
    targets = 2 * target_own.shape[0]

    def ordered(mask):
        pieces = mask.reshape(2, -1)
        return jnp.where(here == 0, pieces, pieces[::-1]).reshape(-1)

    position = lax.rem(
        jnp.arange(targets, dtype=jnp.int32) + here * (targets // 2), targets
    ).astype(F32)
    source_keys = jnp.where(ordered(src_mask) == 1, 0.0, FAR)[:, None]
    target_keys = jnp.where(ordered(tgt_mask) == 1, position, FAR)[:, None]
    nowhere_source = jnp.zeros((1, sources), F32)
    nowhere_target = jnp.zeros((1, targets), F32)
    target_queries = position[None, :]
    flag = objective.astype(F32)[0]
    enc_weight = jnp.broadcast_to(1.0 - 0.5 * flag, (sources, 1))
    dec_weight = (0.5 + 0.5 * flag) * (0.25 + 0.75 * loss_all)

    gains = [norm_gain[i : i + 1] for i in range(5)]
    offsets = [norm_bias[i : i + 1] for i in range(5)]
    b_out = [attn_out_bias[i : i + 1] for i in range(3)]
    b_two = [ffn_out_bias[i : i + 1] for i in range(2)]
    b_one = [ffn_in_bias[i : i + 1] for i in range(2)]

    def first_attention(own, other, norm, layer, key_at, query_at):
        count = 2 * own.shape[0]
        narrow = shape(count, local, BF16)
        return run(
            first_attention_body,
            (
                shape(count, width, BF16), narrow, narrow, narrow,
                shape(local, count, BF16), shape(8, count, F32),
                shape(count, width, F32), shape(count, width, BF16),
            ),
            own, other, gains[norm], offsets[norm], attn_in[layer], attn_in_bias[layer],
            attn_out[layer], b_out[layer], key_at, query_at,
            scratch=[pltpu.VMEM((count, local), BF16)],
            flops=8 * count * width * local + 4 * count * count * local,
        )

    def feed(before, recv, norm, layer):
        count = before.shape[0]
        return run(
            feed_body,
            (
                shape(count, width, F32), shape(count, width, BF16),
                shape(count, hidden_width, BF16), shape(count, hidden_width, BF16),
                shape(count, width, F32), shape(count, width, BF16),
            ),
            before, recv, gains[norm], offsets[norm], ffn_in[layer], b_one[layer],
            ffn_out[layer], b_two[layer],
            flops=4 * count * width * hidden_width,
        )

    h0, q0, k0, v0, turned0, log0, base0, send0 = first_attention(
        source_own, source_other, 0, 0, source_keys, nowhere_source
    )
    recv0 = swap(send0)
    h2, q1, k1, v1, turned1, log1, base1, send1 = first_attention(
        target_own, target_other, 2, 1, target_keys, target_queries
    )
    x1, h1, f0, slope0, base2, send2 = feed(base0, recv0, 1, 0)
    recv2 = swap(send2)
    recv1 = swap(send1)
    narrow = shape(sources, local, BF16)
    memory, k2, v2 = run(
        memory_body, (shape(sources, width, BF16), narrow, narrow),
        base2, recv2, attn_in[2], attn_in_bias[2],
        flops=4 * sources * width * local,
    )
    x3, h3, q2, turned2, log2, base3, send3 = run(
        cross_attention_body,
        (
            shape(targets, width, F32), shape(targets, width, BF16),
            shape(targets, local, BF16), shape(local, targets, BF16), shape(8, targets, F32),
            shape(targets, width, F32), shape(targets, width, BF16),
        ),
        base1, recv1, gains[3], offsets[3], attn_in[2], attn_in_bias[2], attn_out[2], b_out[2],
        k2, v2, source_keys, nowhere_target,
        scratch=[pltpu.VMEM((targets, local), BF16)],
        flops=4 * targets * width * local + 4 * targets * sources * local,
    )
    recv3 = swap(send3)
    x4, h4, f1, slope1, base4, send4 = feed(base3, recv3, 4, 1)
    half = targets // 2
    decoded = (base4[:half] + swap(send4[half:]).astype(F32)).astype(BF16)

    def feed_back(kind, cot, other, weight, extra, layer, slope):
        count = 2 * cot.shape[0]
        return run(
            functools.partial(feed_back_body, kind),
            (
                shape(count, width, F32), shape(count, width, BF16),
                shape(count, hidden_width, BF16),
                shape(count, width, F32), shape(count, width, BF16),
                shape(1, width, F32), shape(1, hidden_width, F32),
            ),
            cot, other, weight, *extra, ffn_in[layer], ffn_out[layer], slope,
            flops=4 * count * width * hidden_width,
        )

    def attention_back(kind, g, dh, recv, x, norm, layer, q, k, v, log, key_at, query_at):
        count = q.shape[0]
        keys = k.shape[0]
        outs = [
            shape(count, width, F32), shape(count, width, BF16),
            shape(count, local, BF16), shape(keys, local, BF16), shape(keys, local, BF16),
        ]
        if kind == "cross":
            outs += [
                shape(count, width, F32), shape(count, width, BF16),
                shape(keys, width, F32), shape(keys, width, BF16),
            ]
        else:
            outs += [shape(count // 2, width, F32), shape(count // 2, width, BF16)]
        outs += [shape(2, width, F32), shape(1, width, F32), shape(2, local, F32)]
        return run(
            functools.partial(attention_back_body, kind), outs,
            g, dh, recv, x, gains[norm], attn_in[layer], attn_out[layer], q, k, v, log,
            key_at, query_at,
            scratch=[pltpu.VMEM((count, local), BF16), pltpu.VMEM((local, count), F32)],
            flops=8 * count * width * local + 10 * count * keys * local,
        )

    core = bits_of_dp()[0][1]

    def feed_weights(h, du, f, low):
        out = shape(2 * width, width, BF16)
        return run(
            feed_weights_body, (out, out), core, h, du, f, low, scalars=1,
            flops=4 * h.shape[0] * width * hidden_width,
        )

    def attention_weights(h, mem, dq, dk, dv, turned, low):
        out = shape(width, width, BF16)
        return run(
            attention_weights_body, (out, out), core, h, mem, dq, dk, dv, turned, low, scalars=1,
            flops=8 * h.shape[0] * width * local,
        )

    def last_norm(g, dh, recv, own, norm):
        rows = own.shape[0]
        return run(
            last_norm_body, (shape(rows, width, F32), shape(2, width, F32)),
            g, dh, recv, own, gains[norm],
        )

    g4, low4, du1, dh4, dh4_send, two1, one1 = feed_back(
        "dec", dec_own, dec_other, dec_weight, (), 1, slope1
    )
    dh4_recv = swap(dh4_send)
    sum_feed1 = scatter_sum(*feed_weights(h4, du1, f1, low4))
    (
        g3, low3, dq2, dk2, dv2, dh3, dh3_send, mem_grad, mem_send, norm4, out2, in2,
    ) = attention_back(
        "cross", g4, dh4, dh4_recv, x4, 4, 2, q2, k2, v2, log2, source_keys, nowhere_target
    )
    mem_recv = swap(mem_send)
    dh3_recv = swap(dh3_send)
    sum_cross = scatter_sum(*attention_weights(h3, memory, dq2, dk2, dv2, turned2, low3))
    g1, low1, du0, dh1, dh1_send, two0, one0 = feed_back(
        "enc", enc_own, enc_other, enc_weight, (mem_grad, mem_recv), 0, slope0
    )
    dh1_recv = swap(dh1_send)
    sum_feed0 = scatter_sum(*feed_weights(h1, du0, f0, low1))
    g0, low0, dq0, dk0, dv0, dh0, dh0_send, norm1, out0, in0 = attention_back(
        "self", g1, dh1, dh1_recv, x1, 1, 0, q0, k0, v0, log0, source_keys, nowhere_source
    )
    dh0_recv = swap(dh0_send)
    sum_first = scatter_sum(*attention_weights(h0, h0, dq0, dk0, dv0, turned0, low0))
    g2, low2, dq1, dk1, dv1, dh2, dh2_send, norm3, out1, in1 = attention_back(
        "self", g3, dh3, dh3_recv, x3, 3, 1, q1, k1, v1, log1, target_keys, target_queries
    )
    dh2_recv = swap(dh2_send)
    sum_self = scatter_sum(*attention_weights(h2, h2, dq1, dk1, dv1, turned1, low2))
    source_grad, norm0 = last_norm(g0, dh0, dh0_recv, source_own, 0)
    target_grad, norm2 = last_norm(g2, dh2, dh2_recv, target_own, 2)

    shapes = {
        "attn_in": attn_in.shape, "attn_out": attn_out.shape,
        "ffn_in": ffn_in.shape, "ffn_out": ffn_out.shape,
    }
    stacks = {}
    early = lax.all_gather(jnp.concatenate([sum_feed1, sum_cross], axis=0), "dp")
    place_feed(early, 0, 1, stacks, shapes)
    place_attention(early, sum_feed1.shape[0], 2, stacks, shapes)
    late = lax.all_gather(jnp.concatenate([sum_feed0, sum_first, sum_self], axis=0), "dp")
    place_feed(late, 0, 0, stacks, shapes)
    place_attention(late, sum_feed0.shape[0], 0, stacks, shapes)
    place_attention(late, sum_feed0.shape[0] + sum_first.shape[0], 1, stacks, shapes)

    norms = [norm0, norm1, norm2, norm3, norm4]
    shared = jnp.concatenate(
        [n[0:1] for n in norms] + [n[1:2] for n in norms] + [out0, out1, out2, two0, two1], axis=0
    )
    apart = jnp.concatenate(
        [v.reshape(-1) for v in (in0, in1, in2, one0, one1)]
    ).reshape(-1, width)
    shared = shared + swap(shared)
    summed = total_small(jnp.concatenate([shared, apart], axis=0))
    shared, apart = summed[:15], summed[15:].reshape(-1)
    bias_rows = apart[: 6 * local].reshape(3, 2, local)
    hidden_rows = apart[6 * local :].reshape(2, -1)
    return (
        memory[: sources // 2][:, None],
        decoded[:, None],
        source_grad[:, None],
        target_grad[:, None],
        shared[0:5],
        shared[5:10],
        stacks["attn_in"],
        bias_rows,
        stacks["attn_out"],
        shared[10:13],
        stacks["ffn_in"],
        hidden_rows,
        stacks["ffn_out"],
        shared[13:15],
    )


def solution(mesh):
    tokens = P("tensor", "dp", None)
    return jax.shard_map(
        on_device,
        mesh=mesh,
        in_specs=(
            tokens, tokens, P("dp", None), P("dp", None), P("dp"), P("dp", "tensor"),
            tokens, tokens, P(), P(),
            P(None, None, None, "tensor"), P(None, None, "tensor"), P(None, "tensor", None), P(),
            P(None, None, "tensor"), P(None, "tensor"), P(None, "tensor", None), P(),
        ),
        out_specs=(
            tokens, tokens, tokens, tokens, P(), P(),
            P(None, None, None, "tensor"), P(None, None, "tensor"), P(None, "tensor", None), P(),
            P(None, None, "tensor"), P(None, "tensor"), P(None, "tensor", None), P(),
        ),
        check_vma=False,
    )
```

time: 715 us -> 549 us (0.77)
  matrix products: 86.2 us -> 0 us
  other arithmetic: 72.5 us -> 6.01 us
  starting transfers between devices: 100 us -> 41.5 us
  Pallas kernels: 91.6 us -> 123 us
  waiting for transfers between devices: 235 us -> 256 us
  local copies, waits for them, and re-layouts: 102 us -> 94.8 us
    dot_general x66 -> x0, matrix products: 86.2 us -> none  [the longest x48 66.3 us: dot(): lax.dot_general(left, right, (contract, ((), ())), preferred_element_type...]
    ppermute x17, waiting for transfers between devices: 36.4 us -> 103 us  [swap(): return lax.ppermute(values, 'tensor', [(0, 1), (1, 0)])]
    ppermute x84 -> x24, waiting for transfers between devices: 198 us -> 142 us  [across(): return lax.ppermute(values, 'dp', [(i, i ^ stride) for i in range(count)])]
    ppermute x84 -> x24, starting transfers between devices: 77.6 us -> 21.7 us  [across(): return lax.ppermute(values, 'dp', [(i, i ^ stride) for i in range(count)])]
    unnamed x462 -> x317, local copies, waits for them, and re-layouts: 22.7 us -> 68.1 us
    convert_element_type x50 -> x6, other arithmetic: 38.4 us -> 0.26 us  [the longest x5 0.25 us: scatter_sum(): return (keep.astype(F32) + received.astype(F32)).astype(BF16)]
    pallas_call x40 -> x43, Pallas kernels: 91.6 us -> 123 us  [the longest x33 79 us: run(): pl.pallas_call(body, out_shape=list(outs), in_specs=[pl.BlockSpec(memory_...]
    reduce_sum x26 -> x0, other arithmetic: 16.1 us -> none  [the longest x2 3.89 us: attention_backward(): small['gain', norm] = jnp.sum(total * normed, axis=0)]
  transfers between devices with their start and end apart: 101 -> 43, of which waited for: 42 -> 25; matrix products, arithmetic and copies ran while one was open for 34% -> 7% of each run, Pallas kernels for 12% -> 17%
where the time goes in v2:
time: 549 us; the launch traced here: 538 us
  waiting for transfers between devices  256 us (47%)
  Pallas kernels  123 us (22%)
  local copies, waits for them, and re-layouts  94.8 us (17%)
  starting transfers between devices  41.5 us (8%)
  between operations  16.6 us (3%)
  other arithmetic  6.01 us (1%)
    ppermute x24, waiting for transfers between devices, across(): return lax.ppermute(values, 'dp', [(i, i ^ stride) for i in range(count)])  142 us
    ppermute x17, waiting for transfers between devices, swap(): return lax.ppermute(values, 'tensor', [(0, 1), (1, 0)])  103 us
    pallas_call x33, Pallas kernels, run(): pl.pallas_call(body, out_shape=list(outs), in_specs=[pl.BlockSpec(memory_...  79 us
    unnamed x317, local copies, waits for them, and re-layouts  68.1 us
    pallas_call x10, Pallas kernels, place(): pl.pallas_call(place_body, grid=grid, out_shape=jax.ShapeDtypeStruct(out_...  43.9 us
    ppermute x24, starting transfers between devices, across(): return lax.ppermute(values, 'dp', [(i, i ^ stride) for i in range(count)])  21.7 us
    ppermute x17, starting transfers between devices, swap(): return lax.ppermute(values, 'tensor', [(0, 1), (1, 0)])  19.6 us
    all_gather x1, waiting for transfers between devices, on_device(): lax.all_gather(jnp.concatenate([sum_feed0, sum_first, sum_self], axis=0),...  11.7 us
  transfers between devices with their start and end apart: 43, of which 25 were waited for; matrix products, arithmetic and copies ran while one was open for 7% of the time, Pallas kernels for 17%

profile of v2, /device:TPU:0, one launch (start us, length us, event | category | flops | bytes accessed | tf_op | source)
XLA Modules:
  0.0 538.2 jit_solution(7736136833680291590)
XLA Ops:
  7.2 3.0 collective-permute-start
  18.0 4.9 slice_bitcast_fusion.1
  24.2 3.2 slice_bitcast_fusion.4
  27.5 10.4 %shard_map.281 = (bf16[512,768]{1,0:T(8,128)(2,1)S(1)}, bf16[512,384]{1,0:T(8,128)(2,1)S(1)}, bf16[512,384]{1,0:T(8,128)(2,1)S(1)}, bf16[512,384]{1,0:T(8,128)(2...) custom-call(bf16[256,768]{1,0:T(8,128)(2,1)S(1)} %bitcast.81, ...), custom_call_target="tpu_custom_call" | custom-call | flops 1610612736 | bytes 7897088 | tf_op jit(solution)/shard_map/pallas_call | solution.py:34
  47.4 4.2 slice_bitcast_fusion
  51.6 11.3 %collective-permute-done.1.recv_ref = bf16[512,768]{1,0:T(8,128)(2,1)} collective-permute-done((bf16[512,768]{1,0:T(8,128)(2,1)}, bf16[512,768]{1,0:T(8,128)(2,1)}, u32[]{:S(2)}, u32[]{:S(2)}) %collective-permute-start.1) | collective-permute-done | bytes 786464 | tf_op jit(solution)/shard_map/ppermute | solution.py:365
  63.0 6.1 %shard_map.282 = (f32[512,768]{1,0:T(8,128)S(1)}, bf16[512,768]{1,0:T(8,128)(2,1)S(1)}, bf16[512,1536]{1,0:T(8,128)(2,1)S(1)}, bf16[512,1536]{1,0:T(8,128)(2,1)S...) custom-call(f32[512,768]{1,0:T(8,128)S(1)} %copy-done.141, bf16[512,768]{1,0:T(8,128)(2,1)} %collective-permute-done.1.recv_ref, ...), custom_call_target="tpu_custom_call" | custom-call | flops 2415919104 | bytes 14957568 | tf_op jit(solution)/shard_map/pallas_call | solution.py:34
  83.5 4.4 shard_map.284
  97.2 6.3 %collective-permute-done.4.recv_ref = bf16[256,768]{1,0:T(8,128)(2,1)S(1)} collective-permute-done((bf16[256,768]{1,0:T(8,128)(2,1)S(1)}, bf16[256,768]{1,0:T(8,128)(2,1)S(1)}, u32[]{:S(2)}, u32[]{:S(2)}) %collective-permute-start.4) | collective-permute-done | bytes 393248 | tf_op jit(solution)/shard_map/ppermute | solution.py:365
  103.5 4.8 shard_map.285
  115.5 5.5 %collective-permute-done.9 = f32[128,1]{0,1:T(1,128)} collective-permute-done((f32[128,1]{0,1:T(1,128)S(1)}, f32[128,1]{0,1:T(1,128)}, u32[]{:S(2)}, u32[]{:S(2)}) %collective-permute-start.9) | collective-permute-done | bytes 544 | tf_op jit(solution)/shard_map/ppermute | solution.py:365
  129.9 3.3 shard_map.286
  134.0 4.1 shard_map.287
  144.0 10.6 %collective-permute-done.10.refs_2_ = bf16[256,768]{1,0:T(8,128)(2,1)S(1)} collective-permute-done((bf16[256,768]{1,0:T(8,128)(2,1)S(1)}, bf16[256,768]{1,0:T(8,128)(2,1)S(1)}, u32[]{:S(2)}, u32[]{:S(2)}) %collective-permute-start.10) | collective-permute-done | bytes 393248 | tf_op jit(solution)/shard_map/ppermute | solution.py:365
  154.6 5.1 shard_map.288
  164.9 3.1 shard_map.307
  172.3 24.8 %collective-permute-done.34.recv_ref = bf16[768,768]{1,0:T(8,128)(2,1)} collective-permute-done((bf16[768,768]{1,0:T(8,128)(2,1)}, bf16[768,768]{1,0:T(8,128)(2,1)}, u32[]{:S(2)}, u32[]{:S(2)}) %collective-permute-start.34) | collective-permute-done | bytes 1179680 | tf_op jit(solution)/shard_map/ppermute | solution.py:376
  202.9 6.3 %collective-permute-done.38.recv_ref = bf16[384,768]{1,0:T(8,128)(2,1)S(1)} collective-permute-done((bf16[384,768]{1,0:T(8,128)(2,1)}, bf16[384,768]{1,0:T(8,128)(2,1)S(1)}, u32[]{:S(2)}, u32[]{:S(2)}) %collective-permute-start.38) | collective-permute-done | bytes 589856 | tf_op jit(solution)/shard_map/ppermute | solution.py:376
  212.1 10.4 %collective-permute-done.39.recv_ref = bf16[192,768]{1,0:T(8,128)(2,1)S(1)} collective-permute-done((bf16[192,768]{1,0:T(8,128)(2,1)}, bf16[192,768]{1,0:T(8,128)(2,1)S(1)}, u32[]{:S(2)}, u32[]{:S(2)}) %collective-permute-start.39) | collective-permute-done | bytes 294944 | tf_op jit(solution)/shard_map/ppermute | solution.py:376
  229.7 9.3 %collective-permute-done.40 = bf16[96,768]{1,0:T(8,128)(2,1)S(1)} collective-permute-done((bf16[96,768]{1,0:T(8,128)(2,1)S(1)}, bf16[96,768]{1,0:T(8,128)(2,1)S(1)}, u32[]{:S(2)}, u32[]{:S(2)}) %collective-permute-start.40) | collective-permute-done | bytes 147488 | tf_op jit(solution)/shard_map/ppermute | solution.py:376
  239.1 5.3 collective-permute-done.36
  247.6 25.2 %collective-permute-done.7.refs_1_ = bf16[256,768]{1,0:T(8,128)(2,1)S(1)} collective-permute-done((bf16[256,768]{1,0:T(8,128)(2,1)}, bf16[256,768]{1,0:T(8,128)(2,1)S(1)}, u32[]{:S(2)}, u32[]{:S(2)}) %collective-permute-start.7) | collective-permute-done | bytes 393248 | tf_op jit(solution)/shard_map/ppermute | solution.py:365
  279.0 3.0 shard_map.289
  287.0 26.3 %collective-permute-done.14.refs_2_ = bf16[256,768]{1,0:T(8,128)(2,1)S(1)} collective-permute-done((bf16[256,768]{1,0:T(8,128)(2,1)S(1)}, bf16[256,768]{1,0:T(8,128)(2,1)S(1)}, u32[]{:S(2)}, u32[]{:S(2)}) %collective-permute-start.14) | collective-permute-done | bytes 393248 | tf_op jit(solution)/shard_map/ppermute | solution.py:365
  313.5 4.3 shard_map.292
  319.3 9.3 %shard_map.290 = (f32[512,768]{1,0:T(8,128)S(1)}, bf16[512,768]{1,0:T(8,128)(2,1)S(1)}, bf16[512,384]{1,0:T(8,128)(2,1)S(1)}, bf16[512,384]{1,0:T(8,128)(2,1)S(1...) custom-call(f32[512,768]{1,0:T(8,128)S(1)} %get-tuple-element.165.re, ...), custom_call_target="tpu_custom_call" | custom-call | flops 2214592512 | bytes 13798400 | tf_op jit(solution)/shard_map/pallas_call | solution.py:34
  335.2 24.9 %collective-permute-done.22.recv_ref = bf16[768,768]{1,0:T(8,128)(2,1)S(1)} collective-permute-done((bf16[768,768]{1,0:T(8,128)(2,1)S(1)}, bf16[768,768]{1,0:T(8,128)(2,1)S(1)}, u32[]{:S(2)}, u32[]{:S(2)}) %collective-permute-start.22) | collective-permute-done | bytes 1179680 | tf_op jit(solution)/shard_map/ppermute | solution.py:376
  360.5 12.3 %collective-permute-done.30.recv_ref = bf16[384,768]{1,0:T(8,128)(2,1)S(1)} collective-permute-done((bf16[384,768]{1,0:T(8,128)(2,1)S(1)}, bf16[384,768]{1,0:T(8,128)(2,1)S(1)}, u32[]{:S(2)}, u32[]{:S(2)}) %collective-permute-start.30) | collective-permute-done | bytes 589856 | tf_op jit(solution)/shard_map/ppermute | solution.py:376
  373.0 11.8 %collective-permute-done.26.recv_ref = bf16[384,768]{1,0:T(8,128)(2,1)S(1)} collective-permute-done((bf16[384,768]{1,0:T(8,128)(2,1)S(1)}, bf16[384,768]{1,0:T(8,128)(2,1)S(1)}, u32[]{:S(2)}, u32[]{:S(2)}) %collective-permute-start.26) | collective-permute-done | bytes 589856 | tf_op jit(solution)/shard_map/ppermute | solution.py:376
  385.1 3.4 collective-permute-start.32
  388.5 8.1 %collective-permute-done.27.recv_ref = bf16[192,768]{1,0:T(8,128)(2,1)S(1)} collective-permute-done((bf16[192,768]{1,0:T(8,128)(2,1)S(1)}, bf16[192,768]{1,0:T(8,128)(2,1)S(1)}, u32[]{:S(2)}, u32[]{:S(2)}) %collective-permute-start.27) | collective-permute-done | bytes 294944 | tf_op jit(solution)/shard_map/ppermute | solution.py:376
  400.0 12.2 %collective-permute-done.28 = bf16[96,768]{1,0:T(8,128)(2,1)S(1)} collective-permute-done((bf16[96,768]{1,0:T(8,128)(2,1)S(1)}, bf16[96,768]{1,0:T(8,128)(2,1)S(1)}, u32[]{:S(2)}, u32[]{:S(2)}) %collective-permute-start.28) | collective-permute-done | bytes 147488 | tf_op jit(solution)/shard_map/ppermute | solution.py:376
  412.2 5.6 %collective-permute-done.24 = bf16[192,768]{1,0:T(8,128)(2,1)S(1)} collective-permute-done((bf16[192,768]{1,0:T(8,128)(2,1)S(1)}, bf16[192,768]{1,0:T(8,128)(2,1)S(1)}, u32[]{:S(2)}, u32[]{:S(2)}) %collective-permute-start.24) | collective-permute-done | bytes 294944 | tf_op jit(solution)/shard_map/ppermute | solution.py:376
  419.9 5.5 %collective-permute-done.15.recv_ref = bf16[128,768]{1,0:T(8,128)(2,1)S(1)} collective-permute-done((bf16[128,768]{1,0:T(8,128)(2,1)}, bf16[128,768]{1,0:T(8,128)(2,1)S(1)}, u32[]{:S(2)}, u32[]{:S(2)}) %collective-permute-start.15) | collective-permute-done | bytes 196640 | tf_op jit(solution)/shard_map/ppermute | solution.py:365
  427.4 8.9 %collective-permute-done.13.recv_ref = bf16[256,768]{1,0:T(8,128)(2,1)S(1)} collective-permute-done((bf16[256,768]{1,0:T(8,128)(2,1)}, bf16[256,768]{1,0:T(8,128)(2,1)S(1)}, u32[]{:S(2)}, u32[]{:S(2)}) %collective-permute-start.13) | collective-permute-done | bytes 393248 | tf_op jit(solution)/shard_map/ppermute | solution.py:365
  441.7 3.5 collective-permute-done.16
  452.2 3.2 collective-permute-done.19
  460.8 4.7 collective-permute-done.20
  468.6 3.1 copy-done.1
  471.7 8.2 %shard_map.314.refs_0_ = f32[3,3,768,384]{3,2,1,0:T(8,128)} custom-call(bf16[16,288,768]{2,1,0:T(8,128)(2,1)S(1)} %bitcast.66), custom_call_target="tpu_custom_call" | custom-call | tf_op jit(solution)/shard_map/pallas_call | solution.py:404
  481.5 3.6 shard_map.320.refs_0_
  485.1 3.6 shard_map.322.refs_0_
  488.7 11.7 %all-gather.5.cloned.1.call-done = bf16[6144,768]{1,0:T(8,128)(2,1)} async-done(((bf16[384,768]{1,0:T(8,128)(2,1)}), bf16[6144,768]{1,0:T(8,128)(2,1)}) %all-gather.5.cloned.1.call-update) | async-done | bytes 9437200 | tf_op jit(solution)/shard_map/all_gather | solution.py:682
  500.4 3.7 copy-done
  504.1 8.2 %shard_map.315.refs_0_ = f32[3,3,768,384]{3,2,1,0:T(8,128)} custom-call(bf16[16,384,768]{2,1,0:T(8,128)(2,1)S(1)} %bitcast.60, f32[3,3,768,384]{3,2,1,0:T(8,128)} %shard_map.314.refs_0_), custom_call_target="tpu_custom_call", output_to_operand_aliasing={{}: (1, {})} | custom-call | tf_op jit(solution)/shard_map/pallas_call | solution.py:404
  512.3 8.2 %shard_map.316 = f32[3,3,768,384]{3,2,1,0:T(8,128)} custom-call(bf16[16,384,768]{2,1,0:T(8,128)(2,1)S(1)} %bitcast.61, f32[3,3,768,384]{3,2,1,0:T(8,128)} %shard_map.315.refs_0_), custom_call_target="tpu_custom_call", output_to_operand_aliasing={{}: (1, {})} | custom-call | tf_op jit(solution)/shard_map/pallas_call | solution.py:404
  523.7 3.6 shard_map.321
  527.3 3.6 shard_map.323
  (460 shorter events, 145.3 us)
Async XLA Ops:
  7.2 461.4 %all-gather.7.cloned.1.call-start = ((), (), s32[]{:S(2)}) async-start(), calls=%async_computation.1 | async-start | bytes 7520256 | tf_op jit(solution)/shard_map/all_gather | solution.py:679
  7.2 20.2 %collective-permute-start = (bf16[256,768]{1,0:T(8,128)(2,1)}, bf16[256,768]{1,0:T(8,128)(2,1)}, u32[]{:S(2)}, u32[]{:S(2)}) collective-permute-start(bf16[256,768]{1,0:T(8,128)(2,1)} %bitcast.80), channel_id=1, source_target_pairs={{0,1},{1,0},{2,3},{3,2},{4,5},{5,4},{6,7},{7,6},{8,9},{9,8},{10,11... | collective-permute-start | bytes 1179656 | tf_op jit(solution)/shard_map/ppermute | solution.py:365
  10.3 69.1 %collective-permute-start.3 = (bf16[128,768]{1,0:T(8,128)(2,1)}, bf16[128,768]{1,0:T(8,128)(2,1)}, u32[]{:S(2)}, u32[]{:S(2)}) collective-permute-start(bf16[128,768]{1,0:T(8,128)(2,1)} %bitcast.75), channel_id=1, source_target_pairs={{0,1},{1,0},{2,3},{3,2},{4,5},{5,4},{6,7},{7,6},{8,9},{9,8},{10,11... | collective-permute-start | bytes 589832 | tf_op jit(solution)/shard_map/ppermute | solution.py:365
  43.6 19.3 %collective-permute-start.1 = (bf16[512,768]{1,0:T(8,128)(2,1)}, bf16[512,768]{1,0:T(8,128)(2,1)}, u32[]{:S(2)}, u32[]{:S(2)}) collective-permute-start(bf16[512,768]{1,0:T(8,128)(2,1)} %get-tuple-element.143), channel_id=1, source_target_pairs={{0,1},{1,0},{2,3},{3,2},{4,5},{5,4},{6,7},{7,6},{8,9},{9,8},{10,11... | collective-permute-start | bytes 2359304 | tf_op jit(solution)/shard_map/ppermute | solution.py:365
  74.6 19.4 %collective-permute-start.2 = (bf16[512,768]{1,0:T(8,128)(2,1)}, bf16[512,768]{1,0:T(8,128)(2,1)}, u32[]{:S(2)}, u32[]{:S(2)}) collective-permute-start(bf16[512,768]{1,0:T(8,128)(2,1)} %get-tuple-element.145), channel_id=1, source_target_pairs={{0,1},{1,0},{2,3},{3,2},{4,5},{5,4},{6,7},{7,6},{8,9},{9,8},{10,11... | collective-permute-start | bytes 2359304 | tf_op jit(solution)/shard_map/ppermute | solution.py:365
  92.0 11.5 %collective-permute-start.4 = (bf16[256,768]{1,0:T(8,128)(2,1)S(1)}, bf16[256,768]{1,0:T(8,128)(2,1)S(1)}, u32[]{:S(2)}, u32[]{:S(2)}) collective-permute-start(bf16[256,768]{1,0:T(8,128)(2,1)S(1)} %get-tuple-element.148), channel_id=1, source_target_pairs={{0,1},{1,0},{2,3},{3,2},{4,5},{5,4},{6,7},{7,6},{8,9},{9,8},{10,11... | collective-permute-start | bytes 1179656 | tf_op jit(solution)/shard_map/ppermute | solution.py:365
  92.3 41.7 %collective-permute-start.8 = (bf16[128,768]{1,0:T(8,128)(2,1)}, bf16[128,768]{1,0:T(8,128)(2,1)}, u32[]{:S(2)}, u32[]{:S(2)}) collective-permute-start(bf16[128,768]{1,0:T(8,128)(2,1)} %bitcast.20.refs_0_), channel_id=1, source_target_pairs={{0,1},{1,0},{2,3},{3,2},{4,5},{5,4},{6,7},{7,6},{8,9},{9,8},{10,11... | collective-permute-start | bytes 589832 | tf_op jit(solution)/shard_map/ppermute | solution.py:365
  112.8 10.5 %collective-permute-start.5 = (bf16[256,768]{1,0:T(8,128)(2,1)}, bf16[256,768]{1,0:T(8,128)(2,1)}, u32[]{:S(2)}, u32[]{:S(2)}) collective-permute-start(bf16[256,768]{1,0:T(8,128)(2,1)} %get-tuple-element.152), channel_id=1, source_target_pairs={{0,1},{1,0},{2,3},{3,2},{4,5},{5,4},{6,7},{7,6},{8,9},{9,8},{10,11... | collective-permute-start | bytes 1179656 | tf_op jit(solution)/shard_map/ppermute | solution.py:365
  113.7 7.2 %collective-permute-start.9 = (f32[128,1]{0,1:T(1,128)S(1)}, f32[128,1]{0,1:T(1,128)}, u32[]{:S(2)}, u32[]{:S(2)}) collective-permute-start(f32[128,1]{0,1:T(1,128)S(1)} %convert_bitcast_fusion), channel_id=1, source_target_pairs={{0,1},{1,0},{2,3},{3,2},{4,5},{5,4},{6,7},{7,6},{8,9},{9,8},{10,11... | collective-permute-start | bytes 1544 | tf_op jit(solution)/shard_map/ppermute | solution.py:365
  143.0 20.2 %collective-permute-start.33 = (bf16[1536,768]{1,0:T(8,128)(2,1)}, bf16[1536,768]{1,0:T(8,128)(2,1)}, u32[]{:S(2)}, u32[]{:S(2)}) collective-permute-start(bf16[1536,768]{1,0:T(8,128)(2,1)} %get-tuple-element.249), channel_id=1, source_target_pairs={{0,2},{2,0},{4,6},{6,4},{8,10},{10,8},{12,14},{14,12},{16,18},{18,... | collective-permute-start | bytes 7077896 | tf_op jit(solution)/shard_map/ppermute | solution.py:376
  143.0 11.5 %collective-permute-start.10 = (bf16[256,768]{1,0:T(8,128)(2,1)S(1)}, bf16[256,768]{1,0:T(8,128)(2,1)S(1)}, u32[]{:S(2)}, u32[]{:S(2)}) collective-permute-start(bf16[256,768]{1,0:T(8,128)(2,1)S(1)} %get-tuple-element.158), channel_id=1, source_target_pairs={{0,1},{1,0},{2,3},{3,2},{4,5},{5,4},{6,7},{7,6},{8,9},{9,8},{10,11... | collective-permute-start | bytes 1179656 | tf_op jit(solution)/shard_map/ppermute | solution.py:365
  163.1 6.3 %collective-permute-start.37 = (bf16[768,768]{1,0:T(8,128)(2,1)}, bf16[768,768]{1,0:T(8,128)(2,1)}, u32[]{:S(2)}, u32[]{:S(2)}) collective-permute-start(bf16[768,768]{1,0:T(8,128)(2,1)} %get-tuple-element.263), channel_id=1, source_target_pairs={{0,2},{2,0},{4,6},{6,4},{8,10},{10,8},{12,14},{14,12},{16,18},{18,... | collective-permute-start | bytes 3538952 | tf_op jit(solution)/shard_map/ppermute | solution.py:376
  168.0 29.1 %collective-permute-start.34 = (bf16[768,768]{1,0:T(8,128)(2,1)}, bf16[768,768]{1,0:T(8,128)(2,1)}, u32[]{:S(2)}, u32[]{:S(2)}) collective-permute-start(bf16[768,768]{1,0:T(8,128)(2,1)} %get-tuple-element.251), channel_id=1, source_target_pairs={{0,4},{2,6},{4,0},{6,2},{8,12},{10,14},{12,8},{14,10},{16,20},{18,... | collective-permute-start | bytes 3538952 | tf_op jit(solution)/shard_map/ppermute | solution.py:376
  171.6 37.6 %collective-permute-start.38 = (bf16[384,768]{1,0:T(8,128)(2,1)}, bf16[384,768]{1,0:T(8,128)(2,1)S(1)}, u32[]{:S(2)}, u32[]{:S(2)}) collective-permute-start(bf16[384,768]{1,0:T(8,128)(2,1)} %get-tuple-element.265), channel_id=1, source_target_pairs={{0,4},{2,6},{4,0},{6,2},{8,12},{10,14},{12,8},{14,10},{16,20},{18,... | collective-permute-start | bytes 1769480 | tf_op jit(solution)/shard_map/ppermute | solution.py:376
  201.4 24.6 %collective-permute-start.35 = (bf16[384,768]{1,0:T(8,128)(2,1)}, bf16[384,768]{1,0:T(8,128)(2,1)S(1)}, u32[]{:S(2)}, u32[]{:S(2)}) collective-permute-start(bf16[384,768]{1,0:T(8,128)(2,1)} %get-tuple-element.253), channel_id=1, source_target_pairs={{0,8},{2,10},{4,12},{6,14},{8,0},{10,2},{12,4},{14,6},{16,24},{18,... | collective-permute-start | bytes 1769480 | tf_op jit(solution)/shard_map/ppermute | solution.py:376
  210.7 11.8 %collective-permute-start.39 = (bf16[192,768]{1,0:T(8,128)(2,1)}, bf16[192,768]{1,0:T(8,128)(2,1)S(1)}, u32[]{:S(2)}, u32[]{:S(2)}) collective-permute-start(bf16[192,768]{1,0:T(8,128)(2,1)} %get-tuple-element.267), channel_id=1, source_target_pairs={{0,8},{2,10},{4,12},{6,14},{8,0},{10,2},{12,4},{14,6},{16,24},{18,... | collective-permute-start | bytes 884744 | tf_op jit(solution)/shard_map/ppermute | solution.py:376
  223.5 15.5 %collective-permute-start.40 = (bf16[96,768]{1,0:T(8,128)(2,1)S(1)}, bf16[96,768]{1,0:T(8,128)(2,1)S(1)}, u32[]{:S(2)}, u32[]{:S(2)}) collective-permute-start(bf16[96,768]{1,0:T(8,128)(2,1)S(1)} %get-tuple-element.269), channel_id=1, source_target_pairs={{0,16},{2,18},{4,20},{6,22},{8,24},{10,26},{12,28},{14,30},{16,0},... | collective-permute-start | bytes 442376 | tf_op jit(solution)/shard_map/ppermute | solution.py:376
  229.0 43.9 %copy-start.30 = (bf16[512,1536]{1,0:T(8,128)(2,1)S(1)}, bf16[512,1536]{1,0:T(8,128)(2,1)}, u32[]{:S(2)}) copy-start(bf16[512,1536]{1,0:T(8,128)(2,1)} %copy-done.29) | copy-start | bytes 4718596
  229.1 15.3 %collective-permute-start.36 = (bf16[192,768]{1,0:T(8,128)(2,1)S(1)}, bf16[192,768]{1,0:T(8,128)(2,1)S(1)}, u32[]{:S(2)}, u32[]{:S(2)}) collective-permute-start(bf16[192,768]{1,0:T(8,128)(2,1)S(1)} %get-tuple-element.255), channel_id=1, source_target_pairs={{0,16},{2,18},{4,20},{6,22},{8,24},{10,26},{12,28},{14,30},{16,0},... | collective-permute-start | bytes 884744 | tf_op jit(solution)/shard_map/ppermute | solution.py:376
  245.3 255.1 %all-gather.5.cloned.1.call-start = ((), (), s32[]{:S(2)}) async-start(), calls=%async_computation | async-start | bytes 10027008 | tf_op jit(solution)/shard_map/all_gather | solution.py:682
  245.5 27.3 %collective-permute-start.11 = (bf16[512,768]{1,0:T(8,128)(2,1)}, bf16[512,768]{1,0:T(8,128)(2,1)S(1)}, u32[]{:S(2)}, u32[]{:S(2)}) collective-permute-start(bf16[512,768]{1,0:T(8,128)(2,1)} %copy-done.125), channel_id=1, source_target_pairs={{0,1},{1,0},{2,3},{3,2},{4,5},{5,4},{6,7},{7,6},{8,9},{9,8},{10,11... | collective-permute-start | bytes 2359304 | tf_op jit(solution)/shard_map/ppermute | solution.py:365
  246.6 26.2 %collective-permute-start.7 = (bf16[256,768]{1,0:T(8,128)(2,1)}, bf16[256,768]{1,0:T(8,128)(2,1)S(1)}, u32[]{:S(2)}, u32[]{:S(2)}) collective-permute-start(bf16[256,768]{1,0:T(8,128)(2,1)} %bitcast.78), channel_id=1, source_target_pairs={{0,1},{1,0},{2,3},{3,2},{4,5},{5,4},{6,7},{7,6},{8,9},{9,8},{10,11... | collective-permute-start | bytes 1179656 | tf_op jit(solution)/shard_map/ppermute | solution.py:365
  282.1 31.3 %copy-start.13 = (bf16[384,768]{1,0:T(8,128)(2,1)S(1)}, bf16[384,768]{1,0:T(8,128)(2,1)}, u32[]{:S(2)}) copy-start(bf16[384,768]{1,0:T(8,128)(2,1)} %get-tuple-element.335.w_out_ref.refs_6_) | copy-start | bytes 1769476
  282.1 31.2 %copy-start.42 = (f32[256,1]{1,0:T(8,128)S(1)}, f32[256,1]{1,0:T(8,128)}, u32[]{:S(2)}) copy-start(f32[256,1]{1,0:T(8,128)} %copy-done.41) | copy-start | bytes 3076
  282.1 31.2 %copy-start.44 = (f32[256,768]{1,0:T(8,128)S(1)}, f32[256,768]{1,0:T(8,128)}, u32[]{:S(2)}) copy-start(f32[256,768]{1,0:T(8,128)} %copy-done.43) | copy-start | bytes 2359300
  282.1 31.2 %copy-start.46 = (f32[256,768]{1,0:T(8,128)S(1)}, f32[256,768]{1,0:T(8,128)}, u32[]{:S(2)}) copy-start(f32[256,768]{1,0:T(8,128)} %copy-done.45) | copy-start | bytes 2359300
  284.8 45.9 %collective-permute-start.21 = (bf16[1536,768]{1,0:T(8,128)(2,1)S(1)}, bf16[1536,768]{1,0:T(8,128)(2,1)S(1)}, u32[]{:S(2)}, u32[]{:S(2)}) collective-permute-start(bf16[1536,768]{1,0:T(8,128)(2,1)S(1)} %get-tuple-element.209), channel_id=1, source_target_pairs={{0,2},{2,0},{4,6},{6,4},{8,10},{10,8},{12,14},{14,12},{16,18},{18,... | collective-permute-start | bytes 7077896 | tf_op jit(solution)/shard_map/ppermute | solution.py:376
  284.9 34.0 %collective-permute-start.12 = (bf16[512,768]{1,0:T(8,128)(2,1)S(1)}, bf16[512,768]{1,0:T(8,128)(2,1)S(1)}, u32[]{:S(2)}, u32[]{:S(2)}) collective-permute-start(bf16[512,768]{1,0:T(8,128)(2,1)S(1)} %get-tuple-element.167), channel_id=1, source_target_pairs={{0,1},{1,0},{2,3},{3,2},{4,5},{5,4},{6,7},{7,6},{8,9},{9,8},{10,11... | collective-permute-start | bytes 2359304 | tf_op jit(solution)/shard_map/ppermute | solution.py:365
  285.9 27.4 %collective-permute-start.14 = (bf16[256,768]{1,0:T(8,128)(2,1)S(1)}, bf16[256,768]{1,0:T(8,128)(2,1)S(1)}, u32[]{:S(2)}, u32[]{:S(2)}) collective-permute-start(bf16[256,768]{1,0:T(8,128)(2,1)S(1)} %copy-done.130), channel_id=1, source_target_pairs={{0,1},{1,0},{2,3},{3,2},{4,5},{5,4},{6,7},{7,6},{8,9},{9,8},{10,11... | collective-permute-start | bytes 1179656 | tf_op jit(solution)/shard_map/ppermute | solution.py:365
  318.8 13.7 %collective-permute-start.29 = (bf16[768,768]{1,0:T(8,128)(2,1)S(1)}, bf16[768,768]{1,0:T(8,128)(2,1)S(1)}, u32[]{:S(2)}, u32[]{:S(2)}) collective-permute-start(bf16[768,768]{1,0:T(8,128)(2,1)S(1)} %get-tuple-element.237), channel_id=1, source_target_pairs={{0,2},{2,0},{4,6},{6,4},{8,10},{10,8},{12,14},{14,12},{16,18},{18,... | collective-permute-start | bytes 3538952 | tf_op jit(solution)/shard_map/ppermute | solution.py:376
  330.5 3.2 collective-permute-start.25
  331.3 28.9 %collective-permute-start.22 = (bf16[768,768]{1,0:T(8,128)(2,1)S(1)}, bf16[768,768]{1,0:T(8,128)(2,1)S(1)}, u32[]{:S(2)}, u32[]{:S(2)}) collective-permute-start(bf16[768,768]{1,0:T(8,128)(2,1)S(1)} %get-tuple-element.211), channel_id=1, source_target_pairs={{0,4},{2,6},{4,0},{6,2},{8,12},{10,14},{12,8},{14,10},{16,20},{18,... | collective-permute-start | bytes 3538952 | tf_op jit(solution)/shard_map/ppermute | solution.py:376
  332.8 40.0 %collective-permute-start.30 = (bf16[384,768]{1,0:T(8,128)(2,1)S(1)}, bf16[384,768]{1,0:T(8,128)(2,1)S(1)}, u32[]{:S(2)}, u32[]{:S(2)}) collective-permute-start(bf16[384,768]{1,0:T(8,128)(2,1)S(1)} %get-tuple-element.239), channel_id=1, source_target_pairs={{0,4},{2,6},{4,0},{6,2},{8,12},{10,14},{12,8},{14,10},{16,20},{18,... | collective-permute-start | bytes 1769480 | tf_op jit(solution)/shard_map/ppermute | solution.py:376
  334.0 50.8 %collective-permute-start.26 = (bf16[384,768]{1,0:T(8,128)(2,1)S(1)}, bf16[384,768]{1,0:T(8,128)(2,1)S(1)}, u32[]{:S(2)}, u32[]{:S(2)}) collective-permute-start(bf16[384,768]{1,0:T(8,128)(2,1)S(1)} %get-tuple-element.225), channel_id=1, source_target_pairs={{0,4},{2,6},{4,0},{6,2},{8,12},{10,14},{12,8},{14,10},{16,20},{18,... | collective-permute-start | bytes 1769480 | tf_op jit(solution)/shard_map/ppermute | solution.py:376
  360.4 37.2 %collective-permute-start.23 = (bf16[384,768]{1,0:T(8,128)(2,1)S(1)}, bf16[384,768]{1,0:T(8,128)(2,1)S(1)}, u32[]{:S(2)}, u32[]{:S(2)}) collective-permute-start(bf16[384,768]{1,0:T(8,128)(2,1)S(1)} %get-tuple-element.213), channel_id=1, source_target_pairs={{0,8},{2,10},{4,12},{6,14},{8,0},{10,2},{12,4},{14,6},{16,24},{18,... | collective-permute-start | bytes 1769480 | tf_op jit(solution)/shard_map/ppermute | solution.py:376
  372.9 12.1 %collective-permute-start.31 = (bf16[192,768]{1,0:T(8,128)(2,1)S(1)}, bf16[192,768]{1,0:T(8,128)(2,1)S(1)}, u32[]{:S(2)}, u32[]{:S(2)}) collective-permute-start(bf16[192,768]{1,0:T(8,128)(2,1)S(1)} %get-tuple-element.241), channel_id=1, source_target_pairs={{0,8},{2,10},{4,12},{6,14},{8,0},{10,2},{12,4},{14,6},{16,24},{18,... | collective-permute-start | bytes 884744 | tf_op jit(solution)/shard_map/ppermute | solution.py:376
  385.0 11.7 %collective-permute-start.27 = (bf16[192,768]{1,0:T(8,128)(2,1)S(1)}, bf16[192,768]{1,0:T(8,128)(2,1)S(1)}, u32[]{:S(2)}, u32[]{:S(2)}) collective-permute-start(bf16[192,768]{1,0:T(8,128)(2,1)S(1)} %get-tuple-element.227), channel_id=1, source_target_pairs={{0,8},{2,10},{4,12},{6,14},{8,0},{10,2},{12,4},{14,6},{16,24},{18,... | collective-permute-start | bytes 884744 | tf_op jit(solution)/shard_map/ppermute | solution.py:376
  385.1 14.8 %collective-permute-start.32 = (bf16[96,768]{1,0:T(8,128)(2,1)S(1)}, bf16[96,768]{1,0:T(8,128)(2,1)S(1)}, u32[]{:S(2)}, u32[]{:S(2)}) collective-permute-start(bf16[96,768]{1,0:T(8,128)(2,1)S(1)} %get-tuple-element.243), channel_id=1, source_target_pairs={{0,16},{2,18},{4,20},{6,22},{8,24},{10,26},{12,28},{14,30},{16,0},... | collective-permute-start | bytes 442376 | tf_op jit(solution)/shard_map/ppermute | solution.py:376
  396.7 15.5 %collective-permute-start.28 = (bf16[96,768]{1,0:T(8,128)(2,1)S(1)}, bf16[96,768]{1,0:T(8,128)(2,1)S(1)}, u32[]{:S(2)}, u32[]{:S(2)}) collective-permute-start(bf16[96,768]{1,0:T(8,128)(2,1)S(1)} %get-tuple-element.229), channel_id=1, source_target_pairs={{0,16},{2,18},{4,20},{6,22},{8,24},{10,26},{12,28},{14,30},{16,0},... | collective-permute-start | bytes 442376 | tf_op jit(solution)/shard_map/ppermute | solution.py:376
  397.8 20.1 %collective-permute-start.24 = (bf16[192,768]{1,0:T(8,128)(2,1)S(1)}, bf16[192,768]{1,0:T(8,128)(2,1)S(1)}, u32[]{:S(2)}, u32[]{:S(2)}) collective-permute-start(bf16[192,768]{1,0:T(8,128)(2,1)S(1)} %get-tuple-element.215), channel_id=1, source_target_pairs={{0,16},{2,18},{4,20},{6,22},{8,24},{10,26},{12,28},{14,30},{16,0},... | collective-permute-start | bytes 884744 | tf_op jit(solution)/shard_map/ppermute | solution.py:376
  418.9 6.5 %collective-permute-start.15 = (bf16[128,768]{1,0:T(8,128)(2,1)}, bf16[128,768]{1,0:T(8,128)(2,1)S(1)}, u32[]{:S(2)}, u32[]{:S(2)}) collective-permute-start(bf16[128,768]{1,0:T(8,128)(2,1)} %copy-done.133), channel_id=1, source_target_pairs={{0,1},{1,0},{2,3},{3,2},{4,5},{5,4},{6,7},{7,6},{8,9},{9,8},{10,11... | collective-permute-start | bytes 589832 | tf_op jit(solution)/shard_map/ppermute | solution.py:365
  426.6 9.8 %collective-permute-start.13 = (bf16[256,768]{1,0:T(8,128)(2,1)}, bf16[256,768]{1,0:T(8,128)(2,1)S(1)}, u32[]{:S(2)}, u32[]{:S(2)}) collective-permute-start(bf16[256,768]{1,0:T(8,128)(2,1)} %copy-done.128), channel_id=1, source_target_pairs={{0,1},{1,0},{2,3},{3,2},{4,5},{5,4},{6,7},{7,6},{8,9},{9,8},{10,11... | collective-permute-start | bytes 1179656 | tf_op jit(solution)/shard_map/ppermute | solution.py:365
  441.0 4.2 collective-permute-start.16
  445.2 1.3 collective-permute-start.17
  446.5 4.4 collective-permute-start.18
  448.4 8.9 %collective-permute-start.6 = (bf16[128,768]{1,0:T(8,128)(2,1)S(1)}, bf16[128,768]{1,0:T(8,128)(2,1)S(1)}, u32[]{:S(2)}, u32[]{:S(2)}) collective-permute-start(bf16[128,768]{1,0:T(8,128)(2,1)S(1)} %slice.201), channel_id=1, source_target_pairs={{0,1},{1,0},{2,3},{3,2},{4,5},{5,4},{6,7},{7,6},{8,9},{9,8},{10,11... | collective-permute-start | bytes 589832 | tf_op jit(solution)/shard_map/ppermute | solution.py:365
  451.0 4.4 collective-permute-start.19
  455.4 10.1 %collective-permute-start.20 = (f32[22,768]{1,0:T(8,128)S(1)}, f32[22,768]{1,0:T(8,128)S(1)}, u32[]{:S(2)}, u32[]{:S(2)}) collective-permute-start(f32[22,768]{1,0:T(8,128)S(1)} %add.89), channel_id=1, source_target_pairs={{0,16},{2,18},{4,20},{6,22},{8,24},{10,26},{12,28},{14,30},{16,0},... | collective-permute-start | bytes 202760 | tf_op jit(solution)/shard_map/ppermute | solution.py:376
  (148 other events, 979.8 us)
Sparse Core Ops, SparseCore 0:
  245.4 67.2 all-gather.6
  418.9 81.4 all-gather.4

commit v3 on v2

v3 whole, which is shorter than its diff:
```python
import functools

import jax
import jax.numpy as jnp
from jax import lax
from jax.experimental import pallas as pl
from jax.experimental.pallas import tpu as pltpu
from jax.sharding import PartitionSpec as P

HEAD = 64
PAIR = 2 * HEAD
EPSILON = 1e-05
MASKED_SCORE = -1000000000.0
FAR = 1e9
ROOT = 0.7978845608028654
CUBIC = 0.044715
BF16 = jnp.bfloat16
F32 = jnp.float32
VMEM_LIMIT = 18 * 1024 * 1024
BYTES = 3690000
NN = ((1,), (0,))
NT = ((1,), (1,))
TN = ((0,), (0,))
TOKEN = jax.ShapeDtypeStruct((8, 128), F32)


def dot(left, right, contract):
    return lax.dot_general(left, right, (contract, ((), ())), preferred_element_type=F32)


def shape(rows, columns, dtype):
    return jax.ShapeDtypeStruct((rows, columns), dtype)


NEAR = pl.BlockSpec(memory_space=pltpu.VMEM)
AWAY = pl.BlockSpec(memory_space=pl.ANY)
NUMBER = pl.BlockSpec(memory_space=pltpu.SMEM)


class Weight:
    def __init__(self, stack, layer):
        self.stack = stack
        self.layer = layer


class Params:
    def __init__(self, *arrays):
        self.arrays = arrays


class Fetch:
    def __init__(self, source, buffer, semaphore):
        self.copy = pltpu.make_async_copy(source, buffer, semaphore)
        self.copy.start()
        self.buffer = buffer
        self.arrived = False

    def here(self):
        if not self.arrived:
            self.copy.wait()
            self.arrived = True
        return self.buffer


class Order:
    def __init__(self):
        self.token = None

    def call(self, body, outs, ins, microseconds=1, scratch=(), leave=(), limit=VMEM_LIMIT):
        tokens = [] if self.token is None else [self.token]
        specs, args, weights, groups = [], [], [], []
        for value in ins:
            if isinstance(value, Params):
                groups.append(len(args))
                for array in value.arrays:
                    specs.append(NEAR)
                    args.append(pltpu.with_memory_space_constraint(array, pltpu.VMEM))
            elif isinstance(value, Weight):
                weights.append((len(args), value))
                specs.append(AWAY)
                args.append(pltpu.with_memory_space_constraint(value.stack, pltpu.HBM))
            elif value.dtype == jnp.int32 and value.shape == (1,):
                specs.append(NUMBER)
                args.append(value)
            else:
                specs.append(NEAR)
                args.append(pltpu.with_memory_space_constraint(value, pltpu.VMEM))

        def wrapped(*refs):
            in_refs = list(refs[: len(args)])
            refs = refs[len(args) + len(tokens) :]
            out_refs = refs[: len(outs)]
            refs = refs[len(outs) + 1 :]
            if weights:
                semaphores = refs[-1]
                for i, (at, weight) in enumerate(weights):
                    in_refs[at] = Fetch(in_refs[at].at[weight.layer], refs[i], semaphores.at[i])
            for at in reversed(groups):
                in_refs[at : at + 6] = [in_refs[at : at + 6]]
            body(*in_refs, *out_refs, *refs[len(weights) : len(weights) + len(scratch)])

        buffers = [pltpu.VMEM(w.stack.shape[1:], w.stack.dtype) for unused, w in weights]
        semaphores = [pltpu.SemaphoreType.DMA((len(weights),))] if weights else []
        results = pl.pallas_call(
            wrapped,
            out_shape=[
                *[o if i in leave else pltpu.VMEM(o.shape, o.dtype) for i, o in enumerate(outs)],
                TOKEN,
            ],
            in_specs=specs + [AWAY] * len(tokens),
            out_specs=[NEAR] * len(outs) + [AWAY],
            scratch_shapes=[*buffers, *scratch, *semaphores],
            compiler_params=pltpu.CompilerParams(vmem_limit_bytes=limit),
            cost_estimate=pl.CostEstimate(
                flops=0, transcendentals=0, bytes_accessed=int(microseconds * BYTES)
            ),
        )(*args, *tokens)
        self.token = results[-1]
        return results[:-1]


def norm_parts(inputs):
    centre = inputs - jnp.mean(inputs, axis=-1, keepdims=True)
    inverse = lax.rsqrt(jnp.mean(centre * centre, axis=-1, keepdims=True) + EPSILON)
    return centre * inverse, inverse


def norm_back(gradient, normed, inverse, gain):
    scaled = gradient * gain
    mean_plain = jnp.mean(scaled, axis=-1, keepdims=True)
    mean_normed = jnp.mean(scaled * normed, axis=-1, keepdims=True)
    return inverse * (scaled - mean_plain - normed * mean_normed)


def column_sum(values):
    return jnp.sum(values.astype(F32), axis=0, keepdims=True)


def halves(count):
    half = count // 2
    return ((0, half), (half, 0))


def lane_half(which, rows):
    lanes = lax.broadcasted_iota(jnp.int32, (rows, PAIR), 1)
    return (lanes >= HEAD) if which else (lanes < HEAD)


def only_head(which, values):
    return jnp.where(lane_half(which, values.shape[0]), values, jnp.zeros_like(values))


def key_scores(key_pair, query_pair, which, key_at, query_at):
    scores = dot(only_head(which, key_pair), query_pair, NT)
    return jnp.where(key_at <= query_at, scores, MASKED_SCORE)


def attend(q_ref, k_ref, v_ref, key_at, query_at_ref, turned_ref, o_ref, log_ref):
    queries, local = q_ref.shape
    block = min(queries, 256)
    for pair in range(local // PAIR):
        columns = pl.ds(pair * PAIR, PAIR)
        key_pair = k_ref[:, columns]
        value_turned = v_ref[:, columns].astype(F32).T.astype(BF16)
        for start in range(0, queries, block):
            rows = pl.ds(start, block)
            query_pair = q_ref[rows, columns]
            query_at = 0.0 if query_at_ref is None else query_at_ref[:, rows]
            for which in range(2):
                head = 2 * pair + which
                scores = key_scores(key_pair, query_pair, which, key_at, query_at)
                top = jnp.max(scores, axis=0, keepdims=True)
                exponent = jnp.exp(scores - top)
                total = jnp.sum(exponent, axis=0, keepdims=True)
                weights = (exponent * (1.0 / total)).astype(BF16)
                log_ref[pl.ds(head, 1), rows] = top + jnp.log(total)
                mixed = dot(value_turned[which * HEAD : (which + 1) * HEAD], weights, NN)
                turned_ref[pl.ds(head * HEAD, HEAD), rows] = mixed.astype(BF16)
    o_ref[...] = turned_ref[...].astype(F32).T.astype(BF16)


def in_bias_rows(params, layer):
    return params[4][layer, 0:1], params[4][layer, 1:2]


def row_of(ref, index):
    return ref[index : index + 1]


def normalised(value, params, norm):
    normed, unused = norm_parts(value)
    return (normed * row_of(params[0], norm) + row_of(params[1], norm)).astype(BF16)


def column(row):
    return jnp.broadcast_to(row, (8, row.shape[1])).T[:, 0:1]


def own_first(row, here):
    half = row.shape[1] // 2
    return jnp.where(here == 0, row, jnp.concatenate([row[:, half:], row[:, :half]], axis=1))


def scaled_queries(hidden, w_in, bias):
    return ((dot(hidden, w_in[0], NN) + bias).astype(BF16) * HEAD ** (-0.5)).astype(BF16)


def first_attention(norm, layer, own_ref, other_ref, params, w_in, w_out, key_at, query_at_ref, *refs):
    h_ref, q_ref, k_ref, v_ref, turned_ref, log_ref, base_ref, send_ref, o_ref = refs
    half = own_ref.shape[0]
    query_bias, value_bias = in_bias_rows(params, layer)
    for part, source in enumerate((own_ref, other_ref)):
        rows = pl.ds(part * half, half)
        hidden = normalised(source[...].astype(F32), params, norm)
        h_ref[rows] = hidden
        w = w_in.here()
        q_ref[rows] = scaled_queries(hidden, w, query_bias)
        k_ref[rows] = dot(hidden, w[1], NN).astype(BF16)
        v_ref[rows] = (dot(hidden, w[2], NN) + value_bias).astype(BF16)
    attend(q_ref, k_ref, v_ref, key_at, query_at_ref, turned_ref, o_ref, log_ref)
    w = w_out.here()
    for part, source in enumerate((own_ref, other_ref)):
        rows = pl.ds(part * half, half)
        partial = dot(o_ref[rows], w[...], NN)
        send_ref[rows] = partial.astype(BF16)
        base_ref[rows] = source[...].astype(F32) + row_of(params[2], layer) + partial


def enc_first_body(norm, layer, own_ref, other_ref, params, w_in, w_out, mask_ref, here_ref, *refs):
    outs, key_at_ref, o_ref = refs[:-2], refs[-2], refs[-1]
    row = own_first(jnp.where(mask_ref[...] == 1, 0.0, FAR), here_ref[0])
    key_at = column(row)
    key_at_ref[...] = key_at
    first_attention(norm, layer, own_ref, other_ref, params, w_in, w_out, key_at, None, *outs, o_ref)


def dec_first_body(
    norm, layer, own_ref, other_ref, params, w_in, w_out, mask_ref, here_ref,
    cot_ref, loss_ref, objective_ref, place_ref, *refs
):
    outs, (key_at_ref, query_at_ref, gradient_ref, gradient_send_ref, o_ref) = refs[:-5], refs[-5:]
    count = mask_ref.shape[1]
    position = own_first(
        lax.broadcasted_iota(jnp.int32, (1, count), 1).astype(F32), here_ref[0]
    )
    row = jnp.where(own_first(mask_ref[...].astype(F32), here_ref[0]) == 1.0, position, FAR)
    key_at = column(row)
    key_at_ref[...] = key_at
    query_at_ref[...] = position
    flag = objective_ref[0].astype(F32)
    weight = column(0.25 + 0.75 * loss_ref[...].astype(F32)) * (0.5 + 0.5 * flag)
    gradient = cot_ref[...].astype(F32) * weight
    gradient_ref[...] = gradient
    gradient_send_ref[...] = gradient.astype(BF16)
    first_attention(
        norm, layer, own_ref, other_ref, params, w_in, w_out, key_at, query_at_ref, *outs, o_ref
    )


def cross_attention_body(
    norm, layer, before_ref, recv_ref, params, w_in, w_out, k_ref, v_ref, key_at_ref,
    x_ref, h_ref, q_ref, turned_ref, log_ref, base_ref, send_ref, o_ref,
):
    count = x_ref.shape[0]
    half = count // 2
    query_bias, unused = in_bias_rows(params, layer)
    for mine, theirs in halves(count):
        rows = pl.ds(mine, half)
        value = before_ref[rows] + recv_ref[pl.ds(theirs, half)].astype(F32)
        x_ref[rows] = value
        hidden = normalised(value, params, norm)
        h_ref[rows] = hidden
        q_ref[rows] = scaled_queries(hidden, w_in.here(), query_bias)
    attend(q_ref, k_ref, v_ref, key_at_ref[...], None, turned_ref, o_ref, log_ref)
    partial = dot(o_ref[...], w_out.here()[...], NN)
    send_ref[...] = partial.astype(BF16)
    base_ref[...] = x_ref[...] + row_of(params[2], layer) + partial


def memory_body(layer, before_ref, recv_ref, params, w_in, mem_ref, k_ref, v_ref):
    count = mem_ref.shape[0]
    half = count // 2
    unused, value_bias = in_bias_rows(params, layer)
    for mine, theirs in halves(count):
        rows = pl.ds(mine, half)
        memory = (before_ref[rows] + recv_ref[pl.ds(theirs, half)].astype(F32)).astype(BF16)
        mem_ref[rows] = memory
        w = w_in.here()
        k_ref[rows] = dot(memory, w[1], NN).astype(BF16)
        v_ref[rows] = (dot(memory, w[2], NN) + value_bias).astype(BF16)


def feed_body(
    norm, layer, before_ref, recv_ref, params, w_one, w_two,
    x_ref, h_ref, f_ref, slope_ref, base_ref, send_ref,
):
    count = x_ref.shape[0]
    half = count // 2
    for mine, theirs in halves(count):
        rows = pl.ds(mine, half)
        value = before_ref[rows] + recv_ref[pl.ds(theirs, half)].astype(F32)
        x_ref[rows] = value
        hidden = normalised(value, params, norm)
        h_ref[rows] = hidden
        u = dot(hidden, w_one.here()[...], NN) + row_of(params[5], layer)
        square = u * u
        bent = jnp.tanh(u * (ROOT + (ROOT * CUBIC) * square))
        upper = 0.5 + 0.5 * bent
        active = (u * upper).astype(BF16)
        f_ref[rows] = active
        slope = upper + (0.5 * u) * (1.0 - bent * bent) * (ROOT + (3 * ROOT * CUBIC) * square)
        slope_ref[rows] = slope.astype(BF16)
        partial = dot(active, w_two.here()[...], NN)
        send_ref[rows] = partial.astype(BF16)
        base_ref[rows] = value + row_of(params[3], layer) + partial


def feed_back_rows(
    gradient, rows, w_one, w_two, slope_ref, g_ref, low_ref, du_ref, base_ref, send_ref
):
    g_ref[rows] = gradient
    low = gradient.astype(BF16)
    low_ref[rows] = low
    du = (dot(low, w_two.here()[...], NT) * slope_ref[rows].astype(F32)).astype(BF16)
    du_ref[rows] = du
    partial = dot(du, w_one.here()[...], NT)
    send_ref[rows] = partial.astype(BF16)
    base_ref[rows] = partial


def dec_feed_back_body(own_ref, other_ref, w_one, w_two, slope_ref, *outs):
    half = own_ref.shape[0]
    for part, source in enumerate((own_ref, other_ref)):
        feed_back_rows(
            source[...].astype(F32), pl.ds(part * half, half), w_one, w_two, slope_ref, *outs
        )


def source_seed(cot_ref, objective_ref):
    return cot_ref[...].astype(F32) * (1.0 - 0.5 * objective_ref[0].astype(F32))


def enc_feed_back_body(seed_ref, objective_ref, mem_base_ref, recv_ref, w_one, w_two, slope_ref, *outs):
    half = seed_ref.shape[0]
    own, other = pl.ds(0, half), pl.ds(half, half)
    for rows, theirs in ((own, other), (other, own)):
        gradient = mem_base_ref[rows] + recv_ref[theirs].astype(F32)
        if rows is own:
            gradient = gradient + source_seed(seed_ref, objective_ref)
        feed_back_rows(gradient, rows, w_one, w_two, slope_ref, *outs)


def attention_back_body(norm, cross, causal, *refs):
    (g_in_ref, dh_ref, dh_recv_ref, x_ref, params, w_in, w_out, q_ref, k_ref, v_ref, log_ref,
     key_at_ref), refs = refs[:12], refs[12:]
    query_at_ref = seed_ref = mem_base_ref = mem_send_ref = None
    if causal:
        query_at_ref, refs = refs[0], refs[1:]
    if cross:
        (seed_ref, objective_ref), refs = refs[:2], refs[2:]
    (g_ref, low_ref, dq_ref, dk_ref, dv_ref, base_ref, send_ref), refs = refs[:7], refs[7:]
    if cross:
        (mem_base_ref, mem_send_ref), refs = refs[:2], refs[2:]
    sums_ref, do_ref, turned_ref = refs
    gain = row_of(params[0], norm)
    count, local = dq_ref.shape
    half = count // 2
    for part, (mine, theirs) in enumerate(halves(count)):
        rows = pl.ds(mine, half)
        normed, inverse = norm_parts(x_ref[rows])
        dh = dh_ref[rows] + dh_recv_ref[pl.ds(theirs, half)].astype(F32)
        gradient = g_in_ref[rows] + norm_back(dh, normed, inverse, gain)
        g_ref[rows] = gradient
        low = gradient.astype(BF16)
        low_ref[rows] = low
        if part == 0:
            sums_ref[0:1] = column_sum(dh * normed)
            sums_ref[1:2] = column_sum(dh)
            sums_ref[2:3] = column_sum(low)
        do_ref[rows] = dot(low, w_out.here()[...], NT).astype(BF16)
    key_at = key_at_ref[...]
    block = min(count, 256)
    keys = k_ref.shape[0]
    for pair in range(local // PAIR):
        columns = pl.ds(pair * PAIR, PAIR)
        key_pair = k_ref[:, columns]
        key_turned = key_pair.astype(F32).T.astype(BF16)
        value_pair = v_ref[:, columns]
        dk = [None, None]
        dv = [None, None]
        for start in range(0, count, block):
            rows = pl.ds(start, block)
            query_pair = q_ref[rows, columns]
            do_pair = do_ref[rows, columns]
            query_at = 0.0 if query_at_ref is None else query_at_ref[:, rows]
            for which in range(2):
                head = 2 * pair + which
                scores = key_scores(key_pair, query_pair, which, key_at, query_at)
                probs = jnp.exp(scores - log_ref[pl.ds(head, 1), rows])
                prob_grad = dot(only_head(which, value_pair), do_pair, NT)
                product = probs * prob_grad
                inner = jnp.sum(product, axis=0, keepdims=True)
                score_grad = (product - probs * inner).astype(BF16)
                dv_part = dot(probs.astype(BF16), do_pair, NN)
                dk_part = dot(score_grad, query_pair, NN)
                dq_part = dot(key_turned[which * HEAD : (which + 1) * HEAD], score_grad, NN)
                turned_ref[pl.ds(head * HEAD, HEAD), rows] = dq_part * HEAD ** (-0.5)
                dk[which] = dk_part if dk[which] is None else dk[which] + dk_part
                dv[which] = dv_part if dv[which] is None else dv[which] + dv_part
        first = lane_half(0, keys)
        dk_ref[:, columns] = jnp.where(first, dk[0], dk[1]).astype(BF16)
        dv_ref[:, columns] = jnp.where(first, dv[0], dv[1]).astype(BF16)
    dq_ref[...] = turned_ref[...].T.astype(BF16)
    w = w_in.here()
    if cross:
        partial = dot(dk_ref[...], w[1], NT) + dot(dv_ref[...], w[2], NT)
        mem_base_ref[...] = partial
        mem_half = keys // 2
        mem_send_ref[0:mem_half] = (
            partial[0:mem_half] + source_seed(seed_ref, objective_ref)
        ).astype(BF16)
        mem_send_ref[mem_half:] = partial[mem_half:].astype(BF16)
        partial = dot(dq_ref[...], w[0], NT)
        send_ref[...] = partial.astype(BF16)
        base_ref[...] = partial
    else:
        for part in (1, 0):
            rows = pl.ds(part * half, half)
            partial = (
                dot(dq_ref[rows], w[0], NT)
                + dot(dk_ref[rows], w[1], NT)
                + dot(dv_ref[rows], w[2], NT)
            )
            if part == 1:
                send_ref[...] = partial.astype(BF16)
            else:
                base_ref[...] = partial


def last_norm_body(norm, g_ref, dh_ref, recv_ref, x_ref, params, out_ref, sums_ref):
    normed, inverse = norm_parts(x_ref[...].astype(F32))
    dh = dh_ref[...] + recv_ref[...].astype(F32)
    sums_ref[0:1] = column_sum(dh * normed)
    sums_ref[1:2] = column_sum(dh)
    half = out_ref.shape[0]
    out_ref[...] = g_ref[0:half] + norm_back(dh, normed, inverse, row_of(params[0], norm))


def feed_weights_body(h_ref, du_ref, f_ref, low_ref, place_ref, send_ref, keep_ref, sums_ref, hidden_sums_ref):
    bit = bit_of(place_ref, 0)
    width = h_ref.shape[1]
    part = width // 2
    for which, out_ref in ((1 - bit, send_ref), (bit, keep_ref)):
        left = h_ref[:, pl.ds(pl.multiple_of(which * part, 128), part)]
        for side in range(2):
            out_ref[pl.ds(side * part, part)] = dot(
                left, du_ref[:, pl.ds(side * width, width)], TN
            ).astype(BF16)
        left = f_ref[:, pl.ds(pl.multiple_of(which * width, 128), width)]
        out_ref[pl.ds(width, width)] = dot(left, low_ref[...], TN).astype(BF16)
    half = low_ref.shape[0] // 2
    sums_ref[...] = column_sum(low_ref[0:half])
    hidden_sums_ref[...] = column_sum(du_ref[...])


def attention_weights_body(
    h_ref, mem_ref, dq_ref, dk_ref, dv_ref, turned_ref, low_ref, place_ref, send_ref, keep_ref, sums_ref
):
    bit = bit_of(place_ref, 0)
    width = h_ref.shape[1]
    part = width // 2
    quarter = width // 4
    left_side = pl.ds(0, part)
    right_side = pl.ds(part, part)
    for which, out_ref in ((1 - bit, send_ref), (bit, keep_ref)):
        columns = pl.ds(pl.multiple_of(which * part, 128), part)
        out_ref[pl.ds(0, part), left_side] = dot(h_ref[:, columns], dq_ref[...], TN).astype(BF16)
        memory = mem_ref[:, columns]
        out_ref[pl.ds(0, part), right_side] = dot(memory, dk_ref[...], TN).astype(BF16)
        values = dot(memory, dv_ref[...], TN).astype(BF16)
        out_ref[pl.ds(part, quarter), left_side] = values[:quarter]
        out_ref[pl.ds(part, quarter), right_side] = values[quarter:]
        rows = pl.ds(pl.multiple_of(which * quarter, 64), quarter)
        out_ref[pl.ds(part + quarter, quarter)] = dot(turned_ref[rows], low_ref[...], NN).astype(BF16)
    sums_ref[:, left_side] = column_sum(dq_ref[...])
    sums_ref[:, right_side] = column_sum(dv_ref[...])


def bit_of(place_ref, step):
    return (place_ref[0] >> step) & 1


def add_body(step, keep_ref, received_ref, place_ref, send_ref, next_ref):
    bit = bit_of(place_ref, step)
    rows = send_ref.shape[0]
    block = rows
    while block % 32 == 0 and block > 128:
        block //= 2
    for out_ref, which in ((send_ref, 1 - bit), (next_ref, bit)):
        for start in range(0, rows, block):
            part = pl.ds(pl.multiple_of(which * rows + start, 8), block)
            out_ref[pl.ds(start, block)] = (
                keep_ref[part].astype(F32) + received_ref[part].astype(F32)
            ).astype(BF16)


def last_sums_body(*refs):
    out_ref = refs[-1]
    first = 0
    for keep_ref, received_ref in zip(refs[:-1:2], refs[1:-1:2]):
        rows = keep_ref.shape[0]
        total = keep_ref[...].astype(F32) + received_ref[...].astype(F32)
        out_ref[pl.ds(first, rows)] = total.astype(BF16)
        first += rows


def pass_body(value_ref, unused_ref, out_ref):
    out_ref[...] = value_ref[...]


def swap(values):
    return lax.ppermute(values, "tensor", [(0, 1), (1, 0)])


def strides_of_dp():
    return [1 << b for b in range(lax.axis_size("dp").bit_length() - 1)]


def across(values, stride):
    count = lax.axis_size("dp")
    return lax.ppermute(values, "dp", [(i, i ^ stride) for i in range(count)])


class Halving:
    def __init__(self, send, keep, place):
        self.strides = strides_of_dp()
        self.place = place
        self.at = 0
        self.keep = keep
        self.received = across(send, self.strides[0])

    def pending(self):
        return self.at + 1 < len(self.strides)

    def step(self, order):
        self.at += 1
        rows, width = self.keep.shape
        send, self.keep = order.call(
            functools.partial(add_body, self.at), [shape(rows // 2, width, BF16)] * 2,
            [self.keep, self.received, self.place],
        )
        self.received = across(send, self.strides[self.at])


def last_sums(order, halvings):
    rows = [part.keep.shape[0] for part in halvings]
    ins = [value for part in halvings for value in (part.keep, part.received)]
    (result,) = order.call(
        last_sums_body, [shape(sum(rows), halvings[0].keep.shape[1], BF16)], ins, leave=[0]
    )
    return result


def turned_index(index, count):
    bits = count.bit_length() - 1
    return sum(((index >> b) & 1) << (bits - 1 - b) for b in range(bits))


def place_body(count, width, groups, in_ref, *refs):
    wide_ref, semaphores = refs[-2:]
    outs = dict(zip(("ffn_in", "ffn_out", "attn_in", "attn_out"), refs[-7:-3]))
    step = pl.program_id(0)
    shard = turned_index(step, count)
    per_half = count // 2
    upper = lax.div(shard, per_half)
    index = lax.rem(shard, per_half)
    part = width // 2
    quarter = width // 4
    slot = lax.rem(step, 2)

    def copies(at):
        made = []
        for i, (kind, layer, first, rows) in enumerate(groups):
            for side in range(2):
                source = wide_ref.at[at, pl.ds(first, rows), pl.ds(side * part, part)]
                made.append((source, semaphores.at[at, 2 * i + side]))
        return made

    def wait(at):
        for i, (source, semaphore) in enumerate(copies(at)):
            rows = groups[i // 2][3]
            target = outs["ffn_out"].at[0, pl.ds(0, rows), pl.ds(0, part)]
            pltpu.make_async_copy(source, target, semaphore).wait()

    @pl.when(step >= 2)
    def free():
        wait(slot)

    wide_ref[slot] = in_ref[0].astype(F32)
    pairs = copies(slot)
    for i, (kind, layer, first, rows) in enumerate(groups):
        narrow = part // rows
        sources = pairs[2 * i : 2 * i + 2]

        def send(side, target):
            source, semaphore = sources[side]
            pltpu.make_async_copy(source, target, semaphore).start()

        if kind == "feed":
            column = lax.div(index, narrow)

            @pl.when(index < 2 * narrow)
            def first_matrix():
                row = pl.multiple_of(upper * part + lax.rem(index, narrow) * rows, 8)
                for side in range(2):
                    columns = pl.multiple_of(column * width + side * part, 128)
                    send(side, outs["ffn_in"].at[layer, pl.ds(row, rows), pl.ds(columns, part)])

            @pl.when(index >= 2 * narrow)
            def second_matrix():
                row = pl.multiple_of(upper * width + (index - 2 * narrow) * rows, 8)
                for side in range(2):
                    send(
                        side,
                        outs["ffn_out"].at[layer, pl.ds(row, rows), pl.ds(side * part, part)],
                    )
        else:
            few = quarter // rows

            @pl.when(index < narrow)
            def query_and_key():
                row = pl.multiple_of(upper * part + index * rows, 8)
                for side in range(2):
                    send(side, outs["attn_in"].at[layer, side, pl.ds(row, rows)])

            @pl.when((index >= narrow) & (index < narrow + few))
            def value():
                row = pl.multiple_of(upper * part + (index - narrow) * rows, 8)
                for side in range(2):
                    send(side, outs["attn_in"].at[layer, 2, pl.ds(row + side * quarter, rows)])

            @pl.when(index >= narrow + few)
            def output():
                row = pl.multiple_of(upper * quarter + (index - narrow - few) * rows, 8)
                for side in range(2):
                    send(
                        side,
                        outs["attn_out"].at[layer, pl.ds(row, rows), pl.ds(side * part, part)],
                    )

    @pl.when(step == count - 1)
    def drain():
        wait(1 - slot)
        wait(slot)


def place(order, gathered, groups, stacks, shapes):
    count, rows, width = gathered.shape
    previous = [] if stacks is None else stacks
    results = pl.pallas_call(
        functools.partial(place_body, count, width, groups),
        grid=(count,),
        out_shape=[*[jax.ShapeDtypeStruct(dims, F32) for dims in shapes], TOKEN],
        in_specs=[pl.BlockSpec((1, rows, width), lambda i: (i, 0, 0))]
        + [AWAY] * (len(previous) + 1),
        out_specs=[AWAY] * 5,
        scratch_shapes=[
            pltpu.VMEM((2, rows, width), F32),
            pltpu.SemaphoreType.DMA((2, 2 * len(groups))),
        ],
        input_output_aliases={1 + i: i for i in range(len(previous))},
        compiler_params=pltpu.CompilerParams(vmem_limit_bytes=VMEM_LIMIT),
        cost_estimate=pl.CostEstimate(flops=0, transcendentals=0, bytes_accessed=10 * BYTES),
    )(gathered, *previous, order.token)
    order.token = results[-1]
    return results[:-1]


def total_small(values):
    for stride in strides_of_dp():
        values = values + across(values, stride)
    return values


def on_device(
    src_embed, tgt_embed, src_mask, tgt_mask, objective, loss_mask, enc_cot, dec_cot,
    norm_gain, norm_bias, attn_in, attn_in_bias, attn_out, attn_out_bias,
    ffn_in, ffn_in_bias, ffn_out, ffn_out_bias,
):
    order = Order()
    here = lax.axis_index("tensor")
    width = src_embed.shape[2]
    local = attn_in.shape[3]
    hidden_width = ffn_in.shape[2]
    source_own = src_embed.reshape(-1, width)
    target_own = tgt_embed.reshape(-1, width)
    sources = 2 * source_own.shape[0]
    targets = 2 * target_own.shape[0]
    enc_own = enc_cot.reshape(-1, width)
    target_other = swap(target_own)
    source_other = swap(source_own)
    params = Params(norm_gain, norm_bias, attn_out_bias, ffn_out_bias, attn_in_bias, ffn_in_bias)
    core = lax.axis_index("dp").astype(jnp.int32).reshape(1)
    here = here.astype(jnp.int32).reshape(1)

    def first(body, own, other, norm, layer, mask, more_ins, more_outs):
        count = 2 * own.shape[0]
        narrow = shape(count, local, BF16)
        return order.call(
            functools.partial(body, norm, layer),
            [
                shape(count, width, BF16), narrow, narrow, narrow,
                shape(local, count, BF16), shape(8, count, F32),
                shape(count, width, F32), shape(count, width, BF16), shape(count, 1, F32),
                *more_outs,
            ],
            [own, other, params, Weight(attn_in, layer), Weight(attn_out, layer), mask, here, *more_ins],
            microseconds=count / 50,
            scratch=[pltpu.VMEM((count, local), BF16)],
        )

    def feed(before, recv, norm, layer):
        count = before.shape[0]
        return order.call(
            functools.partial(feed_body, norm, layer),
            [
                shape(count, width, F32), shape(count, width, BF16),
                shape(count, hidden_width, BF16), shape(count, hidden_width, BF16),
                shape(count, width, F32), shape(count, width, BF16),
            ],
            [before, recv, params, Weight(ffn_in, layer), Weight(ffn_out, layer)],
            microseconds=count / 90,
        )

    (
        h2, q1, k1, v1, turned1, log1, base1, send1, target_keys,
        target_queries, dec_own, dec_send,
    ) = first(
        dec_first_body, target_own, target_other, 2, 1, tgt_mask,
        [dec_cot.reshape(-1, width), loss_mask, objective, core],
        [shape(1, targets, F32), shape(targets // 2, width, F32), shape(targets // 2, width, BF16)],
    )
    recv1 = swap(send1)
    dec_other = swap(dec_send)
    h0, q0, k0, v0, turned0, log0, base0, send0, source_keys = first(
        enc_first_body, source_own, source_other, 0, 0, src_mask, [], []
    )
    recv0 = swap(send0)
    x1, h1, f0, slope0, base2, send2 = feed(base0, recv0, 1, 0)
    recv2 = swap(send2)
    narrow = shape(sources, local, BF16)
    memory, k2, v2 = order.call(
        functools.partial(memory_body, 2), [shape(sources, width, BF16), narrow, narrow],
        [base2, recv2, params, Weight(attn_in, 2)], microseconds=3,
    )
    x3, h3, q2, turned2, log2, base3, send3 = order.call(
        functools.partial(cross_attention_body, 3, 2),
        [
            shape(targets, width, F32), shape(targets, width, BF16),
            shape(targets, local, BF16), shape(local, targets, BF16), shape(8, targets, F32),
            shape(targets, width, F32), shape(targets, width, BF16),
        ],
        [
            base1, recv1, params, Weight(attn_in, 2), Weight(attn_out, 2), k2, v2, source_keys,
        ],
        microseconds=5,
        scratch=[pltpu.VMEM((targets, local), BF16)],
    )
    recv3 = swap(send3)
    x4, h4, f1, slope1, base4, send4 = feed(base3, recv3, 4, 1)

    def feed_back(body, layer, *ins):
        count = ins[-1].shape[0]
        return order.call(
            body,
            [
                shape(count, width, F32), shape(count, width, BF16),
                shape(count, hidden_width, BF16),
                shape(count, width, F32), shape(count, width, BF16),
            ],
            [*ins[:-1], Weight(ffn_in, layer), Weight(ffn_out, layer), ins[-1]],
            microseconds=count / 90,
        )

    def attention_back(cross, causal, g, dh, recv, x, norm, layer, q, k, v, log, key_at, *more):
        count = q.shape[0]
        keys = k.shape[0]
        outs = [
            shape(count, width, F32), shape(count, width, BF16),
            shape(count, local, BF16), shape(keys, local, BF16), shape(keys, local, BF16),
        ]
        if cross:
            outs += [
                shape(count, width, F32), shape(count, width, BF16),
                shape(keys, width, F32), shape(keys, width, BF16),
            ]
        else:
            outs += [shape(count // 2, width, F32), shape(count // 2, width, BF16)]
        outs += [shape(3, width, F32)]
        return order.call(
            functools.partial(attention_back_body, norm, cross, causal), outs,
            [
                g, dh, recv, x, params, Weight(attn_in, layer), Weight(attn_out, layer),
                q, k, v, log, key_at, *more,
            ],
            microseconds=count * keys / 28000,
            scratch=[pltpu.VMEM((count, local), BF16), pltpu.VMEM((local, count), F32)],
        )

    def feed_weights(h, du, f, low):
        out = shape(2 * width, width, BF16)
        send, keep, sums, hidden_sums = order.call(
            feed_weights_body, [out, out, shape(1, width, F32), shape(1, hidden_width, F32)],
            [h, du, f, low, core], microseconds=3,
        )
        return Halving(send, keep, core), sums, hidden_sums

    def attention_weights(h, mem, dq, dk, dv, turned, low):
        out = shape(width, width, BF16)
        send, keep, sums = order.call(
            attention_weights_body, [out, out, shape(1, width, F32)],
            [h, mem, dq, dk, dv, turned, low, core], microseconds=2,
        )
        return Halving(send, keep, core), sums

    def last_norm(g, dh, recv, own, norm):
        rows = own.shape[0]
        return order.call(
            functools.partial(last_norm_body, norm),
            [shape(rows, width, F32), shape(2, width, F32)],
            [g, dh, recv, own, params], leave=[0],
        )

    g4, low4, du1, dh4, dh4_send = feed_back(
        dec_feed_back_body, 1, dec_own, dec_other, slope1
    )
    dh4_recv = swap(dh4_send)
    sum_feed1, two1, one1 = feed_weights(h4, du1, f1, low4)
    g3, low3, dq2, dk2, dv2, dh3, dh3_send, mem_grad, mem_send, sums4 = attention_back(
        True, False, g4, dh4, dh4_recv, x4, 4, 2, q2, k2, v2, log2, source_keys, enc_own, objective
    )
    mem_recv = swap(mem_send)
    sum_feed1.step(order)
    sum_cross, in2 = attention_weights(h3, memory, dq2, dk2, dv2, turned2, low3)
    g1, low1, du0, dh1, dh1_send = feed_back(
        enc_feed_back_body, 0, enc_own, objective, mem_grad, mem_recv, slope0
    )
    dh1_recv = swap(dh1_send)
    sum_feed1.step(order)
    sum_cross.step(order)
    sum_feed0, two0, one0 = feed_weights(h1, du0, f0, low1)
    (dh3_late,) = order.call(
        pass_body, [shape(targets, width, BF16)], [dh3_send, dh1_recv], microseconds=0.5
    )
    dh3_recv = swap(dh3_late)
    g0, low0, dq0, dk0, dv0, dh0, dh0_send, sums1 = attention_back(
        False, False, g1, dh1, dh1_recv, x1, 1, 0, q0, k0, v0, log0, source_keys
    )
    dh0_recv = swap(dh0_send)
    sum_feed1.step(order)
    sum_cross.step(order)
    sum_feed0.step(order)
    sum_first, in0 = attention_weights(h0, h0, dq0, dk0, dv0, turned0, low0)
    g2, low2, dq1, dk1, dv1, dh2, dh2_send, sums3 = attention_back(
        False, True, g3, dh3, dh3_recv, x3, 3, 1, q1, k1, v1, log1, target_keys, target_queries
    )
    dh2_recv = swap(dh2_send)
    sum_self, in1 = attention_weights(h2, h2, dq1, dk1, dv1, turned1, low2)
    sum_first.step(order)
    source_grad, sums0 = last_norm(g0, dh0, dh0_recv, source_own, 0)
    sum_cross.step(order)
    sum_self.step(order)
    target_grad, sums2 = last_norm(g2, dh2, dh2_recv, target_own, 2)
    sum_feed0.step(order)
    early_parts, late_parts = [sum_feed1, sum_cross], [sum_feed0, sum_first, sum_self]
    for parts in (early_parts, late_parts):
        while any(part.pending() for part in parts):
            for part in parts:
                if part.pending():
                    part.step(order)
    early = lax.all_gather(last_sums(order, early_parts), "dp")
    late = lax.all_gather(last_sums(order, late_parts), "dp")
    half = targets // 2
    decoded = (base4[:half] + swap(send4[half:]).astype(F32)).astype(BF16)

    shapes = [ffn_in.shape, ffn_out.shape, attn_in.shape, attn_out.shape]
    wide, thin = sum_feed1.keep.shape[0], sum_cross.keep.shape[0]
    stacks = place(
        order, early, [("feed", 1, 0, wide), ("attention", 2, wide, thin)], None, shapes
    )
    stacks = place(
        order, late,
        [
            ("feed", 0, 0, wide), ("attention", 0, wide, thin),
            ("attention", 1, wide + thin, thin),
        ],
        stacks, shapes,
    )

    sums = [sums0, sums1, sums2, sums3, sums4]
    shared = jnp.concatenate(
        [v[0:1] for v in sums] + [v[1:2] for v in sums]
        + [sums1[2:3], sums3[2:3], sums4[2:3], two0, two1],
        axis=0,
    )
    apart = jnp.concatenate(
        [in0, in1, in2, one0.reshape(-1, width), one1.reshape(-1, width)], axis=0
    )
    shared = shared + swap(shared)
    summed = total_small(jnp.concatenate([shared, apart], axis=0))
    return (
        memory[: sources // 2][:, None],
        decoded[:, None],
        source_grad[:, None],
        target_grad[:, None],
        summed[0:5],
        summed[5:10],
        stacks[2],
        summed[15:18].reshape(3, 2, local),
        stacks[3],
        summed[10:13],
        stacks[0],
        summed[18:22].reshape(2, hidden_width),
        stacks[1],
        summed[13:15],
    )


def solution(mesh):
    tokens = P("tensor", "dp", None)
    return jax.shard_map(
        on_device,
        mesh=mesh,
        in_specs=(
            tokens, tokens, P("dp", None), P("dp", None), P("dp"), P("dp", "tensor"),
            tokens, tokens, P(), P(),
            P(None, None, None, "tensor"), P(None, None, "tensor"), P(None, "tensor", None), P(),
            P(None, None, "tensor"), P(None, "tensor"), P(None, "tensor", None), P(),
        ),
        out_specs=(
            tokens, tokens, tokens, tokens, P(), P(),
            P(None, None, None, "tensor"), P(None, None, "tensor"), P(None, "tensor", None), P(),
            P(None, None, "tensor"), P(None, "tensor"), P(None, "tensor", None), P(),
        ),
        check_vma=False,
    )
```

time: 549 us -> 490 us (0.89)
  local copies, waits for them, and re-layouts: 94.8 us -> 22.8 us
  waiting for transfers between devices: 256 us -> 296 us
  Pallas kernels: 123 us -> 98.8 us
    all_gather x2, waiting for transfers between devices: 11.7 us -> 84.5 us  [the longest x1 72.1 us: on_device(): late = lax.all_gather(last_sums(order, late_parts), 'dp')]
    unnamed x317 -> x54, local copies, waits for them, and re-layouts: 68.1 us -> 17.8 us
    ppermute x24, waiting for transfers between devices: 142 us -> 91.8 us  [across(): return lax.ppermute(values, 'dp', [(i, i ^ stride) for i in range(count)])]
    pallas_call x43 -> x38, Pallas kernels: 123 us -> 98.8 us  [the longest x36 82 us: call(): pl.pallas_call(wrapped, out_shape=[*[o if i in leave else pltpu.VMEM(o.sh...]
    ppermute x17 -> x15, waiting for transfers between devices: 103 us -> 119 us  [swap(): return lax.ppermute(values, 'tensor', [(0, 1), (1, 0)])]
    squeeze x5 -> x0, local copies, waits for them, and re-layouts: 16.3 us -> none  [the longest x1 4.89 us: feed(): ffn_in[layer]]
    ppermute x17 -> x15, starting transfers between devices: 19.6 us -> 19.3 us  [swap(): return lax.ppermute(values, 'tensor', [(0, 1), (1, 0)])]
  transfers between devices with their start and end apart: 43 -> 41, of which waited for: 25 -> 27; matrix products, arithmetic and copies ran while one was open for 7% -> 2% of each run, Pallas kernels for 17% -> 12%
where the time goes in v3:
time: 490 us; the launch traced here: 480 us
  waiting for transfers between devices  296 us (60%)
  Pallas kernels  98.8 us (20%)
  starting transfers between devices  46.2 us (9%)
  local copies, waits for them, and re-layouts  22.8 us (5%)
  between operations  15.8 us (3%)
    ppermute x15, waiting for transfers between devices, swap(): return lax.ppermute(values, 'tensor', [(0, 1), (1, 0)])  119 us
    ppermute x24, waiting for transfers between devices, across(): return lax.ppermute(values, 'dp', [(i, i ^ stride) for i in range(count)])  91.8 us
    pallas_call x36, Pallas kernels, call(): pl.pallas_call(wrapped, out_shape=[*[o if i in leave else pltpu.VMEM(o.sh...  82 us
    all_gather x1, waiting for transfers between devices, on_device(): late = lax.all_gather(last_sums(order, late_parts), 'dp')  72.1 us
    ppermute x24, starting transfers between devices, across(): return lax.ppermute(values, 'dp', [(i, i ^ stride) for i in range(count)])  26.9 us
    ppermute x15, starting transfers between devices, swap(): return lax.ppermute(values, 'tensor', [(0, 1), (1, 0)])  19.3 us
    unnamed x54, local copies, waits for them, and re-layouts  17.8 us
    pallas_call x2, Pallas kernels, place(): pl.pallas_call(functools.partial(place_body, count, width, groups), grid=...  16.8 us
  transfers between devices with their start and end apart: 41, of which 27 were waited for; matrix products, arithmetic and copies ran while one was open for 2% of the time, Pallas kernels for 12%

profile of v3, /device:TPU:0, one launch (start us, length us, event | category | flops | bytes accessed | tf_op | source)
XLA Modules:
  0.0 480.2 jit_solution(15665299577513655270)
XLA Ops:
  7.2 3.0 collective-permute-start
  11.0 12.8 %collective-permute-done.1.refs_1_ = bf16[128,768]{1,0:T(8,128)(2,1)S(1)} collective-permute-done((bf16[128,768]{1,0:T(8,128)(2,1)}, bf16[128,768]{1,0:T(8,128)(2,1)S(1)}, u32[]{:S(2)}, u32[]{:S(2)}) %collective-permute-start.1) | collective-permute-done | bytes 196640 | tf_op jit(solution)/shard_map/ppermute | solution.py:522
  31.3 4.9 %shard_map.281 = (bf16[256,768]{1,0:T(8,128)(2,1)S(1)}, bf16[256,384]{1,0:T(8,128)(2,1)S(1)}, bf16[256,384]{1,0:T(8,128)(2,1)S(1)}, bf16[256,384]{1,0:T(8,128)(2...) custom-call(bf16[128,768]{1,0:T(8,128)(2,1)S(1)} %bitcast.23, ...), custom_call_target="tpu_custom_call" | custom-call | bytes 18892800 | tf_op jit(solution)/shard_map/pallas_call | solution.py:104
  36.3 9.6 %shard_map.282 = (bf16[512,768]{1,0:T(8,128)(2,1)S(1)}, bf16[512,384]{1,0:T(8,128)(2,1)S(1)}, bf16[512,384]{1,0:T(8,128)(2,1)S(1)}, bf16[512,384]{1,0:T(8,128)(2...) custom-call(bf16[256,768]{1,0:T(8,128)(2,1)S(1)} %bitcast.19, ...), custom_call_target="tpu_custom_call" | custom-call | bytes 37785600 | tf_op jit(solution)/shard_map/pallas_call | solution.py:104
  45.9 1.8 collective-permute-start.2
  47.7 17.0 %collective-permute-done.2.refs_1_ = bf16[512,768]{1,0:T(8,128)(2,1)S(1)} collective-permute-done((bf16[512,768]{1,0:T(8,128)(2,1)S(1)}, bf16[512,768]{1,0:T(8,128)(2,1)S(1)}, u32[]{:S(2)}, u32[]{:S(2)}) %collective-permute-start.2) | collective-permute-done | bytes 786464 | tf_op jit(solution)/shard_map/ppermute | solution.py:522
  64.7 6.2 %shard_map.283 = (f32[512,768]{1,0:T(8,128)S(1)}, bf16[512,768]{1,0:T(8,128)(2,1)S(1)}, bf16[512,1536]{1,0:T(8,128)(2,1)S(1)}, bf16[512,1536]{1,0:T(8,128)(2,1)S...) custom-call(f32[512,768]{1,0:T(8,128)S(1)} %get-tuple-element.193.refs_0_, ...), custom_call_target="tpu_custom_call" | custom-call | bytes 20992000 | tf_op jit(solution)/shard_map/pallas_call | solution.py:104
  73.0 18.5 %collective-permute-done.3.refs_1_ = bf16[512,768]{1,0:T(8,128)(2,1)S(1)} collective-permute-done((bf16[512,768]{1,0:T(8,128)(2,1)S(1)}, bf16[512,768]{1,0:T(8,128)(2,1)S(1)}, u32[]{:S(2)}, u32[]{:S(2)}) %collective-permute-start.3) | collective-permute-done | bytes 786464 | tf_op jit(solution)/shard_map/ppermute | solution.py:522
  91.4 2.5 shard_map.284
  93.9 3.3 collective-permute-done.4.refs_1_
  97.2 5.5 %shard_map.285 = (f32[256,768]{1,0:T(8,128)S(1)}, bf16[256,768]{1,0:T(8,128)(2,1)S(1)}, bf16[256,384]{1,0:T(8,128)(2,1)S(1)}, bf16[384,256]{1,0:T(8,128)(2,1)S(1...) custom-call(f32[256,768]{1,0:T(8,128)S(1)} %get-tuple-element.200.refs_0, ...), custom_call_target="tpu_custom_call" | custom-call | bytes 18450000 | tf_op jit(solution)/shard_map/pallas_call | solution.py:104
  104.8 8.5 %collective-permute-done.5.refs_1_ = bf16[256,768]{1,0:T(8,128)(2,1)S(1)} collective-permute-done((bf16[256,768]{1,0:T(8,128)(2,1)S(1)}, bf16[256,768]{1,0:T(8,128)(2,1)S(1)}, u32[]{:S(2)}, u32[]{:S(2)}) %collective-permute-start.5) | collective-permute-done | bytes 393248 | tf_op jit(solution)/shard_map/ppermute | solution.py:522
  113.3 3.9 shard_map.286
  118.0 6.0 %shard_map.287 = (f32[256,768]{1,0:T(8,128)S(1)}, bf16[256,768]{1,0:T(8,128)(2,1)S(1)}, bf16[256,1536]{1,0:T(8,128)(2,1)S(1)}, f32[256,768]{1,0:T(8,128)S(1)}, b...) custom-call(f32[128,768]{1,0:T(8,128)S(1)} %get-tuple-element.211.refs_0_, ...), custom_call_target="tpu_custom_call" | custom-call | bytes 10496000 | tf_op jit(solution)/shard_map/pallas_call | solution.py:104
  126.5 10.7 %collective-permute-done.8.refs_2_ = bf16[256,768]{1,0:T(8,128)(2,1)S(1)} collective-permute-done((bf16[256,768]{1,0:T(8,128)(2,1)S(1)}, bf16[256,768]{1,0:T(8,128)(2,1)S(1)}, u32[]{:S(2)}, u32[]{:S(2)}) %collective-permute-start.8) | collective-permute-done | bytes 393248 | tf_op jit(solution)/shard_map/ppermute | solution.py:522
  137.2 6.6 %shard_map.289 = (f32[256,768]{1,0:T(8,128)S(1)}, bf16[256,768]{1,0:T(8,128)(2,1)S(1)}, bf16[256,384]{1,0:T(8,128)(2,1)S(1)}, bf16[512,384]{1,0:T(8,128)(2,1)S(1...) custom-call(f32[256,768]{1,0:T(8,128)S(1)} %get-tuple-element.215.re, ...), custom_call_target="tpu_custom_call" | custom-call | bytes 17273416 | tf_op jit(solution)/shard_map/pallas_call | solution.py:104
  148.2 18.4 %collective-permute-done.9.refs_3_ = bf16[512,768]{1,0:T(8,128)(2,1)S(1)} collective-permute-done((bf16[512,768]{1,0:T(8,128)(2,1)S(1)}, bf16[512,768]{1,0:T(8,128)(2,1)S(1)}, u32[]{:S(2)}, u32[]{:S(2)}) %collective-permute-start.9) | collective-permute-done | bytes 786464 | tf_op jit(solution)/shard_map/ppermute | solution.py:522
  166.6 5.7 %shard_map.292 = (f32[512,768]{1,0:T(8,128)S(1)}, bf16[512,768]{1,0:T(8,128)(2,1)S(1)}, bf16[512,1536]{1,0:T(8,128)(2,1)S(1)}, f32[512,768]{1,0:T(8,128)S(1)}, b...) custom-call(bf16[256,768]{1,0:T(8,128)(2,1)S(1)} %bitcast.17, s32[1]{0:T(128)S(6)} %copy.42.refs_14_.refs_18_.refs_1_, ...), custom_call_target="tpu_custom_call" | custom-call | bytes 20992000 | tf_op jit(solution)/shard_map/pallas_call | solution.py:104
  172.8 2.9 shard_map.295
  179.6 16.3 %collective-permute-done.11.refs_1_.refs_2_ = bf16[512,768]{1,0:T(8,128)(2,1)S(1)} collective-permute-done((bf16[512,768]{1,0:T(8,128)(2,1)S(1)}, bf16[512,768]{1,0:T(8,128)(2,1)S(1)}, u32[]{:S(2)}, u32[]{:S(2)}) %collective-permute-start.11) | collective-permute-done | bytes 786464 | tf_op jit(solution)/shard_map/ppermute | solution.py:522
  197.4 10.3 %shard_map.297 = (f32[512,768]{1,0:T(8,128)S(1)}, bf16[512,768]{1,0:T(8,128)(2,1)S(1)}, bf16[512,384]{1,0:T(8,128)(2,1)S(1)}, bf16[512,384]{1,0:T(8,128)(2,1)S(1...) custom-call(f32[512,768]{1,0:T(8,128)S(1)} %get-tuple-element.241.re, ...), custom_call_target="tpu_custom_call" | custom-call | bytes 34546832 | tf_op jit(solution)/shard_map/pallas_call | solution.py:104
  208.6 1.8 shard_map.301
  210.5 6.0 %shard_map.302 = (f32[256,768]{1,0:T(8,128)S(1)}, bf16[256,768]{1,0:T(8,128)(2,1)S(1)}, bf16[256,384]{1,0:T(8,128)(2,1)S(1)}, bf16[256,384]{1,0:T(8,128)(2,1)S(1...) custom-call(f32[256,768]{1,0:T(8,128)S(1)} %get-tuple-element.285.re, ...), custom_call_target="tpu_custom_call" | custom-call | bytes 8636708 | tf_op jit(solution)/shard_map/pallas_call | solution.py:104
  222.4 8.1 %collective-permute-done.14.refs_2_ = bf16[256,768]{1,0:T(8,128)(2,1)S(1)} collective-permute-done((bf16[256,768]{1,0:T(8,128)(2,1)S(1)}, bf16[256,768]{1,0:T(8,128)(2,1)S(1)}, u32[]{:S(2)}, u32[]{:S(2)}) %collective-permute-start.14) | collective-permute-done | bytes 393248 | tf_op jit(solution)/shard_map/ppermute | solution.py:522
  231.6 1.9 collective-permute-done.20.refs_2_
  234.0 12.0 %collective-permute-done.28.refs_1_ = bf16[768,768]{1,0:T(8,128)(2,1)S(1)} collective-permute-done((bf16[768,768]{1,0:T(8,128)(2,1)S(1)}, bf16[768,768]{1,0:T(8,128)(2,1)S(1)}, u32[]{:S(2)}, u32[]{:S(2)}) %collective-permute-start.28) | collective-permute-done | bytes 1179680 | tf_op jit(solution)/shard_map/ppermute | solution.py:531
  249.9 10.9 %collective-permute-done.29.refs_1_ = bf16[384,768]{1,0:T(8,128)(2,1)S(1)} collective-permute-done((bf16[384,768]{1,0:T(8,128)(2,1)S(1)}, bf16[384,768]{1,0:T(8,128)(2,1)S(1)}, u32[]{:S(2)}, u32[]{:S(2)}) %collective-permute-start.29) | collective-permute-done | bytes 589856 | tf_op jit(solution)/shard_map/ppermute | solution.py:531
  260.9 3.2 collective-permute-done.31.refs_1_
  264.8 9.9 %collective-permute-done.33.refs_1_ = bf16[384,768]{1,0:T(8,128)(2,1)S(1)} collective-permute-done((bf16[384,768]{1,0:T(8,128)(2,1)S(1)}, bf16[384,768]{1,0:T(8,128)(2,1)S(1)}, u32[]{:S(2)}, u32[]{:S(2)}) %collective-permute-start.33) | collective-permute-done | bytes 589856 | tf_op jit(solution)/shard_map/ppermute | solution.py:531
  275.4 2.6 collective-permute-start.37
  278.4 10.8 %collective-permute-done.35.refs_1_ = bf16[192,768]{1,0:T(8,128)(2,1)S(1)} collective-permute-done((bf16[192,768]{1,0:T(8,128)(2,1)S(1)}, bf16[192,768]{1,0:T(8,128)(2,1)S(1)}, u32[]{:S(2)}, u32[]{:S(2)}) %collective-permute-start.35) | collective-permute-done | bytes 294944 | tf_op jit(solution)/shard_map/ppermute | solution.py:531
  289.3 5.2 %collective-permute-done.37.refs_1_ = bf16[192,768]{1,0:T(8,128)(2,1)S(1)} collective-permute-done((bf16[192,768]{1,0:T(8,128)(2,1)S(1)}, bf16[192,768]{1,0:T(8,128)(2,1)S(1)}, u32[]{:S(2)}, u32[]{:S(2)}) %collective-permute-start.37) | collective-permute-done | bytes 294944 | tf_op jit(solution)/shard_map/ppermute | solution.py:531
  294.5 3.2 collective-permute-done.38.refs_3_
  298.7 2.9 collective-permute-start.34
  301.7 11.1 %collective-permute-done.30.refs_1_ = bf16[192,768]{1,0:T(8,128)(2,1)S(1)} collective-permute-done((bf16[192,768]{1,0:T(8,128)(2,1)}, bf16[192,768]{1,0:T(8,128)(2,1)S(1)}, u32[]{:S(2)}, u32[]{:S(2)}) %collective-permute-start.30) | collective-permute-done | bytes 294944 | tf_op jit(solution)/shard_map/ppermute | solution.py:531
  314.4 9.0 %collective-permute-done.36.refs_5_ = bf16[96,768]{1,0:T(8,128)(2,1)S(1)} collective-permute-done((bf16[96,768]{1,0:T(8,128)(2,1)}, bf16[96,768]{1,0:T(8,128)(2,1)S(1)}, u32[]{:S(2)}, u32[]{:S(2)}) %collective-permute-start.36) | collective-permute-done | bytes 147488 | tf_op jit(solution)/shard_map/ppermute | solution.py:531
  324.7 4.0 collective-permute-done.23
  331.2 1.7 collective-permute-start.6
  334.6 7.3 %collective-permute-start.26 = (f32[22,768]{1,0:T(8,128)S(1)}, f32[22,768]{1,0:T(8,128)S(1)}, u32[]{:S(2)}, u32[]{:S(2)}) collective-permute-start(f32[22,768]{1,0:T(8,128)S(1)} %add.21), channel_id=1, source_target_pairs={{0,8},{2,10},{4,12},{6,14},{8,0},{10,2},{12,4},{14,6},{16,24},{18,... | collective-permute-start | bytes 202760 | tf_op jit(solution)/shard_map/ppermute | solution.py:531
  342.6 6.3 %collective-permute-done.26 = f32[22,768]{1,0:T(8,128)S(1)} collective-permute-done((f32[22,768]{1,0:T(8,128)S(1)}, f32[22,768]{1,0:T(8,128)S(1)}, u32[]{:S(2)}, u32[]{:S(2)}) %collective-permute-start.26) | collective-permute-done | bytes 67616 | tf_op jit(solution)/shard_map/ppermute | solution.py:531
  349.0 3.6 collective-permute-start.27
  356.2 5.6 %collective-permute-done.27 = f32[22,768]{1,0:T(8,128)S(1)} collective-permute-done((f32[22,768]{1,0:T(8,128)S(1)}, f32[22,768]{1,0:T(8,128)S(1)}, u32[]{:S(2)}, u32[]{:S(2)}) %collective-permute-start.27) | collective-permute-done | bytes 67616 | tf_op jit(solution)/shard_map/ppermute | solution.py:531
  364.9 12.4 %all-gather.7.cloned.1.call-done = bf16[4608,768]{1,0:T(8,128)(2,1)} async-done(((bf16[288,768]{1,0:T(8,128)(2,1)}), bf16[4608,768]{1,0:T(8,128)(2,1)}) %all-gather.7.cloned.1.call-update) | async-done | bytes 7077904 | tf_op jit(solution)/shard_map/all_gather | solution.py:881
  377.3 3.0 copy-done.1
  380.3 7.9 %shard_map.317 = (f32[2,768,1536]{2,1,0:T(8,128)}, f32[2,1536,768]{2,1,0:T(8,128)}, f32[3,3,768,384]{3,2,1,0:T(8,128)}, f32[3,384,768]{2,1,0:T(8,128)}, f32[8,128]{1,0:T(8,128)S(1)}) custom-call(bf16[16,288,768]{2,1,0:T(8,128)(2,1)S(1)} %bitcast.15, f32[8,128]{1,0:T(8,128)S(1)} %get-tuple-element.360.refs_0_), custom_call_target="tpu_custom_call" | custom-call | bytes 36900000 | tf_op jit(solution)/shard_map/pallas_call | solution.py:660
  388.2 72.1 %all-gather.5.cloned.1.call-done = bf16[6144,768]{1,0:T(8,128)(2,1)} async-done(((bf16[384,768]{1,0:T(8,128)(2,1)}), bf16[6144,768]{1,0:T(8,128)(2,1)}) %all-gather.5.cloned.1.call-update) | async-done | bytes 9437200 | tf_op jit(solution)/shard_map/all_gather | solution.py:882
  460.3 3.7 copy-done
  464.0 8.9 %shard_map.318 = (f32[2,768,1536]{2,1,0:T(8,128)}, f32[2,1536,768]{2,1,0:T(8,128)}, f32[3,3,768,384]{3,2,1,0:T(8,128)}, f32[3,384,768]{2,1,0:T(8,128)}, f32[8,128]{1,0:T(8,128)}) custom-call(bf16[16,384,768]{2,1,0:T(8,128)(2,1)S(1)} %bitcast.14, ...), custom_call_target="tpu_custom_call", output_to_operand_aliasing={{0}: (1, {}), {1}: (2, {}), {2}: (3, {}), {3}: (4, {})} | custom-call | bytes 36900000 | tf_op jit(solution)/shard_map/pallas_call | solution.py:660
  (153 shorter events, 54.9 us)
Async XLA Ops:
  7.2 370.1 %all-gather.7.cloned.1.call-start = ((), (), s32[]{:S(2)}) async-start(), calls=%async_computation.1 | async-start | bytes 7520256 | tf_op jit(solution)/shard_map/all_gather | solution.py:881
  7.2 29.0 %collective-permute-start = (bf16[256,768]{1,0:T(8,128)(2,1)}, bf16[256,768]{1,0:T(8,128)(2,1)S(1)}, u32[]{:S(2)}, u32[]{:S(2)}) collective-permute-start(bf16[256,768]{1,0:T(8,128)(2,1)} %bitcast.18), channel_id=1, source_target_pairs={{0,1},{1,0},{2,3},{3,2},{4,5},{5,4},{6,7},{7,6},{8,9},{9,8},{10,11... | collective-permute-start | bytes 1179656 | tf_op jit(solution)/shard_map/ppermute | solution.py:522
  10.3 13.5 %collective-permute-start.1 = (bf16[128,768]{1,0:T(8,128)(2,1)}, bf16[128,768]{1,0:T(8,128)(2,1)S(1)}, u32[]{:S(2)}, u32[]{:S(2)}) collective-permute-start(bf16[128,768]{1,0:T(8,128)(2,1)} %bitcast.22), channel_id=1, source_target_pairs={{0,1},{1,0},{2,3},{3,2},{4,5},{5,4},{6,7},{7,6},{8,9},{9,8},{10,11... | collective-permute-start | bytes 589832 | tf_op jit(solution)/shard_map/ppermute | solution.py:522
  36.3 28.4 %copy-start.9 = (f32[3,768]{1,0:T(4,128)S(1)}, f32[3,768]{1,0:T(4,128)}, u32[]{:S(2)}) copy-start(f32[3,768]{1,0:T(4,128)} %refs_6_.21) | copy-start | bytes 27652
  36.3 28.4 %copy-start.11 = (f32[2,1536]{1,0:T(2,128)S(1)}, f32[2,1536]{1,0:T(2,128)}, u32[]{:S(2)}) copy-start(f32[2,1536]{1,0:T(2,128)} %refs_9_.19) | copy-start | bytes 36868
  36.3 28.4 %copy-start.13 = (f32[3,2,384]{2,1,0:T(2,128)S(1)}, f32[3,2,384]{2,1,0:T(2,128)}, u32[]{:S(2)}) copy-start(f32[3,2,384]{2,1,0:T(2,128)} %refs_8_.21) | copy-start | bytes 27652
  36.3 28.4 %copy-start.17 = (f32[2,768]{1,0:T(2,128)S(1)}, f32[2,768]{1,0:T(2,128)}, u32[]{:S(2)}) copy-start(f32[2,768]{1,0:T(2,128)} %refs_7_.21) | copy-start | bytes 18436
  45.9 18.8 %collective-permute-start.2 = (bf16[512,768]{1,0:T(8,128)(2,1)S(1)}, bf16[512,768]{1,0:T(8,128)(2,1)S(1)}, u32[]{:S(2)}, u32[]{:S(2)}) collective-permute-start(bf16[512,768]{1,0:T(8,128)(2,1)S(1)} %get-tuple-element.194), channel_id=1, source_target_pairs={{0,1},{1,0},{2,3},{3,2},{4,5},{5,4},{6,7},{7,6},{8,9},{9,8},{10,11... | collective-permute-start | bytes 2359304 | tf_op jit(solution)/shard_map/ppermute | solution.py:522
  70.9 20.5 %collective-permute-start.3 = (bf16[512,768]{1,0:T(8,128)(2,1)S(1)}, bf16[512,768]{1,0:T(8,128)(2,1)S(1)}, u32[]{:S(2)}, u32[]{:S(2)}) collective-permute-start(bf16[512,768]{1,0:T(8,128)(2,1)S(1)} %get-tuple-element.197), channel_id=1, source_target_pairs={{0,1},{1,0},{2,3},{3,2},{4,5},{5,4},{6,7},{7,6},{8,9},{9,8},{10,11... | collective-permute-start | bytes 2359304 | tf_op jit(solution)/shard_map/ppermute | solution.py:522
  72.4 24.8 %collective-permute-start.4 = (bf16[256,768]{1,0:T(8,128)(2,1)S(1)}, bf16[256,768]{1,0:T(8,128)(2,1)S(1)}, u32[]{:S(2)}, u32[]{:S(2)}) collective-permute-start(bf16[256,768]{1,0:T(8,128)(2,1)S(1)} %get-tuple-element.201), channel_id=1, source_target_pairs={{0,1},{1,0},{2,3},{3,2},{4,5},{5,4},{6,7},{7,6},{8,9},{9,8},{10,11... | collective-permute-start | bytes 1179656 | tf_op jit(solution)/shard_map/ppermute | solution.py:522
  102.7 10.6 %collective-permute-start.5 = (bf16[256,768]{1,0:T(8,128)(2,1)S(1)}, bf16[256,768]{1,0:T(8,128)(2,1)S(1)}, u32[]{:S(2)}, u32[]{:S(2)}) collective-permute-start(bf16[256,768]{1,0:T(8,128)(2,1)S(1)} %get-tuple-element.207), channel_id=1, source_target_pairs={{0,1},{1,0},{2,3},{3,2},{4,5},{5,4},{6,7},{7,6},{8,9},{9,8},{10,11... | collective-permute-start | bytes 1179656 | tf_op jit(solution)/shard_map/ppermute | solution.py:522
  103.8 14.1 %collective-permute-start.7 = (bf16[128,768]{1,0:T(8,128)(2,1)S(1)}, bf16[128,768]{1,0:T(8,128)(2,1)S(1)}, u32[]{:S(2)}, u32[]{:S(2)}) collective-permute-start(bf16[128,768]{1,0:T(8,128)(2,1)S(1)} %get-tuple-element.212), channel_id=1, source_target_pairs={{0,1},{1,0},{2,3},{3,2},{4,5},{5,4},{6,7},{7,6},{8,9},{9,8},{10,11... | collective-permute-start | bytes 589832 | tf_op jit(solution)/shard_map/ppermute | solution.py:522
  124.0 13.2 %copy-start.6 = (bf16[256,1,768]{2,0,1:T(8,128)(2,1)S(1)}, bf16[256,1,768]{2,0,1:T(8,128)(2,1)}, u32[]{:S(2)}) copy-start(bf16[256,1,768]{2,0,1:T(8,128)(2,1)} %param.24) | copy-start | bytes 1179652
  125.6 18.2 %collective-permute-start.10 = (bf16[1536,768]{1,0:T(8,128)(2,1)S(1)}, bf16[1536,768]{1,0:T(8,128)(2,1)S(1)}, u32[]{:S(2)}, u32[]{:S(2)}) collective-permute-start(bf16[1536,768]{1,0:T(8,128)(2,1)S(1)} %get-tuple-element.237), channel_id=1, source_target_pairs={{0,2},{2,0},{4,6},{6,4},{8,10},{10,8},{12,14},{14,12},{16,18},{18,... | collective-permute-start | bytes 7077896 | tf_op jit(solution)/shard_map/ppermute | solution.py:531
  125.6 11.5 %collective-permute-start.8 = (bf16[256,768]{1,0:T(8,128)(2,1)S(1)}, bf16[256,768]{1,0:T(8,128)(2,1)S(1)}, u32[]{:S(2)}, u32[]{:S(2)}) collective-permute-start(bf16[256,768]{1,0:T(8,128)(2,1)S(1)} %get-tuple-element.217), channel_id=1, source_target_pairs={{0,1},{1,0},{2,3},{3,2},{4,5},{5,4},{6,7},{7,6},{8,9},{9,8},{10,11... | collective-permute-start | bytes 1179656 | tf_op jit(solution)/shard_map/ppermute | solution.py:522
  144.3 27.9 %collective-permute-start.13 = (bf16[768,768]{1,0:T(8,128)(2,1)S(1)}, bf16[768,768]{1,0:T(8,128)(2,1)S(1)}, u32[]{:S(2)}, u32[]{:S(2)}) collective-permute-start(bf16[768,768]{1,0:T(8,128)(2,1)S(1)} %get-tuple-element.257), channel_id=1, source_target_pairs={{0,4},{2,6},{4,0},{6,2},{8,12},{10,14},{12,8},{14,10},{16,20},{18,... | collective-permute-start | bytes 3538952 | tf_op jit(solution)/shard_map/ppermute | solution.py:531
  146.5 26.0 %collective-permute-start.12 = (bf16[768,768]{1,0:T(8,128)(2,1)S(1)}, bf16[768,768]{1,0:T(8,128)(2,1)S(1)}, u32[]{:S(2)}, u32[]{:S(2)}) collective-permute-start(bf16[768,768]{1,0:T(8,128)(2,1)S(1)} %get-tuple-element.255), channel_id=1, source_target_pairs={{0,2},{2,0},{4,6},{6,4},{8,10},{10,8},{12,14},{14,12},{16,18},{18,... | collective-permute-start | bytes 3538952 | tf_op jit(solution)/shard_map/ppermute | solution.py:531
  146.6 20.0 %collective-permute-start.9 = (bf16[512,768]{1,0:T(8,128)(2,1)S(1)}, bf16[512,768]{1,0:T(8,128)(2,1)S(1)}, u32[]{:S(2)}, u32[]{:S(2)}) collective-permute-start(bf16[512,768]{1,0:T(8,128)(2,1)S(1)} %get-tuple-element.228), channel_id=1, source_target_pairs={{0,1},{1,0},{2,3},{3,2},{4,5},{5,4},{6,7},{7,6},{8,9},{9,8},{10,11... | collective-permute-start | bytes 2359304 | tf_op jit(solution)/shard_map/ppermute | solution.py:522
  175.8 32.3 %collective-permute-start.15 = (bf16[1536,768]{1,0:T(8,128)(2,1)S(1)}, bf16[1536,768]{1,0:T(8,128)(2,1)S(1)}, u32[]{:S(2)}, u32[]{:S(2)}) collective-permute-start(bf16[1536,768]{1,0:T(8,128)(2,1)S(1)} %get-tuple-element.273), channel_id=1, source_target_pairs={{0,2},{2,0},{4,6},{6,4},{8,10},{10,8},{12,14},{14,12},{16,18},{18,... | collective-permute-start | bytes 7077896 | tf_op jit(solution)/shard_map/ppermute | solution.py:531
  175.9 20.0 %collective-permute-start.11 = (bf16[512,768]{1,0:T(8,128)(2,1)S(1)}, bf16[512,768]{1,0:T(8,128)(2,1)S(1)}, u32[]{:S(2)}, u32[]{:S(2)}) collective-permute-start(bf16[512,768]{1,0:T(8,128)(2,1)S(1)} %get-tuple-element.243), channel_id=1, source_target_pairs={{0,1},{1,0},{2,3},{3,2},{4,5},{5,4},{6,7},{7,6},{8,9},{9,8},{10,11... | collective-permute-start | bytes 2359304 | tf_op jit(solution)/shard_map/ppermute | solution.py:522
  177.4 30.3 %collective-permute-start.17 = (bf16[384,768]{1,0:T(8,128)(2,1)S(1)}, bf16[384,768]{1,0:T(8,128)(2,1)S(1)}, u32[]{:S(2)}, u32[]{:S(2)}) collective-permute-start(bf16[384,768]{1,0:T(8,128)(2,1)S(1)} %get-tuple-element.277), channel_id=1, source_target_pairs={{0,8},{2,10},{4,12},{6,14},{8,0},{10,2},{12,4},{14,6},{16,24},{18,... | collective-permute-start | bytes 1769480 | tf_op jit(solution)/shard_map/ppermute | solution.py:531
  179.0 28.9 %collective-permute-start.16 = (bf16[384,768]{1,0:T(8,128)(2,1)S(1)}, bf16[384,768]{1,0:T(8,128)(2,1)S(1)}, u32[]{:S(2)}, u32[]{:S(2)}) collective-permute-start(bf16[384,768]{1,0:T(8,128)(2,1)S(1)} %get-tuple-element.275), channel_id=1, source_target_pairs={{0,4},{2,6},{4,0},{6,2},{8,12},{10,14},{12,8},{14,10},{16,20},{18,... | collective-permute-start | bytes 1769480 | tf_op jit(solution)/shard_map/ppermute | solution.py:531
  195.8 14.6 %collective-permute-start.19 = (bf16[256,768]{1,0:T(8,128)(2,1)S(1)}, bf16[256,768]{1,0:T(8,128)(2,1)S(1)}, u32[]{:S(2)}, u32[]{:S(2)}) collective-permute-start(bf16[256,768]{1,0:T(8,128)(2,1)S(1)} %get-tuple-element.287), channel_id=1, source_target_pairs={{0,1},{1,0},{2,3},{3,2},{4,5},{5,4},{6,7},{7,6},{8,9},{9,8},{10,11... | collective-permute-start | bytes 1179656 | tf_op jit(solution)/shard_map/ppermute | solution.py:522
  210.4 10.2 %collective-permute-start.18 = (bf16[768,768]{1,0:T(8,128)(2,1)S(1)}, bf16[768,768]{1,0:T(8,128)(2,1)S(1)}, u32[]{:S(2)}, u32[]{:S(2)}) collective-permute-start(bf16[768,768]{1,0:T(8,128)(2,1)S(1)} %get-tuple-element.283), channel_id=1, source_target_pairs={{0,2},{2,0},{4,6},{6,4},{8,10},{10,8},{12,14},{14,12},{16,18},{18,... | collective-permute-start | bytes 3538952 | tf_op jit(solution)/shard_map/ppermute | solution.py:531
  217.5 13.9 %collective-permute-start.21 = (bf16[768,768]{1,0:T(8,128)(2,1)S(1)}, bf16[768,768]{1,0:T(8,128)(2,1)S(1)}, u32[]{:S(2)}, u32[]{:S(2)}) collective-permute-start(bf16[768,768]{1,0:T(8,128)(2,1)S(1)} %get-tuple-element.309), channel_id=1, source_target_pairs={{0,2},{2,0},{4,6},{6,4},{8,10},{10,8},{12,14},{14,12},{16,18},{18,... | collective-permute-start | bytes 3538952 | tf_op jit(solution)/shard_map/ppermute | solution.py:531
  218.0 28.0 %collective-permute-start.28 = (bf16[768,768]{1,0:T(8,128)(2,1)S(1)}, bf16[768,768]{1,0:T(8,128)(2,1)S(1)}, u32[]{:S(2)}, u32[]{:S(2)}) collective-permute-start(bf16[768,768]{1,0:T(8,128)(2,1)S(1)} %get-tuple-element.329), channel_id=1, source_target_pairs={{0,4},{2,6},{4,0},{6,2},{8,12},{10,14},{12,8},{14,10},{16,20},{18,... | collective-permute-start | bytes 3538952 | tf_op jit(solution)/shard_map/ppermute | solution.py:531
  218.5 12.0 %collective-permute-start.14 = (bf16[256,768]{1,0:T(8,128)(2,1)S(1)}, bf16[256,768]{1,0:T(8,128)(2,1)S(1)}, u32[]{:S(2)}, u32[]{:S(2)}) collective-permute-start(bf16[256,768]{1,0:T(8,128)(2,1)S(1)} %get-tuple-element.265), channel_id=1, source_target_pairs={{0,1},{1,0},{2,3},{3,2},{4,5},{5,4},{6,7},{7,6},{8,9},{9,8},{10,11... | collective-permute-start | bytes 1179656 | tf_op jit(solution)/shard_map/ppermute | solution.py:522
  219.8 11.4 %collective-permute-start.22 = (bf16[192,768]{1,0:T(8,128)(2,1)S(1)}, bf16[192,768]{1,0:T(8,128)(2,1)S(1)}, u32[]{:S(2)}, u32[]{:S(2)}) collective-permute-start(bf16[192,768]{1,0:T(8,128)(2,1)S(1)} %get-tuple-element.311), channel_id=1, source_target_pairs={{0,8},{2,10},{4,12},{6,14},{8,0},{10,2},{12,4},{14,6},{16,24},{18,... | collective-permute-start | bytes 884744 | tf_op jit(solution)/shard_map/ppermute | solution.py:531
  220.6 12.9 %collective-permute-start.20 = (bf16[128,768]{1,0:T(8,128)(2,1)S(1)}, bf16[128,768]{1,0:T(8,128)(2,1)S(1)}, u32[]{:S(2)}, u32[]{:S(2)}) collective-permute-start(bf16[128,768]{1,0:T(8,128)(2,1)S(1)} %get-tuple-element.307), channel_id=1, source_target_pairs={{0,1},{1,0},{2,3},{3,2},{4,5},{5,4},{6,7},{7,6},{8,9},{9,8},{10,11... | collective-permute-start | bytes 589832 | tf_op jit(solution)/shard_map/ppermute | solution.py:522
  246.2 14.5 %collective-permute-start.29 = (bf16[384,768]{1,0:T(8,128)(2,1)S(1)}, bf16[384,768]{1,0:T(8,128)(2,1)S(1)}, u32[]{:S(2)}, u32[]{:S(2)}) collective-permute-start(bf16[384,768]{1,0:T(8,128)(2,1)S(1)} %get-tuple-element.332), channel_id=1, source_target_pairs={{0,8},{2,10},{4,12},{6,14},{8,0},{10,2},{12,4},{14,6},{16,24},{18,... | collective-permute-start | bytes 1769480 | tf_op jit(solution)/shard_map/ppermute | solution.py:531
  247.9 16.3 %collective-permute-start.31 = (bf16[384,768]{1,0:T(8,128)(2,1)S(1)}, bf16[384,768]{1,0:T(8,128)(2,1)S(1)}, u32[]{:S(2)}, u32[]{:S(2)}) collective-permute-start(bf16[384,768]{1,0:T(8,128)(2,1)S(1)} %get-tuple-element.337), channel_id=1, source_target_pairs={{0,4},{2,6},{4,0},{6,2},{8,12},{10,14},{12,8},{14,10},{16,20},{18,... | collective-permute-start | bytes 1769480 | tf_op jit(solution)/shard_map/ppermute | solution.py:531
  248.4 26.3 %collective-permute-start.33 = (bf16[384,768]{1,0:T(8,128)(2,1)S(1)}, bf16[384,768]{1,0:T(8,128)(2,1)S(1)}, u32[]{:S(2)}, u32[]{:S(2)}) collective-permute-start(bf16[384,768]{1,0:T(8,128)(2,1)S(1)} %get-tuple-element.342), channel_id=1, source_target_pairs={{0,4},{2,6},{4,0},{6,2},{8,12},{10,14},{12,8},{14,10},{16,20},{18,... | collective-permute-start | bytes 1769480 | tf_op jit(solution)/shard_map/ppermute | solution.py:531
  260.9 28.4 %copy-start.23 = (bf16[192,768]{1,0:T(8,128)(2,1)}, bf16[192,768]{1,0:T(8,128)(2,1)S(1)}, u32[]{:S(2)}) copy-start(bf16[192,768]{1,0:T(8,128)(2,1)S(1)} %get-tuple-element.335) | copy-start | bytes 884740
  264.3 14.0 %collective-permute-start.32 = (bf16[192,768]{1,0:T(8,128)(2,1)S(1)}, bf16[192,768]{1,0:T(8,128)(2,1)S(1)}, u32[]{:S(2)}, u32[]{:S(2)}) collective-permute-start(bf16[192,768]{1,0:T(8,128)(2,1)S(1)} %get-tuple-element.340), channel_id=1, source_target_pairs={{0,8},{2,10},{4,12},{6,14},{8,0},{10,2},{12,4},{14,6},{16,24},{18,... | collective-permute-start | bytes 884744 | tf_op jit(solution)/shard_map/ppermute | solution.py:531
  274.8 14.3 %collective-permute-start.35 = (bf16[192,768]{1,0:T(8,128)(2,1)S(1)}, bf16[192,768]{1,0:T(8,128)(2,1)S(1)}, u32[]{:S(2)}, u32[]{:S(2)}) collective-permute-start(bf16[192,768]{1,0:T(8,128)(2,1)S(1)} %get-tuple-element.348), channel_id=1, source_target_pairs={{0,8},{2,10},{4,12},{6,14},{8,0},{10,2},{12,4},{14,6},{16,24},{18,... | collective-permute-start | bytes 884744 | tf_op jit(solution)/shard_map/ppermute | solution.py:531
  275.4 19.2 %collective-permute-start.37 = (bf16[192,768]{1,0:T(8,128)(2,1)S(1)}, bf16[192,768]{1,0:T(8,128)(2,1)S(1)}, u32[]{:S(2)}, u32[]{:S(2)}) collective-permute-start(bf16[192,768]{1,0:T(8,128)(2,1)S(1)} %get-tuple-element.353), channel_id=1, source_target_pairs={{0,16},{2,18},{4,20},{6,22},{8,24},{10,26},{12,28},{14,30},{16,0},... | collective-permute-start | bytes 884744 | tf_op jit(solution)/shard_map/ppermute | solution.py:531
  277.9 19.7 %collective-permute-start.38 = (bf16[96,768]{1,0:T(8,128)(2,1)S(1)}, bf16[96,768]{1,0:T(8,128)(2,1)S(1)}, u32[]{:S(2)}, u32[]{:S(2)}) collective-permute-start(bf16[96,768]{1,0:T(8,128)(2,1)S(1)} %get-tuple-element.355), channel_id=1, source_target_pairs={{0,16},{2,18},{4,20},{6,22},{8,24},{10,26},{12,28},{14,30},{16,0},... | collective-permute-start | bytes 442376 | tf_op jit(solution)/shard_map/ppermute | solution.py:531
  278.4 20.2 %copy-start.24 = (bf16[96,768]{1,0:T(8,128)(2,1)}, bf16[96,768]{1,0:T(8,128)(2,1)S(1)}, u32[]{:S(2)}) copy-start(bf16[96,768]{1,0:T(8,128)(2,1)S(1)} %get-tuple-element.346) | copy-start | bytes 442372
  298.6 161.7 %all-gather.5.cloned.1.call-start = ((), (), s32[]{:S(2)}) async-start(), calls=%async_computation | async-start | bytes 10027008 | tf_op jit(solution)/shard_map/all_gather | solution.py:882
  298.6 14.2 %collective-permute-start.30 = (bf16[192,768]{1,0:T(8,128)(2,1)}, bf16[192,768]{1,0:T(8,128)(2,1)S(1)}, u32[]{:S(2)}, u32[]{:S(2)}) collective-permute-start(bf16[192,768]{1,0:T(8,128)(2,1)} %copy-done.23), channel_id=1, source_target_pairs={{0,16},{2,18},{4,20},{6,22},{8,24},{10,26},{12,28},{14,30},{16,0},... | collective-permute-start | bytes 884744 | tf_op jit(solution)/shard_map/ppermute | solution.py:531
  298.7 15.7 %collective-permute-start.34 = (bf16[96,768]{1,0:T(8,128)(2,1)}, bf16[96,768]{1,0:T(8,128)(2,1)S(1)}, u32[]{:S(2)}, u32[]{:S(2)}) collective-permute-start(bf16[96,768]{1,0:T(8,128)(2,1)} %copy-done.24), channel_id=1, source_target_pairs={{0,16},{2,18},{4,20},{6,22},{8,24},{10,26},{12,28},{14,30},{16,0},... | collective-permute-start | bytes 442376 | tf_op jit(solution)/shard_map/ppermute | solution.py:531
  301.6 21.8 %collective-permute-start.36 = (bf16[96,768]{1,0:T(8,128)(2,1)}, bf16[96,768]{1,0:T(8,128)(2,1)S(1)}, u32[]{:S(2)}, u32[]{:S(2)}) collective-permute-start(bf16[96,768]{1,0:T(8,128)(2,1)} %copy-done.25), channel_id=1, source_target_pairs={{0,16},{2,18},{4,20},{6,22},{8,24},{10,26},{12,28},{14,30},{16,0},... | collective-permute-start | bytes 442376 | tf_op jit(solution)/shard_map/ppermute | solution.py:531
  324.6 4.2 collective-permute-start.23
  328.8 1.3 collective-permute-start.24
  330.1 4.4 collective-permute-start.25
  331.2 21.5 %collective-permute-start.6 = (bf16[128,768]{1,0:T(8,128)(2,1)S(1)}, bf16[128,768]{1,0:T(8,128)(2,1)S(1)}, u32[]{:S(2)}, u32[]{:S(2)}) collective-permute-start(bf16[128,768]{1,0:T(8,128)(2,1)S(1)} %slice.68), channel_id=1, source_target_pairs={{0,1},{1,0},{2,3},{3,2},{4,5},{5,4},{6,7},{7,6},{8,9},{9,8},{10,11... | collective-permute-start | bytes 589832 | tf_op jit(solution)/shard_map/ppermute | solution.py:522
  334.6 14.4 %collective-permute-start.26 = (f32[22,768]{1,0:T(8,128)S(1)}, f32[22,768]{1,0:T(8,128)S(1)}, u32[]{:S(2)}, u32[]{:S(2)}) collective-permute-start(f32[22,768]{1,0:T(8,128)S(1)} %add.21), channel_id=1, source_target_pairs={{0,8},{2,10},{4,12},{6,14},{8,0},{10,2},{12,4},{14,6},{16,24},{18,... | collective-permute-start | bytes 202760 | tf_op jit(solution)/shard_map/ppermute | solution.py:531
  349.0 12.8 %collective-permute-start.27 = (f32[22,768]{1,0:T(8,128)S(1)}, f32[22,768]{1,0:T(8,128)S(1)}, u32[]{:S(2)}, u32[]{:S(2)}) collective-permute-start(f32[22,768]{1,0:T(8,128)S(1)} %add.22), channel_id=1, source_target_pairs={{0,16},{2,18},{4,20},{6,22},{8,24},{10,26},{12,28},{14,30},{16,0},... | collective-permute-start | bytes 202760 | tf_op jit(solution)/shard_map/ppermute | solution.py:531
  (19 other events, 46.4 us)
Sparse Core Ops, SparseCore 0:
  298.7 78.5 all-gather.6
  379.6 80.6 all-gather.4
